TPU v7x, 32 devices: a whole 2x2x4 slice. The times are simulated.
32 devices in a mesh: dp: 16 (over z, y, x), tensor: 2 (over core).
Axes of the slice: x: 2, y: 2, z: 4, core: 2. Of those that a mesh axis runs over, the one named last changes fastest.
Arguments:
- tokens: bfloat16 [32768, 768], P(('dp', 'tensor')), may hold values from -6 to 6
- w_query: bfloat16 [768, 768], P('dp', 'tensor'), may hold values from -0.21875 to 0.21875
- w_key: bfloat16 [768, 768], P('dp', 'tensor'), may hold values from -0.21875 to 0.21875
- w_value: bfloat16 [768, 768], P('dp', 'tensor'), may hold values from -0.21875 to 0.21875
- w_out: bfloat16 [768, 768], P('tensor', 'dp'), may hold values from -3.5 to 3.5
- w_gate: bfloat16 [768, 2048], P('dp', 'tensor'), may hold values from -0.21875 to 0.21875
- w_up: bfloat16 [768, 2048], P('dp', 'tensor'), may hold values from -0.21875 to 0.21875
- w_down: bfloat16 [2048, 768], P('tensor', 'dp'), may hold values from -0.125 to 0.125
- gain_attn: float32 [768], replicated, may hold values from 0.5 to 1.5
- gain_ffn: float32 [768], replicated, may hold values from 0.5 to 1.5
- lengths: int32 [16, 3], P('dp'), may hold values from 0 to 2048, as said below
- cotangent: bfloat16 [32768, 768], P(('dp', 'tensor')), may hold values from -6 to 6
Outputs:
- output: bfloat16 [32768, 768], P(('dp', 'tensor'))
- input_grad: bfloat16 [32768, 768], P(('dp', 'tensor'))
- grad_query: float32 [768, 768], P('dp', 'tensor')
- grad_key: float32 [768, 768], P('dp', 'tensor')
- grad_value: float32 [768, 768], P('dp', 'tensor')
- grad_out: float32 [768, 768], P('tensor', 'dp')
- grad_gate: float32 [768, 2048], P('dp', 'tensor')
- grad_up: float32 [768, 2048], P('dp', 'tensor')
- grad_down: float32 [2048, 768], P('tensor', 'dp')
- grad_gain_attn: float32 [768], replicated
- grad_gain_ffn: float32 [768], replicated
Inputs may be any that keep to these rules, and one draw needn't show every extreme that they name: `lengths`: each row holds one to 3 documents packed from the group's first slot, then zeros; a nonzero length is at least 512; a row sums to 2048 at most; some row holds one document of 2048 slots.
All inputs are finite; a program needn't handle non-finite values.
Results may differ from a plain program's by a relative error of at most 0.019.
Values may be sent and summed in bfloat16 or wider, within the bound.
No kernel may reach another device: no remote copies, remote signals or barrier semaphores. Data moves between devices by JAX's collectives and lax.ppermute only.
A program may use at most 256 MiB of HBM per device.

v0:
```python
from functools import partial

import jax
import jax.numpy as jnp
from jax import lax
from jax.sharding import PartitionSpec as P

HEAD = 64


EPS = 1e-05
ROPE_BASE = 10000.0
NEGATIVE = -1e30


def layout(lengths_row, slots):
    index = jnp.arange(slots, dtype=jnp.int32)
    ends = jnp.cumsum(lengths_row)
    passed = index[:, None] >= ends[None, :]
    segment_ids = jnp.sum(passed.astype(jnp.int32), axis=1)
    begins = jnp.sum(jnp.where(passed, lengths_row[None, :], 0), axis=1)
    valid = index < ends[-1]
    return (jnp.where(valid, segment_ids, -1), index - begins, valid, index)


def tables(position, head_size):
    half = head_size // 2
    inverse = ROPE_BASE ** (-(jnp.arange(half, dtype=jnp.float32) * 2.0 / head_size))
    angle = position.astype(jnp.float32)[:, None] * inverse[None, :]
    angle = jnp.concatenate([angle, angle], axis=1)
    return (jnp.cos(angle), jnp.sin(angle))


def rotate(values, cosine, sine):
    half = values.shape[-1] // 2
    turned = jnp.concatenate([-values[..., half:], values[..., :half]], axis=-1)
    return values * cosine[:, None, :] + turned * sine[:, None, :]


def unrotate(grads, cosine, sine):
    half = grads.shape[-1] // 2
    scaled = grads * sine[:, None, :]
    turned = jnp.concatenate([-scaled[..., half:], scaled[..., :half]], axis=-1)
    return grads * cosine[:, None, :] - turned


def inverse_rms(values):
    return lax.rsqrt(jnp.mean(values * values, axis=-1, keepdims=True) + EPS)


def tdot(left, right):
    return lax.dot_general(
        left, right, (((0,), (0,)), ((), ())), preferred_element_type=jnp.float32
    )


def rdot(left, right):
    return lax.dot_general(
        left, right, (((1,), (1,)), ((), ())), preferred_element_type=jnp.float32
    )


def masked_scores(queries, keys, seg_rows, valid_rows, index_rows, segment_ids, index, scale):
    scores = jnp.einsum("qhd,khd->hqk", queries, keys, preferred_element_type=jnp.float32) * scale
    allowed = (seg_rows[:, None] == segment_ids[None, :]) & (
        index[None, :] <= index_rows[:, None]
    ) & valid_rows[:, None] | (index[None, :] == index_rows[:, None])
    return jnp.where(allowed[None], scores, NEGATIVE)


def forward_block(item, keys, values, segment_ids, index, scale):
    queries, seg_rows, valid_rows, index_rows = item
    scores = masked_scores(
        queries, keys, seg_rows, valid_rows, index_rows, segment_ids, index, scale
    )
    peak = jnp.max(scores, axis=-1, keepdims=True)
    expo = jnp.exp(scores - peak)
    summed = jnp.sum(expo, axis=-1, keepdims=True)
    probs = expo / summed
    mixed = jnp.einsum(
        "hqk,khd->qhd", probs.astype(jnp.bfloat16), values, preferred_element_type=jnp.float32
    )
    return (mixed, peak + jnp.log(summed))


def backward_block(carry, item, keys, values, segment_ids, index, scale):
    key_acc, value_acc = carry
    queries, grad_rows, lse_rows, seg_rows, valid_rows, index_rows = item
    scores = masked_scores(
        queries, keys, seg_rows, valid_rows, index_rows, segment_ids, index, scale
    )
    probs = jnp.exp(scores - lse_rows)
    value_acc = value_acc + jnp.einsum(
        "hqk,qhd->khd", probs.astype(jnp.bfloat16), grad_rows, preferred_element_type=jnp.float32
    )
    grad_probs = jnp.einsum("qhd,khd->hqk", grad_rows, values, preferred_element_type=jnp.float32)
    inner = jnp.sum(grad_probs * probs, axis=-1, keepdims=True)
    grad_scores = (probs * (grad_probs - inner) * scale).astype(jnp.bfloat16)
    query_grad = jnp.einsum("hqk,khd->qhd", grad_scores, keys, preferred_element_type=jnp.float32)
    key_acc = key_acc + jnp.einsum(
        "hqk,qhd->khd", grad_scores, queries, preferred_element_type=jnp.float32
    )
    return ((key_acc, value_acc), query_grad)


def local(
    tokens,
    w_query,
    w_key,
    w_value,
    w_out,
    w_gate,
    w_up,
    w_down,
    gain_attn,
    gain_ffn,
    lengths,
    cotangent,
):
    local_rows = tokens.shape[0]
    slots = local_rows * lax.axis_size("tensor")
    segment_ids, position, valid, index = layout(lengths[0], slots)
    own_valid = lax.dynamic_slice_in_dim(valid, lax.axis_index("tensor") * local_rows, local_rows)
    full_query, full_key, full_value, full_out, full_gate, full_up, full_down = (
        lax.all_gather(w_query, "dp", axis=0, tiled=True),
        lax.all_gather(w_key, "dp", axis=0, tiled=True),
        lax.all_gather(w_value, "dp", axis=0, tiled=True),
        lax.all_gather(w_out, "dp", axis=1, tiled=True),
        lax.all_gather(w_gate, "dp", axis=0, tiled=True),
        lax.all_gather(w_up, "dp", axis=0, tiled=True),
        lax.all_gather(w_down, "dp", axis=1, tiled=True),
    )
    heads_here = full_query.shape[1] // HEAD
    scale = HEAD ** (-0.5)
    cosine, sine = tables(position, HEAD)
    full_x = lax.all_gather(tokens, "tensor", axis=0, tiled=True)
    queries = rotate(
        jnp.dot(full_x, full_query, preferred_element_type=jnp.float32).reshape(
            slots, heads_here, HEAD
        ),
        cosine,
        sine,
    ).astype(jnp.bfloat16)
    keys = rotate(
        jnp.dot(full_x, full_key, preferred_element_type=jnp.float32).reshape(
            slots, heads_here, HEAD
        ),
        cosine,
        sine,
    ).astype(jnp.bfloat16)
    values = (
        jnp.dot(full_x, full_value, preferred_element_type=jnp.float32)
        .astype(jnp.bfloat16)
        .reshape(slots, heads_here, HEAD)
    )
    block = min(512, slots)
    blocks = slots // block
    query_blocks = queries.reshape(blocks, block, heads_here, HEAD)
    seg_blocks = segment_ids.reshape(blocks, block)
    valid_blocks = valid.reshape(blocks, block)
    index_blocks = index.reshape(blocks, block)
    runner = partial(
        forward_block, keys=keys, values=values, segment_ids=segment_ids, index=index, scale=scale
    )
    mixed, lse = lax.map(runner, (query_blocks, seg_blocks, valid_blocks, index_blocks))
    mixed = mixed.reshape(slots, heads_here * HEAD).astype(jnp.bfloat16)
    attn = lax.psum_scatter(
        jnp.dot(mixed, full_out, preferred_element_type=jnp.float32).astype(jnp.bfloat16),
        "tensor",
        scatter_dimension=0,
        tiled=True,
    ).astype(jnp.float32)
    first = tokens.astype(jnp.float32) + attn
    rms_first = inverse_rms(first)
    normed = first * rms_first * gain_attn
    full_normed = lax.all_gather(normed.astype(jnp.bfloat16), "tensor", axis=0, tiled=True)
    gate = jnp.dot(full_normed, full_gate, preferred_element_type=jnp.float32)
    upper = jnp.dot(full_normed, full_up, preferred_element_type=jnp.float32)
    sigma = jax.nn.sigmoid(gate)
    silu_gate = gate * sigma
    hidden = (silu_gate * upper).astype(jnp.bfloat16)
    ffn = lax.psum_scatter(
        jnp.dot(hidden, full_down, preferred_element_type=jnp.float32).astype(jnp.bfloat16),
        "tensor",
        scatter_dimension=0,
        tiled=True,
    ).astype(jnp.float32)
    second = normed + ffn
    rms_second = inverse_rms(second)
    output = jnp.where(own_valid[:, None], second * rms_second * gain_ffn, 0.0).astype(jnp.bfloat16)
    grad_y = jnp.where(own_valid[:, None], cotangent.astype(jnp.float32), 0.0)
    scaled_y = grad_y * gain_ffn
    part_gain_ffn = jnp.sum(grad_y * second * rms_second, axis=0)
    d_second = rms_second * scaled_y - second * rms_second**3 * jnp.mean(
        scaled_y * second, axis=-1, keepdims=True
    )
    full_d_ffn = lax.all_gather(d_second.astype(jnp.bfloat16), "tensor", axis=0, tiled=True)
    d_hidden = rdot(full_d_ffn, full_down)
    d_gate = (d_hidden * upper * sigma * (1.0 + gate * (1.0 - sigma))).astype(jnp.bfloat16)
    d_upper = (d_hidden * silu_gate).astype(jnp.bfloat16)
    grad_down = tdot(hidden, full_d_ffn)
    grad_gate = tdot(full_normed, d_gate)
    grad_up = tdot(full_normed, d_upper)
    d_normed = d_second + lax.psum_scatter(
        (rdot(d_gate, full_gate) + rdot(d_upper, full_up)).astype(jnp.bfloat16),
        "tensor",
        scatter_dimension=0,
        tiled=True,
    ).astype(jnp.float32)
    scaled_n = d_normed * gain_attn
    part_gain_attn = jnp.sum(d_normed * first * rms_first, axis=0)
    d_first = rms_first * scaled_n - first * rms_first**3 * jnp.mean(
        scaled_n * first, axis=-1, keepdims=True
    )
    full_d_attn = lax.all_gather(d_first.astype(jnp.bfloat16), "tensor", axis=0, tiled=True)
    grad_out = tdot(mixed, full_d_attn)
    d_mixed = (
        rdot(full_d_attn, full_out).astype(jnp.bfloat16).reshape(blocks, block, heads_here, HEAD)
    )
    stepper = partial(
        backward_block, keys=keys, values=values, segment_ids=segment_ids, index=index, scale=scale
    )
    empty = jnp.zeros((slots, heads_here, HEAD), jnp.float32)
    sums_kv, query_rot = lax.scan(
        stepper,
        (empty, empty),
        (query_blocks, d_mixed, lse, seg_blocks, valid_blocks, index_blocks),
    )
    key_rot, value_grad = sums_kv
    d_query = (
        unrotate(query_rot.reshape(slots, heads_here, HEAD), cosine, sine)
        .reshape(slots, heads_here * HEAD)
        .astype(jnp.bfloat16)
    )
    d_key = unrotate(key_rot, cosine, sine).reshape(slots, heads_here * HEAD).astype(jnp.bfloat16)
    d_value = value_grad.reshape(slots, heads_here * HEAD).astype(jnp.bfloat16)
    grad_query = tdot(full_x, d_query)
    grad_key = tdot(full_x, d_key)
    grad_value = tdot(full_x, d_value)
    input_grad = (
        d_first
        + lax.psum_scatter(
            (rdot(d_query, full_query) + rdot(d_key, full_key) + rdot(d_value, full_value)).astype(
                jnp.bfloat16
            ),
            "tensor",
            scatter_dimension=0,
            tiled=True,
        ).astype(jnp.float32)
    ).astype(jnp.bfloat16)
    grad_query, grad_key, grad_value, grad_out, grad_gate, grad_up, grad_down = (
        lax.psum_scatter(grad_query, "dp", scatter_dimension=0, tiled=True),
        lax.psum_scatter(grad_key, "dp", scatter_dimension=0, tiled=True),
        lax.psum_scatter(grad_value, "dp", scatter_dimension=0, tiled=True),
        lax.psum_scatter(grad_out, "dp", scatter_dimension=1, tiled=True),
        lax.psum_scatter(grad_gate, "dp", scatter_dimension=0, tiled=True),
        lax.psum_scatter(grad_up, "dp", scatter_dimension=0, tiled=True),
        lax.psum_scatter(grad_down, "dp", scatter_dimension=1, tiled=True),
    )
    gain_totals = lax.psum((part_gain_attn, part_gain_ffn), ("dp", "tensor"))
    return (
        output,
        input_grad,
        grad_query,
        grad_key,
        grad_value,
        grad_out,
        grad_gate,
        grad_up,
        grad_down,
        gain_totals[0],
        gain_totals[1],
    )


def solution(mesh):
    return jax.shard_map(
        local,
        mesh=mesh,
        in_specs=(
            P(("dp", "tensor"), None),
            P("dp", "tensor"),
            P("dp", "tensor"),
            P("dp", "tensor"),
            P("tensor", "dp"),
            P("dp", "tensor"),
            P("dp", "tensor"),
            P("tensor", "dp"),
            P(),
            P(),
            P("dp", None),
            P(("dp", "tensor"), None),
        ),
        out_specs=(
            P(("dp", "tensor"), None),
            P(("dp", "tensor"), None),
            P("dp", "tensor"),
            P("dp", "tensor"),
            P("dp", "tensor"),
            P("tensor", "dp"),
            P("dp", "tensor"),
            P("dp", "tensor"),
            P("tensor", "dp"),
            P(),
            P(),
        ),
        check_vma=False,
    )
```

profile of v0, /device:TPU:0, one launch (start us, length us, event | category | flops | bytes accessed | tf_op | source)
XLA Modules:
  0.0 2158.3 jit_solution(2219448435944795772)
XLA Ops:
  20.5 45.8 %all_gather.34 = bf16[768,384]{1,0:T(8,128)(2,1)S(1)} all-gather(bf16[48,384]{1,0:T(8,128)(2,1)S(1)} %copy-done.34), channel_id=1, replica_groups=mesh['dp'=16,'tensor'=2] {'dp'}, dimensions={0}, use_global_device_ids=true | all-gather | bytes 626688 | tf_op jit(solution)/shard_map/all_gather | solution.py:125
  66.3 39.0 %all_gather.35 = bf16[768,384]{1,0:T(8,128)(2,1)S(1)} all-gather(bf16[48,384]{1,0:T(8,128)(2,1)S(1)} %copy-done.35), channel_id=1, replica_groups=mesh['dp'=16,'tensor'=2] {'dp'}, dimensions={0}, use_global_device_ids=true | all-gather | bytes 626688 | tf_op jit(solution)/shard_map/all_gather | solution.py:126
  105.3 43.5 %all_gather.36 = bf16[768,384]{1,0:T(8,128)(2,1)} all-gather(bf16[48,384]{1,0:T(8,128)(2,1)S(1)} %copy-done.36), channel_id=1, replica_groups=mesh['dp'=16,'tensor'=2] {'dp'}, dimensions={0}, use_global_device_ids=true | all-gather | bytes 626688 | tf_op jit(solution)/shard_map/all_gather | solution.py:127
  148.8 41.7 %all_gather.37 = bf16[384,768]{0,1:T(8,128)(2,1)} all-gather(bf16[384,48]{0,1:T(8,128)(2,1)S(1)} %copy-done.37), channel_id=1, replica_groups=mesh['dp'=16,'tensor'=2] {'dp'}, dimensions={1}, use_global_device_ids=true | all-gather | bytes 626688 | tf_op jit(solution)/shard_map/all_gather | solution.py:128
  223.2 152.0 %while.30 = (s32[]{:T(128)}, bf16[4,512,6,64]{1,3,2,0:T(8,128)(2,1)}, f32[4,6,512,1]{2,1,3,0:T(8,128)S(1)}, s32[4,512]{1,0:T(4,128)S(1)}, s32[2048]{0:T(1024)S(1...) while((s32[]{:T(128)}, ...), condition=%wide.region_6.7_spmd.clone.clone, body=%wide.region_3.6_spmd.clone.clone.sunk | while | flops 1692398592 | bytes 96741056 | solution.py:165
  397.1 45.4 %all-gather.12.cloned.1.call-done = bf16[768,1024]{1,0:T(8,128)(2,1)} async-done(((bf16[48,1024]{1,0:T(8,128)(2,1)}), bf16[768,1024]{1,0:T(8,128)(2,1)}) %all-gather.12.cloned.1.call-update) | async-done | bytes 1572880 | tf_op jit(solution)/shard_map/all_gather | solution.py:129
  464.2 53.3 %all-gather.14.cloned.1.call-done = bf16[768,1024]{1,0:T(8,128)(2,1)} async-done(((bf16[48,1024]{1,0:T(8,128)(2,1)}), bf16[768,1024]{1,0:T(8,128)(2,1)}) %all-gather.14.cloned.1.call-update) | async-done | bytes 1572880 | tf_op jit(solution)/shard_map/all_gather | solution.py:130
  531.3 46.1 %all-gather.16.cloned.1.call-done = bf16[1024,768]{0,1:T(8,128)(2,1)} async-done(((bf16[1024,48]{0,1:T(8,128)(2,1)}), bf16[1024,768]{0,1:T(8,128)(2,1)}) %all-gather.16.cloned.1.call-update) | async-done | bytes 1572880 | tf_op jit(solution)/shard_map/all_gather | solution.py:131
  682.0 512.1 %while.31 = (s32[]{:T(128)}, f32[2048,6,64]{0,2,1:T(8,128)}, f32[2048,6,64]{0,2,1:T(8,128)}, f32[4,512,6,64]{1,0,3,2:T(4,128)}, bf16[4,512,6,64]{1,3,2,0:T(8,128...) while((s32[]{:T(128)}, f32[2048,6,64]{0,2,1:T(8,128)}, ...), condition=%wide.region_16.17_spmd.clone.clone, body=%wide.region_14.16_spmd.clone.clone.sunk | while | flops 4199557120 | bytes 286107392 | solution.py:224
  720.7 35.0 %fusion.196 = f32[1,512,6,64]{1,3,2,0:T(8,128)S(1)} fusion(bf16[2048,6,64]{0,2,1:T(8,128)(2,1)S(1)} %get-tuple-element.719, f32[6,512,2048]{2,1,0:T(8,128)} %fusion.193, f32[6,512,2048]{2,1,0:T(8,128)} %fusion.194, f32[6,512]{1,0:T(8,128)S(1)} %dynamic-slice_bitcast_fusion.2, pred[512,2048]{1,0:T(8,128)(4,1)S(1)} %fusion.195), kind=kOutput, calls=%fused_computation.50.clone.1 | convolution fusion | flops 874517504 | bytes 53751808 | tf_op jit(solution)/shard_map/while/body/eval_jaxpr/hqk,khd->qhd/dot_general | solution.py:99
  755.7 37.1 %bitcast_add_fusion.4 = f32[2048,6,64]{0,2,1:T(8,128)} fusion(f32[2048,6,64]{0,2,1:T(8,128)} %get-tuple-element.696, f32[6,512,2048]{2,1,0:T(8,128)} %fusion.193, f32[6,512,2048]{2,1,0:T(8,128)} %fusion.194, f32[6,512]{1,0:T(8,128)S(1)} %dynamic-slice_bitcast_fusion.2, pred[512,2048]{1,0:T(8,128)(4,1)S(1)} %fusion.195, pred[]{:T(512)S(6)} %compare.3, ...), kind=kOutput, calls=%fused_computation.49.clone.1 | convolution fusion | flops 876090368 | bytes 109477896 | tf_op jit(solution)/shard_map/while/body/eval_jaxpr/hqk,qhd->khd/dot_general | solution.py:100
  848.0 35.0 %fusion.196 = f32[1,512,6,64]{1,3,2,0:T(8,128)S(1)} fusion(bf16[2048,6,64]{0,2,1:T(8,128)(2,1)S(1)} %get-tuple-element.719, f32[6,512,2048]{2,1,0:T(8,128)} %fusion.193, f32[6,512,2048]{2,1,0:T(8,128)} %fusion.194, f32[6,512]{1,0:T(8,128)S(1)} %dynamic-slice_bitcast_fusion.2, pred[512,2048]{1,0:T(8,128)(4,1)S(1)} %fusion.195), kind=kOutput, calls=%fused_computation.50.clone.1 | convolution fusion | flops 874517504 | bytes 53751808 | tf_op jit(solution)/shard_map/while/body/eval_jaxpr/hqk,khd->qhd/dot_general | solution.py:99
  883.0 37.9 %bitcast_add_fusion.4 = f32[2048,6,64]{0,2,1:T(8,128)} fusion(f32[2048,6,64]{0,2,1:T(8,128)} %get-tuple-element.696, f32[6,512,2048]{2,1,0:T(8,128)} %fusion.193, f32[6,512,2048]{2,1,0:T(8,128)} %fusion.194, f32[6,512]{1,0:T(8,128)S(1)} %dynamic-slice_bitcast_fusion.2, pred[512,2048]{1,0:T(8,128)(4,1)S(1)} %fusion.195, pred[]{:T(512)S(6)} %compare.3, ...), kind=kOutput, calls=%fused_computation.49.clone.1 | convolution fusion | flops 876090368 | bytes 109477896 | tf_op jit(solution)/shard_map/while/body/eval_jaxpr/hqk,qhd->khd/dot_general | solution.py:100
  976.1 35.0 %fusion.196 = f32[1,512,6,64]{1,3,2,0:T(8,128)S(1)} fusion(bf16[2048,6,64]{0,2,1:T(8,128)(2,1)S(1)} %get-tuple-element.719, f32[6,512,2048]{2,1,0:T(8,128)} %fusion.193, f32[6,512,2048]{2,1,0:T(8,128)} %fusion.194, f32[6,512]{1,0:T(8,128)S(1)} %dynamic-slice_bitcast_fusion.2, pred[512,2048]{1,0:T(8,128)(4,1)S(1)} %fusion.195), kind=kOutput, calls=%fused_computation.50.clone.1 | convolution fusion | flops 874517504 | bytes 53751808 | tf_op jit(solution)/shard_map/while/body/eval_jaxpr/hqk,khd->qhd/dot_general | solution.py:99
  1011.1 37.9 %bitcast_add_fusion.4 = f32[2048,6,64]{0,2,1:T(8,128)} fusion(f32[2048,6,64]{0,2,1:T(8,128)} %get-tuple-element.696, f32[6,512,2048]{2,1,0:T(8,128)} %fusion.193, f32[6,512,2048]{2,1,0:T(8,128)} %fusion.194, f32[6,512]{1,0:T(8,128)S(1)} %dynamic-slice_bitcast_fusion.2, pred[512,2048]{1,0:T(8,128)(4,1)S(1)} %fusion.195, pred[]{:T(512)S(6)} %compare.3, ...), kind=kOutput, calls=%fused_computation.49.clone.1 | convolution fusion | flops 876090368 | bytes 109477896 | tf_op jit(solution)/shard_map/while/body/eval_jaxpr/hqk,qhd->khd/dot_general | solution.py:100
  1139.2 37.9 %bitcast_add_fusion.4 = f32[2048,6,64]{0,2,1:T(8,128)} fusion(f32[2048,6,64]{0,2,1:T(8,128)} %get-tuple-element.696, f32[6,512,2048]{2,1,0:T(8,128)} %fusion.193, f32[6,512,2048]{2,1,0:T(8,128)} %fusion.194, f32[6,512]{1,0:T(8,128)S(1)} %dynamic-slice_bitcast_fusion.2, pred[512,2048]{1,0:T(8,128)(4,1)S(1)} %fusion.195, pred[]{:T(512)S(6)} %compare.3, ...), kind=kOutput, calls=%fused_computation.49.clone.1 | convolution fusion | flops 876090368 | bytes 109477896 | tf_op jit(solution)/shard_map/while/body/eval_jaxpr/hqk,qhd->khd/dot_general | solution.py:100
  1269.7 40.7 %all-reduce = (f32[768]{0:T(1024)}, f32[768]{0:T(1024)}) all-reduce(f32[768]{0:T(1024)S(1)} %copy-done.38, f32[768]{0:T(1024)S(1)} %copy-done.40), channel_id=1, replica_groups=mesh['dp'=16,'tensor'=2] {'dp','tensor'}, use_global_device_ids=true, to_apply=%region_26.27 | all-reduce | flops 1536 | bytes 12288 | tf_op jit(solution)/shard_map/psum | solution.py:260
  1314.2 53.9 %reduce-scatter.32.cloned.1.call-done = f32[1024,48]{0,1:T(8,128)} async-done(((f32[1024,768]{0,1:T(8,128)}), f32[1024,48]{0,1:T(8,128)}) %reduce-scatter.32.cloned.1.call-update) | async-done | bytes 196624 | tf_op jit(solution)/shard_map/reduce_scatter | solution.py:258
  1368.2 135.4 %reduce-scatter.28.cloned.1.call-done = f32[48,1024]{1,0:T(8,128)} async-done(((f32[768,1024]{1,0:T(8,128)}), f32[48,1024]{1,0:T(8,128)}) %reduce-scatter.28.cloned.1.call-update) | async-done | bytes 196624 | tf_op jit(solution)/shard_map/reduce_scatter | solution.py:256
  1503.6 135.4 %reduce-scatter.30.cloned.1.call-done = f32[48,1024]{1,0:T(8,128)} async-done(((f32[768,1024]{1,0:T(8,128)}), f32[48,1024]{1,0:T(8,128)}) %reduce-scatter.30.cloned.1.call-update) | async-done | bytes 196624 | tf_op jit(solution)/shard_map/reduce_scatter | solution.py:257
  1639.0 128.2 %reduce-scatter.26.cloned.1.call-done = f32[384,48]{0,1:T(8,128)} async-done(((f32[384,768]{0,1:T(8,128)}), f32[384,48]{0,1:T(8,128)}) %reduce-scatter.26.cloned.1.call-update) | async-done | bytes 73744 | tf_op jit(solution)/shard_map/reduce_scatter | solution.py:255
  1767.2 127.8 %reduce-scatter.38.cloned.1.call-done = f32[48,384]{1,0:T(8,128)} async-done(((f32[768,384]{1,0:T(8,128)}), f32[48,384]{1,0:T(8,128)}) %reduce-scatter.38.cloned.1.call-update) | async-done | bytes 73744
  1895.0 127.9 %reduce-scatter.36.cloned.1.call-done = f32[48,384]{1,0:T(8,128)} async-done(((f32[768,384]{1,0:T(8,128)}), f32[48,384]{1,0:T(8,128)}) %reduce-scatter.36.cloned.1.call-update) | async-done | bytes 73744
  2022.9 127.7 %reduce-scatter.34.cloned.1.call-done = f32[48,384]{1,0:T(8,128)} async-done(((f32[768,384]{1,0:T(8,128)}), f32[48,384]{1,0:T(8,128)}) %reduce-scatter.34.cloned.1.call-update) | async-done | bytes 73744
  (311 shorter events, 692.7 us)
Async XLA Ops:
  8.0 12.5 copy-start.34
  8.0 58.3 %copy-start.35 = (bf16[48,384]{1,0:T(8,128)(2,1)S(1)}, bf16[48,384]{1,0:T(8,128)(2,1)}, u32[]{:S(2)}) copy-start(bf16[48,384]{1,0:T(8,128)(2,1)} %param.18) | copy-start | bytes 110596
  8.0 97.3 %copy-start.36 = (bf16[48,384]{1,0:T(8,128)(2,1)S(1)}, bf16[48,384]{1,0:T(8,128)(2,1)}, u32[]{:S(2)}) copy-start(bf16[48,384]{1,0:T(8,128)(2,1)} %param.19) | copy-start | bytes 110596
  8.0 140.8 %copy-start.37 = (bf16[384,48]{0,1:T(8,128)(2,1)S(1)}, bf16[384,48]{0,1:T(8,128)(2,1)}, u32[]{:S(2)}) copy-start(bf16[384,48]{0,1:T(8,128)(2,1)} %param.20) | copy-start | bytes 110596
  8.0 182.5 %all-gather.8.cloned.1.call-start = ((), (), s32[]{:S(2)}) async-start(), calls=%async_computation.11 | async-start | bytes 4718592 | tf_op jit(solution)/shard_map/all_gather | solution.py:136
  8.8 383.0 %reduce-scatter.18.cloned.1.call-start = ((), (), s32[]{:S(2)}) async-start(), calls=%async_computation.12 | async-start | bytes 4718592 | tf_op jit(solution)/shard_map/reduce_scatter | solution.py:167
  66.3 129.3 %copy-start.27 = (bf16[768,384]{1,0:T(8,128)(2,1)}, bf16[768,384]{1,0:T(8,128)(2,1)S(1)}, u32[]{:S(2)}) copy-start(bf16[768,384]{1,0:T(8,128)(2,1)S(1)} %all_gather.34) | copy-start | bytes 1769476
  105.3 95.5 %copy-start.25 = (bf16[768,384]{1,0:T(8,128)(2,1)}, bf16[768,384]{1,0:T(8,128)(2,1)S(1)}, u32[]{:S(2)}) copy-start(bf16[768,384]{1,0:T(8,128)(2,1)S(1)} %all_gather.35) | copy-start | bytes 1769476
  383.6 59.0 %all-gather.12.cloned.1.call-start = ((), (), s32[]{:S(2)}) async-start(), calls=%async_computation.14 | async-start | bytes 1671168 | tf_op jit(solution)/shard_map/all_gather | solution.py:129
  384.1 71.0 %all-gather.10.cloned.1.call-start = ((), (), s32[]{:S(2)}) async-start(), calls=%async_computation.13 | async-start | bytes 4718592 | tf_op jit(solution)/shard_map/all_gather | solution.py:176
  395.7 121.8 %all-gather.14.cloned.1.call-start = ((), (), s32[]{:S(2)}) async-start(), calls=%async_computation.15 | async-start | bytes 1671168 | tf_op jit(solution)/shard_map/all_gather | solution.py:130
  396.3 181.1 %all-gather.16.cloned.1.call-start = ((), (), s32[]{:S(2)}) async-start(), calls=%async_computation.16 | async-start | bytes 1671168 | tf_op jit(solution)/shard_map/all_gather | solution.py:131
  397.1 197.8 %reduce-scatter.20.cloned.1.call-start = ((), (), s32[]{:S(2)}) async-start(), calls=%async_computation.17 | async-start | bytes 4718592 | tf_op jit(solution)/shard_map/reduce_scatter | solution.py:182
  585.2 31.5 %all-gather.18.cloned.1.call-start = ((), (), s32[]{:S(2)}) async-start(), calls=%async_computation.18 | async-start | bytes 4718592 | tf_op jit(solution)/shard_map/all_gather | solution.py:197
  603.5 45.3 %reduce-scatter.22.cloned.1.call-start = ((), (), s32[]{:S(2)}) async-start(), calls=%async_computation.19 | async-start | bytes 4718592 | tf_op jit(solution)/shard_map/reduce_scatter | solution.py:204
  636.8 33.3 %all-gather.20.cloned.1.call-start = ((), (), s32[]{:S(2)}) async-start(), calls=%async_computation.20 | async-start | bytes 4718592 | tf_op jit(solution)/shard_map/all_gather | solution.py:215
  656.6 653.8 %reduce-scatter.24.cloned.1.call-start = ((), (), s32[]{:S(2)}) async-start(), calls=%async_computation.21 | async-start | bytes 4718592 | tf_op jit(solution)/shard_map/reduce_scatter | solution.py:242
  1219.0 149.2 %reduce-scatter.32.cloned.1.call-start = ((), (), s32[]{:S(2)}) async-start(), calls=%async_computation.25 | async-start | bytes 3342336 | tf_op jit(solution)/shard_map/reduce_scatter | solution.py:258
  1227.5 276.1 %reduce-scatter.28.cloned.1.call-start = ((), (), s32[]{:S(2)}) async-start(), calls=%async_computation.23 | async-start | bytes 3342336 | tf_op jit(solution)/shard_map/reduce_scatter | solution.py:256
  1236.3 402.7 %reduce-scatter.30.cloned.1.call-start = ((), (), s32[]{:S(2)}) async-start(), calls=%async_computation.24 | async-start | bytes 3342336 | tf_op jit(solution)/shard_map/reduce_scatter | solution.py:257
  1244.6 522.6 %reduce-scatter.26.cloned.1.call-start = ((), (), s32[]{:S(2)}) async-start(), calls=%async_computation.22 | async-start | bytes 1253376 | tf_op jit(solution)/shard_map/reduce_scatter | solution.py:255
  1250.0 645.0 %reduce-scatter.38.cloned.1.call-start = ((), (), s32[]{:S(2)}) async-start(), calls=%async_computation.28 | async-start | bytes 1253376
  1257.8 765.1 %reduce-scatter.36.cloned.1.call-start = ((), (), s32[]{:S(2)}) async-start(), calls=%async_computation.27 | async-start | bytes 1253376
  1264.9 885.7 %reduce-scatter.34.cloned.1.call-start = ((), (), s32[]{:S(2)}) async-start(), calls=%async_computation.26 | async-start | bytes 1253376
  (55 other events, 287.7 us)
Sparse Core Ops, SparseCore 0:
  10.4 14.8 all-gather.7
  383.7 8.0 reduce-scatter.17
  585.4 9.4 reduce-scatter.19
  656.7 13.3 all-gather.19
  1219.1 12.0 reduce-scatter.23
  1236.6 131.5 reduce-scatter.31
  1373.7 129.8 reduce-scatter.27
  1509.1 129.8 reduce-scatter.29
  1644.3 122.7 reduce-scatter.25
  1772.4 122.5 reduce-scatter.37
  1900.3 122.5 reduce-scatter.35
  2028.1 122.5 reduce-scatter.33
Sparse Core Ops, SparseCore 1:
  387.2 55.3 all-gather.11
  444.6 10.5 all-gather.9
  458.2 59.3 all-gather.13
  520.7 56.6 all-gather.15
  603.6 13.1 all-gather.17
  636.9 11.9 reduce-scatter.21
where the time goes:
time: 2160 us
  waiting for transfers between devices  1050 us (49%)
  matrix products  641 us (30%)
  blocking collectives  211 us (10%)
  local copies, waits for them, and re-layouts  124 us (6%)
  other arithmetic  112 us (5%)
    unnamed x21, waiting for transfers between devices  386 us
    dot_general x4, matrix products, backward_block(): jnp.einsum('hqk,qhd->khd', grad_scores, queries, preferred_element_type=j...  151 us
    dot_general x4, matrix products, backward_block(): jnp.einsum('hqk,khd->qhd', grad_scores, keys, preferred_element_type=jnp....  140 us
    reduce_scatter x1, waiting for transfers between devices, local(): lax.psum_scatter(grad_gate, 'dp', scatter_dimension=0, tiled=True)  135 us
    reduce_scatter x1, waiting for transfers between devices, local(): lax.psum_scatter(grad_up, 'dp', scatter_dimension=0, tiled=True)  135 us
    reduce_scatter x1, waiting for transfers between devices, local(): lax.psum_scatter(grad_out, 'dp', scatter_dimension=1, tiled=True)  128 us
    dot_general x8, matrix products, masked_scores(): jnp.einsum('qhd,khd->hqk', queries, keys, preferred_element_type=jnp.floa...  88 us
    dynamic_update_slice x8, local copies, waits for them, and re-layouts, local(): lax.map(runner, (query_blocks, seg_blocks, valid_blocks, index_blocks))  67.4 us
  transfers between devices with their start and end apart: 18, of which 16 were waited for; matrix products, arithmetic and copies ran while one was open for 4% of the time, Pallas kernels for 0%

commit v1 on v0

v1 whole, which is shorter than its diff:
```python
from functools import partial

import jax
import jax.numpy as jnp
from jax import lax
from jax.experimental import pallas as pl
from jax.experimental.pallas import tpu as pltpu
from jax.sharding import PartitionSpec as P

HEAD = 64
PAIR = 2 * HEAD
EPS = 1e-05
ROPE_BASE = 10000.0
NEGATIVE = -1e30
F32 = jnp.float32
BF16 = jnp.bfloat16
VMEM_LIMIT = 56 * 1024 * 1024


def mm(left, right):
    return jnp.dot(left, right, preferred_element_type=F32)


def rdot(left, right):
    return lax.dot_general(left, right, (((1,), (1,)), ((), ())), preferred_element_type=F32)


def tdot(left, right):
    return lax.dot_general(left, right, (((0,), (0,)), ((), ())), preferred_element_type=F32)


def params(limit=VMEM_LIMIT, dims=1):
    return pltpu.CompilerParams(
        vmem_limit_bytes=limit, dimension_semantics=("arbitrary",) * dims
    )


def cost(flops, nbytes, trans=0):
    return pl.CostEstimate(flops=int(flops), bytes_accessed=int(nbytes), transcendentals=int(trans))


def swap_halves(values):
    lane = lax.broadcasted_iota(jnp.int32, values.shape, 1) % HEAD
    half = HEAD // 2
    width = values.shape[1]
    return jnp.where(
        lane < half, pltpu.roll(values, width - half, 1), pltpu.roll(values, half, 1)
    )


def project_kernel(sched, own_ref, oth_ref, wq_ref, wk_ref, wv_ref, cos_ref, sin_ref,
                   q_ref, k_ref, v_ref, vt_ref, *, half):
    step = pl.program_id(0)
    x = jnp.where(step < half, own_ref[...], oth_ref[...])
    cosine, sine = cos_ref[...], sin_ref[...]
    width = wq_ref.shape[1]
    for w_ref, out_ref, scale in ((wq_ref, q_ref, HEAD ** -0.5), (wk_ref, k_ref, 1.0)):
        u = mm(x, w_ref[...])
        for at in range(0, width, PAIR):
            piece = u[:, at:at + PAIR]
            turned = piece * cosine + swap_halves(piece) * sine
            out_ref[:, at:at + PAIR] = (turned * scale).astype(BF16)
    v = mm(x, wv_ref[...])
    v_ref[...] = v.astype(BF16)
    vt_ref[...] = v.T.astype(BF16)


def project(sched, own, oth, wq, wk, wv, cosine, sine, block):
    rows, width = own.shape[0], own.shape[1]
    slots = 2 * rows
    half = rows // block
    cols = wq.shape[1]

    def place(step, sched):
        return lax.rem(step + sched[0] * half, 2 * half)

    weight = pl.BlockSpec((width, cols), lambda s, sched: (0, 0))
    table = pl.BlockSpec((block, PAIR), lambda s, sched: (place(s, sched), 0))
    out = pl.BlockSpec((block, cols), lambda s, sched: (place(s, sched), 0))
    return pl.pallas_call(
        partial(project_kernel, half=half),
        grid_spec=pltpu.PrefetchScalarGridSpec(
            num_scalar_prefetch=1,
            grid=(2 * half,),
            in_specs=[
                pl.BlockSpec((block, width), lambda s, sched: (jnp.minimum(s, half - 1), 0)),
                pl.BlockSpec((block, width), lambda s, sched: (jnp.maximum(s - half, 0), 0)),
                weight, weight, weight, table, table,
            ],
            out_specs=[out, out, out,
                       pl.BlockSpec((cols, block), lambda s, sched: (0, place(s, sched)))],
        ),
        out_shape=[jax.ShapeDtypeStruct((slots, cols), BF16)] * 3
        + [jax.ShapeDtypeStruct((cols, slots), BF16)],
        compiler_params=params(),
        cost_estimate=cost(6 * slots * width * cols, 14 * slots * cols),
        name="project",
    )(sched, own, oth, wq, wk, wv, cosine, sine)


def head_masks(values):
    lane = lax.broadcasted_iota(jnp.int32, (1, PAIR), 1)
    low = (lane < HEAD).astype(values.dtype)
    return (values * low, values * (1 - low))


def allowed_block(start, key_at, query_at, bk, bq):
    key_index = key_at + lax.broadcasted_iota(jnp.int32, (bk, bq), 0)
    query_index = query_at + lax.broadcasted_iota(jnp.int32, (bk, bq), 1)
    return (key_index >= start) & (key_index <= query_index)


def forward_kernel(sched, q_ref, k_ref, vt_ref, start_ref, oth_ref, own_ref, lse_ref, acc_ref,
                   *, bq, bk, blocks):
    step = pl.program_id(1)
    half = blocks // 2
    i = lax.rem(step + (1 - sched[0]) * half, blocks)
    queries = head_masks(q_ref[...])
    start = start_ref[...]
    ratio = bq // bk
    acc_ref[...] = jnp.zeros_like(acc_ref)

    def visit(j, carry, masked):
        at = pl.multiple_of(j * bk, bk)
        keys = k_ref[pl.ds(at, bk), :]
        if masked:
            allowed = allowed_block(start, at, i * bq, bk, bq)
        out = []
        for h in range(2):
            peak, total = carry[2 * h], carry[2 * h + 1]
            scores = rdot(keys, queries[h])
            if masked:
                scores = jnp.where(allowed, scores, NEGATIVE)
            new_peak = jnp.maximum(peak, jnp.max(scores, axis=0, keepdims=True))
            fade = jnp.exp(peak - new_peak)
            expo = jnp.exp(scores - new_peak)
            total = total * fade + jnp.sum(expo, axis=0, keepdims=True)
            rows = pl.ds(h * HEAD, HEAD)
            acc_ref[rows, :] = acc_ref[rows, :] * fade + mm(
                vt_ref[rows, pl.ds(at, bk)], expo.astype(BF16)
            )
            out += [new_peak, total]
        return tuple(out)

    low = sched[2 + i]
    mid = jnp.minimum(sched[2 + blocks + i], i * ratio)
    carry = (jnp.full((1, bq), NEGATIVE, F32), jnp.zeros((1, bq), F32)) * 2
    carry = lax.fori_loop(low, mid, lambda j, c: visit(j, c, True), carry)
    carry = lax.fori_loop(jnp.maximum(low, mid), i * ratio, lambda j, c: visit(j, c, False), carry)
    for d in range(ratio):
        carry = visit(i * ratio + d, carry, True)
    result = []
    for h in range(2):
        peak, total = carry[2 * h], carry[2 * h + 1]
        result.append(acc_ref[h * HEAD:(h + 1) * HEAD, :] / total)
        lse_ref[h:h + 1, :] = peak + jnp.log(total)
    mixed = jnp.concatenate(result, axis=0).T.astype(BF16)

    @pl.when(step < half)
    def _():
        oth_ref[...] = mixed

    @pl.when(step >= half)
    def _():
        own_ref[...] = mixed


def attend_forward(sched, q, k, vt, start, bq, bk):
    slots, cols = q.shape
    pairs, blocks = cols // PAIR, slots // bq
    half = blocks // 2

    def place(n, sched):
        return lax.rem(n + (1 - sched[0]) * half, blocks)

    return pl.pallas_call(
        partial(forward_kernel, bq=bq, bk=bk, blocks=blocks),
        grid_spec=pltpu.PrefetchScalarGridSpec(
            num_scalar_prefetch=1,
            grid=(pairs, blocks),
            in_specs=[
                pl.BlockSpec((bq, PAIR), lambda p, n, s: (place(n, s), p)),
                pl.BlockSpec((slots, PAIR), lambda p, n, s: (0, p)),
                pl.BlockSpec((PAIR, slots), lambda p, n, s: (p, 0)),
                pl.BlockSpec((1, bq), lambda p, n, s: (0, place(n, s))),
            ],
            out_specs=[
                pl.BlockSpec((bq, PAIR), lambda p, n, s: (jnp.minimum(n, half - 1), p)),
                pl.BlockSpec((bq, PAIR), lambda p, n, s: (jnp.maximum(n - half, 0), p)),
                pl.BlockSpec((None, 2, bq), lambda p, n, s: (p, 0, place(n, s))),
            ],
            scratch_shapes=[pltpu.VMEM((PAIR, bq), F32)],
        ),
        out_shape=[
            jax.ShapeDtypeStruct((slots // 2, cols), BF16),
            jax.ShapeDtypeStruct((slots // 2, cols), BF16),
            jax.ShapeDtypeStruct((pairs, 2, slots), F32),
        ],
        compiler_params=params(dims=2),
        cost_estimate=cost(2 * slots * slots * cols * 2, 8 * slots * cols, slots * slots * 6),
        name="attend_forward",
    )(sched, q, k, vt, start)


def backward_kernel(sched, q_ref, k_ref, v_ref, cos_ref, sin_ref, start_ref, lse_ref,
                    o_oth_ref, o_own_ref, g_oth_ref, g_own_ref,
                    dq_ref, dk_ref, dv_ref, kt_ref, dqt_ref, dk_acc, dv_acc, *, bq, bk, blocks):
    step = pl.program_id(1)
    half = blocks // 2
    i = lax.rem(step + (1 - sched[0]) * half, blocks)
    ratio = bq // bk

    @pl.when(step == 0)
    def _():
        kt_ref[...] = k_ref[...].astype(F32).T.astype(BF16)
        dk_acc[...] = jnp.zeros_like(dk_acc)
        dv_acc[...] = jnp.zeros_like(dv_acc)

    first = step < half
    grads = jnp.where(first, g_oth_ref[...], g_own_ref[...])
    mixed = jnp.where(first, o_oth_ref[...], o_own_ref[...])
    queries = head_masks(q_ref[...])
    couts = head_masks(grads)
    start = start_ref[...]
    product = grads.astype(F32) * mixed.astype(F32)
    big = product.astype(BF16)
    small = (product - big.astype(F32)).astype(BF16)
    row = lax.broadcasted_iota(jnp.int32, (16, PAIR), 0)
    lane = lax.broadcasted_iota(jnp.int32, (16, PAIR), 1)
    pick = jnp.where(lane // HEAD == row, 1.0, 0.0).astype(BF16)
    inner = rdot(pick, big) + rdot(pick, small)
    lse = lse_ref[...]
    dqt_ref[...] = jnp.zeros_like(dqt_ref)

    def visit(j, masked):
        at = pl.multiple_of(j * bk, bk)
        where = pl.ds(at, bk)
        keys, values = k_ref[where, :], v_ref[where, :]
        if masked:
            allowed = allowed_block(start, at, i * bq, bk, bq)
        dk_part, dv_part = [], []
        for h in range(2):
            rows = pl.ds(h * HEAD, HEAD)
            probs = jnp.exp(rdot(keys, queries[h]) - lse[h:h + 1, :])
            if masked:
                probs = jnp.where(allowed, probs, 0.0)
            d_probs = rdot(values, couts[h])
            d_scores = (probs * (d_probs - inner[h:h + 1, :])).astype(BF16)
            dv_part.append(mm(probs.astype(BF16), couts[h]))
            dk_part.append(mm(d_scores, queries[h]))
            dqt_ref[rows, :] += mm(kt_ref[rows, where], d_scores)
        dk_acc[where, :] += dk_part[0] + dk_part[1]
        dv_acc[where, :] += dv_part[0] + dv_part[1]

    low = sched[2 + i]
    mid = jnp.minimum(sched[2 + blocks + i], i * ratio)

    @pl.loop(low, mid)
    def _(j):
        visit(j, True)

    @pl.loop(jnp.maximum(low, mid), i * ratio)
    def _(j):
        visit(j, False)

    for d in range(ratio):
        visit(i * ratio + d, True)

    def unrotate(g, cosine, sine):
        return g * cosine - swap_halves(g) * sine

    here = pl.ds(pl.multiple_of(i * bq, bq), bq)
    dq = dqt_ref[...].T * (HEAD ** -0.5)
    dq_ref[...] = unrotate(dq, cos_ref[here, :], sin_ref[here, :]).astype(BF16)

    @pl.when(step == blocks - 1)
    def _():
        dk_ref[...] = unrotate(dk_acc[...], cos_ref[...], sin_ref[...]).astype(BF16)
        dv_ref[...] = dv_acc[...].astype(BF16)


def attend_backward(sched, q, k, v, cosine, sine, start, lse, o_oth, o_own, g_oth, g_own, bq, bk):
    slots, cols = q.shape
    pairs, blocks = cols // PAIR, slots // bq
    half = blocks // 2

    def place(n, sched):
        return lax.rem(n + (1 - sched[0]) * half, blocks)

    whole = pl.BlockSpec((slots, PAIR), lambda p, n, s: (0, p))
    table = pl.BlockSpec((slots, PAIR), lambda p, n, s: (0, 0))
    oth = pl.BlockSpec((bq, PAIR), lambda p, n, s: (jnp.minimum(n, half - 1), p))
    own = pl.BlockSpec((bq, PAIR), lambda p, n, s: (jnp.maximum(n - half, 0), p))
    query = pl.BlockSpec((bq, PAIR), lambda p, n, s: (place(n, s), p))
    return pl.pallas_call(
        partial(backward_kernel, bq=bq, bk=bk, blocks=blocks),
        grid_spec=pltpu.PrefetchScalarGridSpec(
            num_scalar_prefetch=1,
            grid=(pairs, blocks),
            in_specs=[
                query, whole, whole, table, table,
                pl.BlockSpec((1, bq), lambda p, n, s: (0, place(n, s))),
                pl.BlockSpec((None, 2, bq), lambda p, n, s: (p, 0, place(n, s))),
                oth, own, oth, own,
            ],
            out_specs=[query, whole, whole],
            scratch_shapes=[
                pltpu.VMEM((PAIR, slots), BF16),
                pltpu.VMEM((PAIR, bq), F32),
                pltpu.VMEM((slots, PAIR), F32),
                pltpu.VMEM((slots, PAIR), F32),
            ],
        ),
        out_shape=[jax.ShapeDtypeStruct((slots, cols), BF16)] * 3,
        compiler_params=params(dims=2),
        cost_estimate=cost(5 * slots * slots * cols * 2, 20 * slots * cols, slots * slots * 6),
        name="attend_backward",
    )(sched, q, k, v, cosine, sine, start, lse, o_oth, o_own, g_oth, g_own)


def feed_kernel(sched, x_ref, own_ref, oth_ref, dy_ref, w_ref, ga_ref, gf_ref,
                out_ref, dfirst_ref, gown_ref, goth_ref, normed_ref, dffn_ref, dattn_ref,
                hidden_ref, dgate_ref, dup_ref, gains_ref,
                gate_s, up_s, sig_s, *, block, local, hid, head_cols):
    step = pl.program_id(0)
    me = sched[0]
    out_at = 3 * hid
    outs = slice(out_at, out_at + head_cols)
    x = x_ref[...].astype(F32)
    attn = rdot(own_ref[...], w_ref[me, :, outs]) + rdot(oth_ref[...], w_ref[1 - me, :, outs])
    first = x + attn
    rms1 = lax.rsqrt(jnp.mean(first * first, axis=-1, keepdims=True) + EPS)
    unit1 = first * rms1
    normed = unit1 * ga_ref[...]
    normed_b = normed.astype(BF16)
    normed_ref[...] = normed_b
    ffn = None
    for t in range(2):
        cols = slice(t * hid, (t + 1) * hid)
        gate = mm(normed_b, w_ref[t, :, 0:hid])
        upper = mm(normed_b, w_ref[t, :, hid:2 * hid])
        sigma = 1.0 / (1.0 + jnp.exp(-gate))
        hidden = (gate * sigma * upper).astype(BF16)
        gate_s[:, cols] = gate
        up_s[:, cols] = upper
        sig_s[:, cols] = sigma
        hidden_ref[:, cols] = hidden
        part = rdot(hidden, w_ref[t, :, 2 * hid:3 * hid])
        ffn = part if ffn is None else ffn + part
    second = normed + ffn
    rms2 = lax.rsqrt(jnp.mean(second * second, axis=-1, keepdims=True) + EPS)
    unit2 = second * rms2
    slot = me * local + step * block + lax.broadcasted_iota(jnp.int32, (block, 1), 0)
    valid = slot < sched[1]
    out_ref[...] = jnp.where(valid, unit2 * gf_ref[...], 0.0).astype(BF16)
    dy = jnp.where(valid, dy_ref[...].astype(F32), 0.0)
    gain_ffn = jnp.sum(dy * unit2, axis=0, keepdims=True)
    scaled = dy * gf_ref[...]
    d_second = rms2 * (scaled - unit2 * jnp.mean(scaled * unit2, axis=-1, keepdims=True))
    d_ffn = d_second.astype(BF16)
    dffn_ref[...] = d_ffn
    d_normed = d_second
    for t in range(2):
        cols = slice(t * hid, (t + 1) * hid)
        d_hidden = mm(d_ffn, w_ref[t, :, 2 * hid:3 * hid])
        gate, sigma = gate_s[:, cols], sig_s[:, cols]
        slope = d_hidden * sigma
        d_gate = (slope * up_s[:, cols] * (1.0 + gate * (1.0 - sigma))).astype(BF16)
        d_up = (slope * gate).astype(BF16)
        dgate_ref[:, cols] = d_gate
        dup_ref[:, cols] = d_up
        d_normed = d_normed + rdot(d_gate, w_ref[t, :, 0:hid]) + rdot(d_up, w_ref[t, :, hid:2 * hid])
    gain_attn = jnp.sum(d_normed * unit1, axis=0, keepdims=True)
    scaled = d_normed * ga_ref[...]
    d_first = rms1 * (scaled - unit1 * jnp.mean(scaled * unit1, axis=-1, keepdims=True))
    dfirst_ref[...] = d_first
    d_attn = d_first.astype(BF16)
    dattn_ref[...] = d_attn
    gown_ref[...] = mm(d_attn, w_ref[me, :, outs]).astype(BF16)
    goth_ref[...] = mm(d_attn, w_ref[1 - me, :, outs]).astype(BF16)

    @pl.when(step == 0)
    def _():
        gains_ref[...] = jnp.zeros_like(gains_ref)

    gains_ref[0:1, :] += gain_attn
    gains_ref[1:2, :] += gain_ffn


def feed(sched, x, own, oth, dy, weights, gain_attn, gain_ffn, hid, block):
    local, width = x.shape
    head_cols = own.shape[1]
    rows = pl.BlockSpec((block, width), lambda s, sched: (s, 0))
    heads = pl.BlockSpec((block, head_cols), lambda s, sched: (s, 0))
    wide = pl.BlockSpec((block, 2 * hid), lambda s, sched: (s, 0))
    gain = pl.BlockSpec((1, width), lambda s, sched: (0, 0))
    full = pl.BlockSpec(weights.shape, lambda s, sched: (0, 0, 0), pipeline_mode=pl.Buffered(1))

    def shape(cols, dtype):
        return jax.ShapeDtypeStruct((local, cols), dtype)

    return pl.pallas_call(
        partial(feed_kernel, block=block, local=local, hid=hid, head_cols=head_cols),
        grid_spec=pltpu.PrefetchScalarGridSpec(
            num_scalar_prefetch=1,
            grid=(local // block,),
            in_specs=[rows, heads, heads, rows, full, gain, gain],
            out_specs=[rows, rows, heads, heads, rows, rows, rows, wide, wide, wide,
                       pl.BlockSpec((8, width), lambda s, sched: (0, 0))],
            scratch_shapes=[pltpu.VMEM((block, 2 * hid), F32)] * 3,
        ),
        out_shape=[
            shape(width, BF16), shape(width, F32), shape(head_cols, BF16), shape(head_cols, BF16),
            shape(width, BF16), shape(width, BF16), shape(width, BF16),
            shape(2 * hid, BF16), shape(2 * hid, BF16), shape(2 * hid, BF16),
            jax.ShapeDtypeStruct((8, width), F32),
        ],
        compiler_params=params(),
        cost_estimate=cost(8 * local * width * (3 * hid + head_cols) , 30 * local * width),
        name="feed",
    )(sched, x, own, oth, dy, weights, gain_attn, gain_ffn)


def weight_grad_kernel(sched, normed_ref, dffn_ref, dattn_ref, hidden_ref, dgate_ref, dup_ref,
                       own_ref, oth_ref, out_ref, *, hid):
    t = pl.program_id(0)
    normed, d_ffn = normed_ref[...], dffn_ref[...]
    out_ref[0, :, 0:hid] = tdot(normed, dgate_ref[...]).astype(BF16)
    out_ref[0, :, hid:2 * hid] = tdot(normed, dup_ref[...]).astype(BF16)
    out_ref[0, :, 2 * hid:3 * hid] = tdot(d_ffn, hidden_ref[...]).astype(BF16)
    mixed = jnp.where(t == sched[0], own_ref[...], oth_ref[...])
    out_ref[0, :, 3 * hid:] = tdot(dattn_ref[...], mixed).astype(BF16)


def weight_grads(sched, normed, d_ffn, d_attn, hidden, d_gate, d_up, own, oth, hid):
    local, width = normed.shape
    head_cols = own.shape[1]
    total = 3 * hid + head_cols
    rows = pl.BlockSpec((local, width), lambda t, sched: (0, 0))
    heads = pl.BlockSpec((local, head_cols), lambda t, sched: (0, 0))
    wide = pl.BlockSpec((local, hid), lambda t, sched: (0, t))
    return pl.pallas_call(
        partial(weight_grad_kernel, hid=hid),
        grid_spec=pltpu.PrefetchScalarGridSpec(
            num_scalar_prefetch=1,
            grid=(2,),
            in_specs=[rows, rows, rows, wide, wide, wide, heads, heads],
            out_specs=pl.BlockSpec((1, width, total), lambda t, sched: (t, 0, 0)),
        ),
        out_shape=jax.ShapeDtypeStruct((2, width, total), BF16),
        compiler_params=params(),
        cost_estimate=cost(4 * local * width * total, 8 * local * total),
        name="weight_grads",
    )(sched, normed, d_ffn, d_attn, hidden, d_gate, d_up, own, oth)


def input_weight_kernel(sched, own_ref, oth_ref, dq_ref, dk_ref, dv_ref, out_ref, *, local):
    me = sched[0]
    here = pl.ds(pl.multiple_of(me * local, local), local)
    there = pl.ds(pl.multiple_of((1 - me) * local, local), local)
    cols = dq_ref.shape[1]
    for at, ref in enumerate((dq_ref, dk_ref, dv_ref)):
        part = tdot(own_ref[...], ref[here, :]) + tdot(oth_ref[...], ref[there, :])
        out_ref[:, at * cols:(at + 1) * cols] = part.astype(BF16)


def input_weight_grads(sched, own, oth, dq, dk, dv, block=256):
    local, width = own.shape
    slots, cols = dq.shape
    rows = pl.BlockSpec((local, block), lambda s, sched: (0, s))
    full = pl.BlockSpec((slots, cols), lambda s, sched: (0, 0))
    return pl.pallas_call(
        partial(input_weight_kernel, local=local),
        grid_spec=pltpu.PrefetchScalarGridSpec(
            num_scalar_prefetch=1,
            grid=(width // block,),
            in_specs=[rows, rows, full, full, full],
            out_specs=pl.BlockSpec((block, 3 * cols), lambda s, sched: (s, 0)),
        ),
        out_shape=jax.ShapeDtypeStruct((width, 3 * cols), BF16),
        compiler_params=params(),
        cost_estimate=cost(6 * slots * width * cols, 6 * slots * cols),
        name="input_weight_grads",
    )(sched, own, oth, dq, dk, dv)


def input_grad_kernel(sched, dq_ref, dk_ref, dv_ref, wq_ref, wk_ref, wv_ref, dfirst_ref,
                      oth_ref, own_ref, *, half):
    step = pl.program_id(0)
    part = (rdot(dq_ref[...], wq_ref[...]) + rdot(dk_ref[...], wk_ref[...])
            + rdot(dv_ref[...], wv_ref[...]))

    @pl.when(step < half)
    def _():
        oth_ref[...] = part.astype(BF16)

    @pl.when(step >= half)
    def _():
        own_ref[...] = dfirst_ref[...] + part


def input_grads(sched, dq, dk, dv, wq, wk, wv, d_first, block):
    local, width = d_first.shape
    cols = dq.shape[1]
    half = local // block

    def place(n, sched):
        return lax.rem(n + (1 - sched[0]) * half, 2 * half)

    heads = pl.BlockSpec((block, cols), lambda n, s: (place(n, s), 0))
    weight = pl.BlockSpec((width, cols), lambda n, s: (0, 0))
    own = pl.BlockSpec((block, width), lambda n, s: (jnp.maximum(n - half, 0), 0))
    return pl.pallas_call(
        partial(input_grad_kernel, half=half),
        grid_spec=pltpu.PrefetchScalarGridSpec(
            num_scalar_prefetch=1,
            grid=(2 * half,),
            in_specs=[heads, heads, heads, weight, weight, weight, own],
            out_specs=[pl.BlockSpec((block, width), lambda n, s: (jnp.minimum(n, half - 1), 0)), own],
        ),
        out_shape=[jax.ShapeDtypeStruct((local, width), BF16),
                   jax.ShapeDtypeStruct((local, width), F32)],
        compiler_params=params(),
        cost_estimate=cost(12 * local * width * cols, 12 * local * width),
        name="input_grads",
    )(sched, dq, dk, dv, wq, wk, wv, d_first)


def exchange(value):
    return lax.ppermute(value, "tensor", [(0, 1), (1, 0)])


def flip(value, bit):
    count = lax.axis_size("dp")
    return lax.ppermute(value, "dp", [(at, at ^ (1 << bit)) for at in range(count)])


def bit_orders(count):
    bits = count.bit_length() - 1
    low = list(range(min(2, bits)))
    high = list(range(min(2, bits), bits))
    return high + low, high + low[::-1]


def gather_rows(piece, order):
    me = lax.axis_index("dp")
    rows, cols = piece.shape
    held = piece[None]
    for bit in order:
        other = flip(held, bit)
        mine = ((me >> bit) & 1) == 0
        held = jnp.stack([jnp.where(mine, held, other), jnp.where(mine, other, held)])
    bits = len(order)
    held = held.reshape((2,) * bits + (rows, cols))
    axes = [bits - 1 - order.index(bit) for bit in range(bits - 1, -1, -1)]
    return held.transpose(*axes, bits, bits + 1).reshape(-1, cols)


def scatter_rows(total, order):
    me = lax.axis_index("dp")
    bits = len(order)
    rows, cols = total.shape[0] >> bits, total.shape[1]
    held = total.reshape((2,) * bits + (rows, cols))
    left = list(range(bits - 1, -1, -1))
    for bit in order:
        axis = left.index(bit)
        left.pop(axis)
        low = lax.index_in_dim(held, 0, axis, keepdims=False)
        high = lax.index_in_dim(held, 1, axis, keepdims=False)
        mine = ((me >> bit) & 1) == 0
        got = flip(jnp.where(mine, high, low), bit)
        held = (jnp.where(mine, low, high).astype(F32) + got.astype(F32)).astype(BF16)
    return held.reshape(rows, cols)


def sum_everywhere(value):
    value = value + exchange(value)
    for bit in range(lax.axis_size("dp").bit_length() - 1):
        value = value + flip(value, bit)
    return value


def local(tokens, w_query, w_key, w_value, w_out, w_gate, w_up, w_down, gain_attn, gain_ffn,
          lengths, cotangent):
    rows, width = tokens.shape
    slots = 2 * rows
    me = lax.axis_index("tensor")
    count = lax.axis_size("dp")
    cols, hid = w_query.shape[1], w_gate.shape[1]
    share = width // count
    bq = bk = 512
    blocks = slots // bq

    packed = jnp.concatenate([w_gate, w_up, w_down.T, w_out.T], axis=1)
    feed_w = lax.all_gather(packed, ("tensor", "dp"), axis=0, tiled=True)
    feed_w = feed_w.reshape(2, width, packed.shape[1])
    fore, back = bit_orders(count)
    full_q = gather_rows(w_query, fore)
    full_k = gather_rows(w_key, back)
    full_v = gather_rows(w_value, fore)
    other_x = exchange(tokens)

    index = jnp.arange(slots, dtype=jnp.int32)
    row = lengths[0]
    ends = jnp.cumsum(row)
    begins = jnp.sum(jnp.where(index[:, None] >= ends[None, :], row[None, :], 0), axis=1)
    position = (index - begins).astype(F32)
    lane = jnp.arange(PAIR, dtype=jnp.int32) % HEAD
    inverse = ROPE_BASE ** (-((lane % (HEAD // 2)).astype(F32) * 2.0 / HEAD))
    angle = position[:, None] * inverse[None, :]
    cosine = jnp.cos(angle)
    sine = jnp.where(lane[None, :] < HEAD // 2, -jnp.sin(angle), jnp.sin(angle))
    block_begin = begins.reshape(blocks, bq)
    sched = jnp.concatenate([
        jnp.stack([me.astype(jnp.int32), ends[-1]]),
        block_begin[:, 0] // bk,
        (block_begin[:, -1] + bk - 1) // bk,
    ])
    start = begins.reshape(1, slots)

    q, k, v, vt = project(sched, tokens, other_x, full_q, full_k, full_v, cosine, sine, 512)
    mixed_send, mixed_own, lse = attend_forward(sched, q, k, vt, start, bq, bk)
    mixed_oth = exchange(mixed_send)
    (output, d_first, g_own, g_send, normed, d_ffn, d_attn, hidden, d_gate, d_up,
     gains) = feed(sched, tokens, mixed_own, mixed_oth, cotangent, feed_w,
                   gain_attn.reshape(1, width), gain_ffn.reshape(1, width), hid, 256)
    g_oth = exchange(g_send)
    grads = weight_grads(sched, normed, d_ffn, d_attn, hidden, d_gate, d_up,
                         mixed_own, mixed_oth, hid)
    reduced = lax.psum_scatter(grads.reshape(2 * width, grads.shape[2]), ("tensor", "dp"),
                               scatter_dimension=0, tiled=True).astype(F32)
    gains = sum_everywhere(gains)
    dq, dk, dv = attend_backward(sched, q, k, v, cosine, sine, start, lse,
                                 mixed_send, mixed_own, g_oth, g_own, bq, bk)
    qkv = input_weight_grads(sched, tokens, other_x, dq, dk, dv)
    fore, back = bit_orders(count)
    edge = 3 * cols // 2
    qkv = jnp.concatenate([scatter_rows(qkv[:, :edge], fore[::-1]),
                           scatter_rows(qkv[:, edge:], back[::-1])], axis=1).astype(F32)
    x_send, x_own = input_grads(sched, dq, dk, dv, full_q, full_k, full_v, d_first, 512)
    input_grad = (x_own + exchange(x_send).astype(F32)).astype(BF16)
    return (
        output,
        input_grad,
        qkv[:, :cols],
        qkv[:, cols:2 * cols],
        qkv[:, 2 * cols:],
        reduced[:, 3 * hid:].T,
        reduced[:, :hid],
        reduced[:, hid:2 * hid],
        reduced[:, 2 * hid:3 * hid].T,
        gains[0],
        gains[1],
    )


def solution(mesh):
    split = P("dp", "tensor")
    turned = P("tensor", "dp")
    slots = P(("dp", "tensor"), None)
    return jax.shard_map(
        local,
        mesh=mesh,
        in_specs=(slots, split, split, split, turned, split, split, turned, P(), P(),
                  P("dp", None), slots),
        out_specs=(slots, slots, split, split, split, turned, split, split, turned, P(), P()),
        check_vma=False,
    )
```

time: 2160 us -> 350 us (0.16)
  waiting for transfers between devices: 1050 us -> 79.3 us
  matrix products: 641 us -> 0 us
  blocking collectives: 211 us -> 0 us
  Pallas kernels: 0 us -> 183 us
  local copies, waits for them, and re-layouts: 124 us -> 14.2 us
  other arithmetic: 112 us -> 15.1 us
  starting transfers between devices: 1.86 us -> 47.1 us
    dot_general x49 -> x0, matrix products: 641 us -> none  [the longest x4 151 us: backward_block(): jnp.einsum('hqk,qhd->khd', grad_scores, queries, preferred_element_type=j...]
    reduce_scatter x8 -> x1, waiting for transfers between devices: 481 us -> 10.4 us  [local(): lax.psum_scatter(grads.reshape(2 * width, grads.shape[2]), ('tensor', 'dp...]
    unnamed x21 -> x2, waiting for transfers between devices: 386 us -> 0.03 us
    all_gather x7 -> x1, waiting for transfers between devices: 184 us -> 0.01 us  [local(): feed_w = lax.all_gather(packed, ('tensor', 'dp'), axis=0, tiled=True)]
    pallas_call x0 -> x7, Pallas kernels: none -> 183 us  [the longest x1 54.8 us: attend_backward(): pl.pallas_call(partial(backward_kernel, bq=bq, bk=bk, blocks=blocks), gri...]
    all_gather x4 -> x0, blocking collectives: 170 us -> none  [the longest x1 45.8 us: local(): lax.all_gather(w_query, 'dp', axis=0, tiled=True)]
    ppermute x0 -> x29, waiting for transfers between devices: none -> 68.8 us  [the longest x24 65.7 us: flip(): lax.ppermute(value, 'dp', [(at, at ^ 1 << bit) for at in range(count)])]
    dynamic_update_slice x8 -> x0, local copies, waits for them, and re-layouts: 67.4 us -> none  [local(): lax.map(runner, (query_blocks, seg_blocks, valid_blocks, index_blocks))]
  transfers between devices with their start and end apart: 18 -> 31, of which waited for: 16 -> 19; matrix products, arithmetic and copies ran while one was open for 4% -> 6% of each run, Pallas kernels for 0% -> 35%
where the time goes in v1:
time: 350 us; the launch traced here: 353 us
  Pallas kernels  183 us (52%)
  waiting for transfers between devices  79.3 us (23%)
  starting transfers between devices  47.1 us (13%)
  other arithmetic  15.1 us (4%)
  between operations  14.5 us (4%)
  local copies, waits for them, and re-layouts  14.2 us (4%)
    ppermute x24, waiting for transfers between devices, flip(): lax.ppermute(value, 'dp', [(at, at ^ 1 << bit) for at in range(count)])  65.7 us
    pallas_call x1, Pallas kernels, attend_backward(): pl.pallas_call(partial(backward_kernel, bq=bq, bk=bk, blocks=blocks), gri...  54.8 us
    ppermute x24, starting transfers between devices, flip(): lax.ppermute(value, 'dp', [(at, at ^ 1 << bit) for at in range(count)])  46.5 us
    pallas_call x1, Pallas kernels, feed(): pl.pallas_call(partial(feed_kernel, block=block, local=local, hid=hid, he...  41.2 us
    pallas_call x1, Pallas kernels, attend_forward(): pl.pallas_call(partial(forward_kernel, bq=bq, bk=bk, blocks=blocks), grid...  36.4 us
    pallas_call x1, Pallas kernels, weight_grads(): pl.pallas_call(partial(weight_grad_kernel, hid=hid), grid_spec=pltpu.Pref...  20 us
    pallas_call x1, Pallas kernels, input_grads(): pl.pallas_call(partial(input_grad_kernel, half=half), grid_spec=pltpu.Pre...  10.9 us
    reduce_scatter x1, waiting for transfers between devices, local(): lax.psum_scatter(grads.reshape(2 * width, grads.shape[2]), ('tensor', 'dp...  10.4 us
  transfers between devices with their start and end apart: 31, of which 19 were waited for; matrix products, arithmetic and copies ran while one was open for 6% of the time, Pallas kernels for 35%

profile of v1, /device:TPU:0, one launch (start us, length us, event | category | flops | bytes accessed | tf_op | source)
XLA Modules:
  0.0 353.3 jit_solution(6653364165472712186)
XLA Ops:
  9.1 3.1 collective-permute-start.9
  16.6 5.6 %negate_select_fusion = (f32[2048,128]{1,0:T(8,128)}, f32[2048,128]{1,0:T(8,128)}) fusion(f32[128]{0:T(128)S(1)} %fusion.22, f32[2048]{0:T(1024)S(1)} %subtract_convert_fusion, pred[128]{0:T(512)(128)(4,1)S(1)} %broadcast_compare_fusion), kind=kLoop, calls=%fused_computation.1 | loop fusion | flops 786432 | bytes 2105984 | tf_op jit(solution)/shard_map/jit(_where)/select_n | solution.py:612
  23.5 2.7 collective-permute-start.10
  26.6 2.7 collective-permute-start.2
  29.3 8.6 %collective-permute-done.10 = bf16[2,1,48,384]{3,2,0,1:T(8,128)(2,1)S(1)} collective-permute-done((bf16[2,1,48,384]{3,2,0,1:T(8,128)(2,1)S(1)}, bf16[2,1,48,384]{3,2,0,1:T(8,128)(2,1)S(1)}, u32[]{:S(2)}, u32[]{:S(2)}) %collective-permute-start.10) | collective-permute-done | bytes 73760 | tf_op jit(solution)/shard_map/ppermute | solution.py:535
  46.7 4.5 %collective-permute-done.7 = bf16[2,2,1,48,384]{4,3,1,0,2:T(8,128)(2,1)S(1)} collective-permute-done((bf16[2,2,1,48,384]{4,3,1,0,2:T(8,128)(2,1)S(1)}, bf16[2,2,1,48,384]{4,3,1,0,2:T(8,128)(2,1)S(1)}, u32[]{:S(2)}, u32[]{:S(2)}) %collective-permute-start.7) | collective-permute-done | bytes 147488 | tf_op jit(solution)/shard_map/ppermute | solution.py:535
  55.2 5.1 %collective-permute-done.12 = bf16[2,2,2,1,48,384]{5,4,2,1,0,3:T(8,128)(2,1)S(1)} collective-permute-done((bf16[2,2,2,1,48,384]{5,4,2,1,0,3:T(8,128)(2,1)S(1)}, bf16[2,2,2,1,48,384]{5,4,2,1,0,3:T(8,128)(2,1)S(1)}, u32[]{:S(2)}, u32[]{:S(2)}) %collective-permute-start.12) | collective-permute-done | bytes 294944 | tf_op jit(solution)/shard_map/ppermute | solution.py:535
  61.4 4.4 %collective-permute-done.8 = bf16[2,2,2,1,48,384]{5,4,2,1,0,3:T(8,128)(2,1)S(1)} collective-permute-done((bf16[2,2,2,1,48,384]{5,4,2,1,0,3:T(8,128)(2,1)S(1)}, bf16[2,2,2,1,48,384]{5,4,2,1,0,3:T(8,128)(2,1)S(1)}, u32[]{:S(2)}, u32[]{:S(2)}) %collective-permute-start.8) | collective-permute-done | bytes 294944 | tf_op jit(solution)/shard_map/ppermute | solution.py:535
  69.1 10.0 %project.1 = (bf16[2048,384]{1,0:T(8,128)(2,1)}, bf16[2048,384]{1,0:T(8,128)(2,1)}, bf16[2048,384]{1,0:T(8,128)(2,1)}, bf16[384,2048]{1,0:T(8,128)(2,1)}) custom-call(s32[10]{0:T(128)} %pad_add_fusion.sched, bf16[1024,768]{1,0:T(8,128)(2,1)} %own_ref.3, bf16[1024,768]{1,0:T(8,128)(2,1)} %copy-done.9, bf16[768,384]{1,0:T(8,128)(2,1)} %bitcast.195, ...), custom_call_target="tpu_custom_call" | custom-call | flops 3623878656 | bytes 11010048 | tf_op jit(solution)/shard_map/project/pallas_call | solution.py:80
  79.1 36.4 %attend_forward.1 = (bf16[1024,384]{1,0:T(8,128)(2,1)}, bf16[1024,384]{1,0:T(8,128)(2,1)}, f32[3,2,2048]{2,1,0:T(2,128)}) custom-call(s32[10]{0:T(128)} %pad_add_fusion.sched, bf16[2048,384]{1,0:T(8,128)(2,1)} %get-tuple-element.34.q_ref, bf16[2048,384]{1,0:T(8,128)(2,1)} %get-tuple-element.35.k_ref, bf16[384,2048]{1,0:T(8,128)(2,1)} %get-tuple-element.36.vt_ref, ...), custom_call_target="tpu_custom_call" | custom-call | flops 6442450944 | bytes 6291456 | tf_op jit(solution)/shard_map/attend_forward/pallas_call | solution.py:176
  118.8 41.2 %feed.1 = (bf16[1024,768]{1,0:T(8,128)(2,1)}, f32[1024,768]{1,0:T(8,128)}, bf16[1024,384]{1,0:T(8,128)(2,1)}, bf16[1024,384]{1,0:T(8,128)(2,1)}, bf16[1024,768]{...) custom-call(s32[10]{0:T(128)} %pad_add_fusion.sched, ...), custom_call_target="tpu_custom_call" | custom-call | flops 21743271936 | bytes 23592960 | tf_op jit(solution)/shard_map/feed/pallas_call | solution.py:402
  160.0 20.0 %weight_grads.1 = bf16[2,768,3456]{2,1,0:T(8,128)(2,1)} custom-call(s32[10]{0:T(128)} %pad_add_fusion.sched, bf16[1024,768]{1,0:T(8,128)(2,1)} %get-tuple-element.50.normed_ref, bf16[1024,768]{1,0:T(8,128)(2,1)} %get-tuple-element.51.dffn_ref, bf16[1024,768]{1,0:T(8,128)(2,1)} %get-tuple-element.52.dattn_ref, ...), custom_call_target="tpu_custom_call" | custom-call | flops 10871635968 | bytes 28311552 | tf_op jit(solution)/shard_map/weight_grads/pallas_call | solution.py:442
  187.5 3.7 %collective-permute-done.26 = f32[8,768]{1,0:T(8,128)S(1)} collective-permute-done((f32[8,768]{1,0:T(8,128)S(1)}, f32[8,768]{1,0:T(8,128)S(1)}, u32[]{:S(2)}, u32[]{:S(2)}) %collective-permute-start.26) | collective-permute-done | bytes 24608 | tf_op jit(solution)/shard_map/ppermute | solution.py:535
  191.2 3.8 %collective-permute-done.27 = f32[8,768]{1,0:T(8,128)S(1)} collective-permute-done((f32[8,768]{1,0:T(8,128)S(1)}, f32[8,768]{1,0:T(8,128)S(1)}, u32[]{:S(2)}, u32[]{:S(2)}) %collective-permute-start.27) | collective-permute-done | bytes 24608 | tf_op jit(solution)/shard_map/ppermute | solution.py:535
  195.0 6.3 %collective-permute-start.28 = (f32[8,768]{1,0:T(8,128)S(1)}, f32[8,768]{1,0:T(8,128)S(1)}, u32[]{:S(2)}, u32[]{:S(2)}) collective-permute-start(f32[8,768]{1,0:T(8,128)S(1)} %add.88), channel_id=1, source_target_pairs={{0,16},{2,18},{4,20},{6,22},{8,24},{10,26},{12,28},{14,30},{16,0},... | collective-permute-start | bytes 73736 | tf_op jit(solution)/shard_map/ppermute | solution.py:535
  204.6 54.8 %attend_backward.1 = (bf16[2048,384]{1,0:T(8,128)(2,1)}, bf16[2048,384]{1,0:T(8,128)(2,1)}, bf16[2048,384]{1,0:T(8,128)(2,1)}) custom-call(s32[10]{0:T(128)} %pad_add_fusion.sched, bf16[2048,384]{1,0:T(8,128)(2,1)} %get-tuple-element.34.q_ref, bf16[2048,384]{1,0:T(8,128)(2,1)} %get-tuple-element.35.k_ref, bf16[2048,384]{1,0:T(8,128)(2,1)} %get-tuple-element.40.v_ref, ...), custom_call_target="tpu_custom_call" | custom-call | flops 16106127360 | bytes 15728640 | tf_op jit(solution)/shard_map/attend_backward/pallas_call | solution.py:295
  259.4 9.8 %input_weight_grads.1 = bf16[768,1152]{1,0:T(8,128)(2,1)} custom-call(s32[10]{0:T(128)} %pad_add_fusion.sched, bf16[1024,768]{1,0:T(8,128)(2,1)} %own_ref.3, bf16[1024,768]{1,0:T(8,128)(2,1)} %copy-done.9, bf16[2048,384]{1,0:T(8,128)(2,1)} %get-tuple-element.44.dq_ref, bf16[2048,384]{1,0:T(8,128)(2,1)} %get-tuple-element.45.dk_ref, ...), custom_call_target="tpu_custom_call" | custom-call | flops 3623878656 | bytes 4718592 | tf_op jit(solution)/shard_map/input_weight_grads/pallas_call | solution.py:472
  274.7 10.9 %input_grads.1 = (bf16[1024,768]{1,0:T(8,128)(2,1)}, f32[1024,768]{1,0:T(8,128)}) custom-call(s32[10]{0:T(128)} %pad_add_fusion.sched, bf16[2048,384]{1,0:T(8,128)(2,1)} %get-tuple-element.44.dq_ref, bf16[2048,384]{1,0:T(8,128)(2,1)} %get-tuple-element.45.dk_ref, bf16[2048,384]{1,0:T(8,128)(2,1)} %get-tuple-element.46.dv_ref, bf16[768,384]{1,0:T(8,128)(2,1)} %bitcast.196, ...), custom_call_target="tpu_custom_call" | custom-call | flops 3623878656 | bytes 9437184 | tf_op jit(solution)/shard_map/input_grads/pallas_call | solution.py:513
  287.4 8.2 %collective-permute-done.21 = bf16[2,2,48,576]{3,2,1,0:T(8,128)(2,1)S(1)} collective-permute-done((bf16[2,2,48,576]{3,2,1,0:T(8,128)(2,1)S(1)}, bf16[2,2,48,576]{3,2,1,0:T(8,128)(2,1)S(1)}, u32[]{:S(2)}, u32[]{:S(2)}) %collective-permute-start.21) | collective-permute-done | bytes 221216 | tf_op jit(solution)/shard_map/ppermute | solution.py:535
  295.7 14.8 %collective-permute-start.22 = (bf16[2,48,576]{2,1,0:T(8,128)(2,1)S(1)}, bf16[2,48,576]{2,1,0:T(8,128)(2,1)S(1)}, u32[]{:S(2)}, u32[]{:S(2)}) collective-permute-start(bf16[2,48,576]{2,1,0:T(8,128)(2,1)S(1)} %select_bitcast_fusion.12), channel_id=1, source_target_pairs={{0,16},{2,18},{4,20},{6,22},{8,24},{10,26},{12,28},{14,30},{16,0},... | collective-permute-start | bytes 331784 | tf_op jit(solution)/shard_map/ppermute | solution.py:535
  310.8 12.7 %collective-permute-done.22 = bf16[2,48,576]{2,1,0:T(8,128)(2,1)S(1)} collective-permute-done((bf16[2,48,576]{2,1,0:T(8,128)(2,1)S(1)}, bf16[2,48,576]{2,1,0:T(8,128)(2,1)S(1)}, u32[]{:S(2)}, u32[]{:S(2)}) %collective-permute-start.22) | collective-permute-done | bytes 110624 | tf_op jit(solution)/shard_map/ppermute | solution.py:535
  323.6 2.6 collective-permute-done.18
  327.8 2.7 collective-permute-done.19
  332.8 10.4 %reduce-scatter.2.cloned.1.call-done = bf16[48,3456]{1,0:T(8,128)(2,1)} async-done(((bf16[1536,3456]{1,0:T(8,128)(2,1)}), bf16[48,3456]{1,0:T(8,128)(2,1)}) %reduce-scatter.2.cloned.1.call-update) | async-done | bytes 331792 | tf_op jit(solution)/shard_map/reduce_scatter | solution.py:630
  (150 shorter events, 54.0 us)
Async XLA Ops:
  7.2 110.8 %all-gather.2.cloned.1.call-start = ((), (), s32[]{:S(2)}) async-start(), calls=%async_computation.1 | async-start | bytes 10948608 | tf_op jit(solution)/shard_map/all_gather | solution.py:595
  9.0 334.2 %reduce-scatter.2.cloned.1.call-start = ((), (), s32[]{:S(2)}) async-start(), calls=%async_computation.2 | async-start | bytes 10948608 | tf_op jit(solution)/shard_map/reduce_scatter | solution.py:630
  9.1 14.4 %collective-permute-start.9 = (bf16[1,48,384]{2,1,0:T(8,128)(2,1)}, bf16[1,48,384]{2,1,0:T(8,128)(2,1)S(1)}, u32[]{:S(2)}, u32[]{:S(2)}) collective-permute-start(bf16[1,48,384]{2,1,0:T(8,128)(2,1)} %bitcast.200), channel_id=1, source_target_pairs={{0,8},{2,10},{4,12},{6,14},{8,0},{10,2},{12,4},{14,6},{16,24},{18,... | collective-permute-start | bytes 110600 | tf_op jit(solution)/shard_map/ppermute | solution.py:535
  12.2 14.0 %collective-permute-start.5 = (bf16[1,48,384]{2,1,0:T(8,128)(2,1)}, bf16[1,48,384]{2,1,0:T(8,128)(2,1)S(1)}, u32[]{:S(2)}, u32[]{:S(2)}) collective-permute-start(bf16[1,48,384]{2,1,0:T(8,128)(2,1)} %bitcast.201), channel_id=1, source_target_pairs={{0,8},{2,10},{4,12},{6,14},{8,0},{10,2},{12,4},{14,6},{16,24},{18,... | collective-permute-start | bytes 110600 | tf_op jit(solution)/shard_map/ppermute | solution.py:535
  12.2 14.4 %collective-permute-start.1 = (bf16[1,48,384]{2,1,0:T(8,128)(2,1)}, bf16[1,48,384]{2,1,0:T(8,128)(2,1)S(1)}, u32[]{:S(2)}, u32[]{:S(2)}) collective-permute-start(bf16[1,48,384]{2,1,0:T(8,128)(2,1)} %bitcast.202), channel_id=1, source_target_pairs={{0,8},{2,10},{4,12},{6,14},{8,0},{10,2},{12,4},{14,6},{16,24},{18,... | collective-permute-start | bytes 110600 | tf_op jit(solution)/shard_map/ppermute | solution.py:535
  14.2 53.7 %collective-permute-start = (bf16[1024,768]{1,0:T(8,128)(2,1)}, bf16[1024,768]{1,0:T(8,128)(2,1)S(1)}, u32[]{:S(2)}, u32[]{:S(2)}) collective-permute-start(bf16[1024,768]{1,0:T(8,128)(2,1)} %own_ref.3), channel_id=1, source_target_pairs={{0,1},{1,0},{2,3},{3,2},{4,5},{5,4},{6,7},{7,6},{8,9},{9,8},{10,11... | collective-permute-start | bytes 4718600 | tf_op jit(solution)/shard_map/ppermute | solution.py:530
  23.5 14.4 %collective-permute-start.10 = (bf16[2,1,48,384]{3,2,0,1:T(8,128)(2,1)S(1)}, bf16[2,1,48,384]{3,2,0,1:T(8,128)(2,1)S(1)}, u32[]{:S(2)}, u32[]{:S(2)}) collective-permute-start(bf16[2,1,48,384]{3,2,0,1:T(8,128)(2,1)S(1)} %fusion.17), channel_id=1, source_target_pairs={{0,16},{2,18},{4,20},{6,22},{8,24},{10,26},{12,28},{14,30},{16,0},... | collective-permute-start | bytes 221192 | tf_op jit(solution)/shard_map/ppermute | solution.py:535
  26.2 14.6 %collective-permute-start.6 = (bf16[2,1,48,384]{3,2,0,1:T(8,128)(2,1)S(1)}, bf16[2,1,48,384]{3,2,0,1:T(8,128)(2,1)S(1)}, u32[]{:S(2)}, u32[]{:S(2)}) collective-permute-start(bf16[2,1,48,384]{3,2,0,1:T(8,128)(2,1)S(1)} %pad_maximum_fusion.8), channel_id=1, source_target_pairs={{0,16},{2,18},{4,20},{6,22},{8,24},{10,26},{12,28},{14,30},{16,0},... | collective-permute-start | bytes 221192 | tf_op jit(solution)/shard_map/ppermute | solution.py:535
  26.6 16.1 %collective-permute-start.2 = (bf16[2,1,48,384]{3,2,0,1:T(8,128)(2,1)S(1)}, bf16[2,1,48,384]{3,2,0,1:T(8,128)(2,1)S(1)}, u32[]{:S(2)}, u32[]{:S(2)}) collective-permute-start(bf16[2,1,48,384]{3,2,0,1:T(8,128)(2,1)S(1)} %pad_maximum_fusion.7), channel_id=1, source_target_pairs={{0,16},{2,18},{4,20},{6,22},{8,24},{10,26},{12,28},{14,30},{16,0},... | collective-permute-start | bytes 221192 | tf_op jit(solution)/shard_map/ppermute | solution.py:535
  38.0 7.9 %collective-permute-start.11 = (bf16[2,2,1,48,384]{4,3,1,0,2:T(8,128)(2,1)S(1)}, bf16[2,2,1,48,384]{4,3,1,0,2:T(8,128)(2,1)S(1)}, u32[]{:S(2)}, u32[]{:S(2)}) collective-permute-start(bf16[2,2,1,48,384]{4,3,1,0,2:T(8,128)(2,1)S(1)} %fusion.14), channel_id=1, source_target_pairs={{0,2},{2,0},{4,6},{6,4},{8,10},{10,8},{12,14},{14,12},{16,18},{18,... | collective-permute-start | bytes 442376 | tf_op jit(solution)/shard_map/ppermute | solution.py:535
  42.9 8.3 %collective-permute-start.7 = (bf16[2,2,1,48,384]{4,3,1,0,2:T(8,128)(2,1)S(1)}, bf16[2,2,1,48,384]{4,3,1,0,2:T(8,128)(2,1)S(1)}, u32[]{:S(2)}, u32[]{:S(2)}) collective-permute-start(bf16[2,2,1,48,384]{4,3,1,0,2:T(8,128)(2,1)S(1)} %fusion.15), channel_id=1, source_target_pairs={{0,4},{2,6},{4,0},{6,2},{8,12},{10,14},{12,8},{14,10},{16,20},{18,... | collective-permute-start | bytes 442376 | tf_op jit(solution)/shard_map/ppermute | solution.py:535
  44.4 9.2 %collective-permute-start.3 = (bf16[2,2,1,48,384]{4,3,1,0,2:T(8,128)(2,1)S(1)}, bf16[2,2,1,48,384]{4,3,1,0,2:T(8,128)(2,1)S(1)}, u32[]{:S(2)}, u32[]{:S(2)}) collective-permute-start(bf16[2,2,1,48,384]{4,3,1,0,2:T(8,128)(2,1)S(1)} %pad_maximum_fusion.4), channel_id=1, source_target_pairs={{0,2},{2,0},{4,6},{6,4},{8,10},{10,8},{12,14},{14,12},{16,18},{18,... | collective-permute-start | bytes 442376 | tf_op jit(solution)/shard_map/ppermute | solution.py:535
  46.1 14.2 %collective-permute-start.12 = (bf16[2,2,2,1,48,384]{5,4,2,1,0,3:T(8,128)(2,1)S(1)}, bf16[2,2,2,1,48,384]{5,4,2,1,0,3:T(8,128)(2,1)S(1)}, u32[]{:S(2)}, u32[]{:S(2)}) collective-permute-start(bf16[2,2,2,1,48,384]{5,4,2,1,0,3:T(8,128)(2,1)S(1)} %fusion.8), channel_id=1, source_target_pairs={{0,4},{2,6},{4,0},{6,2},{8,12},{10,14},{12,8},{14,10},{16,20},{18,... | collective-permute-start | bytes 884744 | tf_op jit(solution)/shard_map/ppermute | solution.py:535
  51.2 14.5 %collective-permute-start.8 = (bf16[2,2,2,1,48,384]{5,4,2,1,0,3:T(8,128)(2,1)S(1)}, bf16[2,2,2,1,48,384]{5,4,2,1,0,3:T(8,128)(2,1)S(1)}, u32[]{:S(2)}, u32[]{:S(2)}) collective-permute-start(bf16[2,2,2,1,48,384]{5,4,2,1,0,3:T(8,128)(2,1)S(1)} %fusion.9), channel_id=1, source_target_pairs={{0,2},{2,0},{4,6},{6,4},{8,10},{10,8},{12,14},{14,12},{16,18},{18,... | collective-permute-start | bytes 884744 | tf_op jit(solution)/shard_map/ppermute | solution.py:535
  53.7 13.2 %collective-permute-start.4 = (bf16[2,2,2,1,48,384]{5,4,2,1,0,3:T(8,128)(2,1)S(1)}, bf16[2,2,2,1,48,384]{5,4,2,1,0,3:T(8,128)(2,1)S(1)}, u32[]{:S(2)}, u32[]{:S(2)}) collective-permute-start(bf16[2,2,2,1,48,384]{5,4,2,1,0,3:T(8,128)(2,1)S(1)} %pad_maximum_fusion.1), channel_id=1, source_target_pairs={{0,4},{2,6},{4,0},{6,2},{8,12},{10,14},{12,8},{14,10},{16,20},{18,... | collective-permute-start | bytes 884744 | tf_op jit(solution)/shard_map/ppermute | solution.py:535
  181.2 22.5 %collective-permute-start.14 = (bf16[1024,384]{1,0:T(8,128)(2,1)S(1)}, bf16[1024,384]{1,0:T(8,128)(2,1)S(1)}, u32[]{:S(2)}, u32[]{:S(2)}) collective-permute-start(bf16[1024,384]{1,0:T(8,128)(2,1)S(1)} %copy-done.10), channel_id=1, source_target_pairs={{0,1},{1,0},{2,3},{3,2},{4,5},{5,4},{6,7},{7,6},{8,9},{9,8},{10,11... | collective-permute-start | bytes 2359304 | tf_op jit(solution)/shard_map/ppermute | solution.py:530
  195.0 8.1 %collective-permute-start.28 = (f32[8,768]{1,0:T(8,128)S(1)}, f32[8,768]{1,0:T(8,128)S(1)}, u32[]{:S(2)}, u32[]{:S(2)}) collective-permute-start(f32[8,768]{1,0:T(8,128)S(1)} %add.88), channel_id=1, source_target_pairs={{0,16},{2,18},{4,20},{6,22},{8,24},{10,26},{12,28},{14,30},{16,0},... | collective-permute-start | bytes 73736 | tf_op jit(solution)/shard_map/ppermute | solution.py:535
  271.5 14.1 %collective-permute-start.20 = (bf16[2,2,2,48,576]{4,3,1,0,2:T(8,128)(2,1)S(1)}, bf16[2,2,2,48,576]{4,3,1,0,2:T(8,128)(2,1)S(1)}, u32[]{:S(2)}, u32[]{:S(2)}) collective-permute-start(bf16[2,2,2,48,576]{4,3,1,0,2:T(8,128)(2,1)S(1)} %select_bitcast_fusion), channel_id=1, source_target_pairs={{0,2},{2,0},{4,6},{6,4},{8,10},{10,8},{12,14},{14,12},{16,18},{18,... | collective-permute-start | bytes 1327112 | tf_op jit(solution)/shard_map/ppermute | solution.py:535
  273.8 13.3 %collective-permute-start.16 = (bf16[2,2,2,48,576]{4,3,1,0,2:T(8,128)(2,1)S(1)}, bf16[2,2,2,48,576]{4,3,1,0,2:T(8,128)(2,1)S(1)}, u32[]{:S(2)}, u32[]{:S(2)}) collective-permute-start(bf16[2,2,2,48,576]{4,3,1,0,2:T(8,128)(2,1)S(1)} %select_bitcast_fusion.1), channel_id=1, source_target_pairs={{0,4},{2,6},{4,0},{6,2},{8,12},{10,14},{12,8},{14,10},{16,20},{18,... | collective-permute-start | bytes 1327112 | tf_op jit(solution)/shard_map/ppermute | solution.py:535
  285.6 45.7 %collective-permute-start.15 = (bf16[1024,768]{1,0:T(8,128)(2,1)}, bf16[1024,768]{1,0:T(8,128)(2,1)S(1)}, u32[]{:S(2)}, u32[]{:S(2)}) collective-permute-start(bf16[1024,768]{1,0:T(8,128)(2,1)} %get-tuple-element.49), channel_id=1, source_target_pairs={{0,1},{1,0},{2,3},{3,2},{4,5},{5,4},{6,7},{7,6},{8,9},{9,8},{10,11... | collective-permute-start | bytes 4718600 | tf_op jit(solution)/shard_map/ppermute | solution.py:530
  285.8 9.8 %collective-permute-start.21 = (bf16[2,2,48,576]{3,2,1,0:T(8,128)(2,1)S(1)}, bf16[2,2,48,576]{3,2,1,0:T(8,128)(2,1)S(1)}, u32[]{:S(2)}, u32[]{:S(2)}) collective-permute-start(bf16[2,2,48,576]{3,2,1,0:T(8,128)(2,1)S(1)} %select_bitcast_fusion.6), channel_id=1, source_target_pairs={{0,4},{2,6},{4,0},{6,2},{8,12},{10,14},{12,8},{14,10},{16,20},{18,... | collective-permute-start | bytes 663560 | tf_op jit(solution)/shard_map/ppermute | solution.py:535
  287.3 23.2 %collective-permute-start.17 = (bf16[2,2,48,576]{3,2,1,0:T(8,128)(2,1)S(1)}, bf16[2,2,48,576]{3,2,1,0:T(8,128)(2,1)S(1)}, u32[]{:S(2)}, u32[]{:S(2)}) collective-permute-start(bf16[2,2,48,576]{3,2,1,0:T(8,128)(2,1)S(1)} %select_bitcast_fusion.7), channel_id=1, source_target_pairs={{0,2},{2,0},{4,6},{6,4},{8,10},{10,8},{12,14},{14,12},{16,18},{18,... | collective-permute-start | bytes 663560 | tf_op jit(solution)/shard_map/ppermute | solution.py:535
  295.7 27.7 %collective-permute-start.22 = (bf16[2,48,576]{2,1,0:T(8,128)(2,1)S(1)}, bf16[2,48,576]{2,1,0:T(8,128)(2,1)S(1)}, u32[]{:S(2)}, u32[]{:S(2)}) collective-permute-start(bf16[2,48,576]{2,1,0:T(8,128)(2,1)S(1)} %select_bitcast_fusion.12), channel_id=1, source_target_pairs={{0,16},{2,18},{4,20},{6,22},{8,24},{10,26},{12,28},{14,30},{16,0},... | collective-permute-start | bytes 331784 | tf_op jit(solution)/shard_map/ppermute | solution.py:535
  310.7 15.5 %collective-permute-start.18 = (bf16[2,48,576]{2,1,0:T(8,128)(2,1)S(1)}, bf16[2,48,576]{2,1,0:T(8,128)(2,1)S(1)}, u32[]{:S(2)}, u32[]{:S(2)}) collective-permute-start(bf16[2,48,576]{2,1,0:T(8,128)(2,1)S(1)} %select_bitcast_fusion.13), channel_id=1, source_target_pairs={{0,16},{2,18},{4,20},{6,22},{8,24},{10,26},{12,28},{14,30},{16,0},... | collective-permute-start | bytes 331784 | tf_op jit(solution)/shard_map/ppermute | solution.py:535
  (20 other events, 199.3 us)
Sparse Core Ops, SparseCore 0:
  10.9 101.9 all-gather.1
  180.2 162.9 reduce-scatter.1

commit v2 on v1

v2 whole, which is shorter than its diff:
```python
from functools import partial

import jax
import jax.numpy as jnp
from jax import lax
from jax.experimental import pallas as pl
from jax.experimental.pallas import tpu as pltpu
from jax.sharding import Mesh
from jax.sharding import PartitionSpec as P

HEAD = 64
PAIR = 2 * HEAD
EPS = 1e-05
ROPE_BASE = 10000.0
NEGATIVE = -1e30
F32 = jnp.float32
BF16 = jnp.bfloat16
VMEM_LIMIT = 56 * 1024 * 1024
DP = ("far", "near")


def mm(left, right):
    return jnp.dot(left, right, preferred_element_type=F32)


def rdot(left, right):
    return lax.dot_general(left, right, (((1,), (1,)), ((), ())), preferred_element_type=F32)


def tdot(left, right):
    return lax.dot_general(left, right, (((0,), (0,)), ((), ())), preferred_element_type=F32)


def params(limit=VMEM_LIMIT, dims=1):
    return pltpu.CompilerParams(
        vmem_limit_bytes=limit, dimension_semantics=("arbitrary",) * dims
    )


def cost(flops, nbytes, trans=0):
    return pl.CostEstimate(flops=int(flops), bytes_accessed=int(nbytes), transcendentals=int(trans))


def swap_halves(values):
    lane = lax.broadcasted_iota(jnp.int32, values.shape, 1) % HEAD
    half = HEAD // 2
    width = values.shape[1]
    return jnp.where(
        lane < half, pltpu.roll(values, width - half, 1), pltpu.roll(values, half, 1)
    )


def head_masks(values):
    lane = lax.broadcasted_iota(jnp.int32, (1, PAIR), 1)
    low = (lane < HEAD).astype(values.dtype)
    return (values * low, values * (1 - low))


def forward_kernel(sched, own_x_ref, oth_x_ref, wq_ref, wk_ref, wv_ref, cos_ref, sin_ref, start_ref,
                   qkv_ref, oth_ref, own_ref, lse_ref, acc_ref, vt_ref, *, bq, bk, sub, chunk, blocks):
    step = pl.program_id(1)
    half = blocks // 2
    i = lax.rem(step + (1 - sched[0]) * half, blocks)

    @pl.when(step == 0)
    def _():
        local = own_x_ref.shape[0]
        weights = jnp.concatenate([wq_ref[...], wk_ref[...], wv_ref[...]], axis=1)
        for x_ref, side in ((own_x_ref, sched[0]), (oth_x_ref, 1 - sched[0])):
            for r in range(0, local, chunk):
                at = pl.multiple_of(side * local + r, chunk)
                here = pl.ds(at, chunk)
                u = mm(x_ref[r:r + chunk, :], weights)
                cosine, sine = cos_ref[here, :], sin_ref[here, :]
                for n, scale in ((0, HEAD ** -0.5), (1, 1.0)):
                    piece = u[:, n * PAIR:(n + 1) * PAIR]
                    turned = piece * cosine + swap_halves(piece) * sine
                    qkv_ref[here, n * PAIR:(n + 1) * PAIR] = (turned * scale).astype(BF16)
                v = u[:, 2 * PAIR:]
                qkv_ref[here, 2 * PAIR:] = v.astype(BF16)
                vt_ref[:, here] = v.T.astype(BF16)

    queries = head_masks(qkv_ref[pl.ds(pl.multiple_of(i * bq, bq), bq), 0:PAIR])
    start = start_ref[...]
    acc_ref[...] = jnp.zeros_like(acc_ref)
    streams = [(h, c) for h in range(2) for c in range(0, bq, sub)]

    def visit(j, carry, masked, last):
        at = pl.multiple_of(i * bq if last else j * bk, bk)
        scores, out = [], []
        for h, c in streams:
            size = c + sub if last else bk
            s = rdot(qkv_ref[pl.ds(at, size), PAIR:2 * PAIR], queries[h][c:c + sub])
            if masked:
                key_index = at + lax.broadcasted_iota(jnp.int32, (size, sub), 0)
                query_index = i * bq + c + lax.broadcasted_iota(jnp.int32, (size, sub), 1)
                allowed = (key_index >= start[:, c:c + sub]) & (key_index <= query_index)
                s = jnp.where(allowed, s, NEGATIVE)
            scores.append(s)
        for n, (h, c) in enumerate(streams):
            size = c + sub if last else bk
            peak, total = carry[2 * n], carry[2 * n + 1]
            new_peak = jnp.maximum(peak, jnp.max(scores[n], axis=0, keepdims=True))
            fade = jnp.exp(peak - new_peak)
            expo = jnp.exp(scores[n] - new_peak)
            total = total * fade + jnp.sum(expo, axis=0, keepdims=True)
            rows, cols = pl.ds(h * HEAD, HEAD), slice(c, c + sub)
            acc_ref[rows, cols] = acc_ref[rows, cols] * fade + mm(
                vt_ref[rows, pl.ds(at, size)], expo.astype(BF16)
            )
            out += [new_peak, total]
        return tuple(out)

    low = sched[2 + i]
    top = i * (bq // bk)
    mid = jnp.minimum(sched[2 + blocks + i], top)
    carry = (jnp.full((1, sub), NEGATIVE, F32), jnp.zeros((1, sub), F32)) * len(streams)
    carry = lax.fori_loop(low, mid, lambda j, c: visit(j, c, True, False), carry)
    carry = lax.fori_loop(jnp.maximum(low, mid), top, lambda j, c: visit(j, c, False, False), carry)
    carry = visit(None, carry, True, True)
    for n, (h, c) in enumerate(streams):
        peak, total = carry[2 * n], carry[2 * n + 1]
        rows, cols = slice(h * HEAD, (h + 1) * HEAD), slice(c, c + sub)
        acc_ref[rows, cols] = acc_ref[rows, cols] / total
        lse_ref[h:h + 1, cols] = peak + jnp.log(total)
    mixed = acc_ref[...].T.astype(BF16)

    @pl.when(step < half)
    def _():
        oth_ref[...] = mixed

    @pl.when(step >= half)
    def _():
        own_ref[...] = mixed


def placing(blocks):
    half = blocks // 2

    def place(n, sched):
        return lax.rem(n + (1 - sched[0]) * half, blocks)

    return place, half


def attend_forward(sched, own_x, oth_x, weights, cosine, sine, start, bq, bk, sub=256, chunk=512):
    local, width = own_x.shape
    slots, cols = 2 * local, weights.shape[1] // 3
    pairs, blocks = cols // PAIR, slots // bq
    place, half = placing(blocks)
    rows = pl.BlockSpec((local, width), lambda p, n, s: (0, 0), pipeline_mode=pl.Buffered(1))
    table = pl.BlockSpec((slots, PAIR), lambda p, n, s: (0, 0), pipeline_mode=pl.Buffered(1))
    return pl.pallas_call(
        partial(forward_kernel, bq=bq, bk=bk, sub=sub, chunk=chunk, blocks=blocks),
        grid_spec=pltpu.PrefetchScalarGridSpec(
            num_scalar_prefetch=1,
            grid=(pairs, blocks),
            in_specs=[
                rows, rows,
                *[pl.BlockSpec((width, PAIR), lambda p, n, s, at=at: (0, at + p))
                  for at in (0, pairs, 2 * pairs)],
                table, table,
                pl.BlockSpec((1, bq), lambda p, n, s: (0, place(n, s))),
            ],
            out_specs=[
                pl.BlockSpec((slots, 3 * PAIR), lambda p, n, s: (0, p)),
                pl.BlockSpec((bq, PAIR), lambda p, n, s: (jnp.minimum(n, half - 1), p)),
                pl.BlockSpec((bq, PAIR), lambda p, n, s: (jnp.maximum(n - half, 0), p)),
                pl.BlockSpec((None, 2, bq), lambda p, n, s: (p, 0, place(n, s))),
            ],
            scratch_shapes=[pltpu.VMEM((PAIR, bq), F32), pltpu.VMEM((PAIR, slots), BF16)],
        ),
        out_shape=[
            jax.ShapeDtypeStruct((slots, 3 * cols), BF16),
            jax.ShapeDtypeStruct((local, cols), BF16),
            jax.ShapeDtypeStruct((local, cols), BF16),
            jax.ShapeDtypeStruct((pairs, 2, slots), F32),
        ],
        compiler_params=params(dims=2),
        cost_estimate=cost(4 * slots * slots * cols + 6 * slots * width * cols,
                           16 * slots * cols, slots * slots * 6),
        name="attend_forward",
    )(sched, own_x, oth_x, weights, weights, weights, cosine, sine, start)


def backward_kernel(sched, q_ref, k_ref, v_ref, cos_ref, sin_ref, start_ref, lse_ref,
                    o_oth_ref, o_own_ref, g_oth_ref, g_own_ref, x_own_ref, x_oth_ref,
                    all_ref, dw_ref, dq_acc, dkt_acc, dvt_acc, *, bq, bk, sub, blocks):
    step = pl.program_id(1)
    half = blocks // 2
    i = lax.rem(step + (1 - sched[0]) * half, blocks)

    @pl.when(step == 0)
    def _():
        dkt_acc[...] = jnp.zeros_like(dkt_acc)
        dvt_acc[...] = jnp.zeros_like(dvt_acc)

    first = step < half
    grads = jnp.where(first, g_oth_ref[...], g_own_ref[...])
    mixed = jnp.where(first, o_oth_ref[...], o_own_ref[...])
    queries = head_masks(q_ref[...])
    couts = head_masks(grads)
    query_t = q_ref[...].astype(F32).T.astype(BF16)
    cout_t = grads.astype(F32).T.astype(BF16)
    start = start_ref[...]
    product = grads.astype(F32) * mixed.astype(F32)
    big = product.astype(BF16)
    small = (product - big.astype(F32)).astype(BF16)
    row = lax.broadcasted_iota(jnp.int32, (PAIR, 2 * PAIR), 0)
    lane = lax.broadcasted_iota(jnp.int32, (PAIR, 2 * PAIR), 1)
    pick = jnp.where(row // HEAD == lane // PAIR, 1.0, 0.0).astype(BF16)
    inner = mm(big, pick) + mm(small, pick)
    lse = [jnp.broadcast_to(lse_ref[h:h + 1, :], (PAIR, bq)).T for h in range(2)]
    dq_acc[...] = jnp.zeros_like(dq_acc)

    def wide(value, size):
        return jnp.concatenate([value] * (size // PAIR), axis=1)

    def visit(j, masked, last):
        at = pl.multiple_of(i * bq if last else j * bk, bk)
        streams = [(c, h) for c in range(0, bq, sub) for h in range(2)]

        def scores(n):
            c, h = streams[n]
            size = c + sub if last else bk
            where = pl.ds(at, size)
            rows = slice(c, c + sub)
            return rdot(queries[h][rows], k_ref[where, :]), rdot(couts[h][rows], v_ref[where, :])

        def absorb(n, pair):
            c, h = streams[n]
            raw, d_probs = pair
            size = c + sub if last else bk
            where = pl.ds(at, size)
            rows = slice(c, c + sub)
            lanes = slice(h * HEAD, (h + 1) * HEAD)
            probs = jnp.exp(raw - wide(lse[h][rows], size))
            if masked:
                begin = jnp.broadcast_to(start[:, rows], (PAIR, sub)).T
                key_index = at + lax.broadcasted_iota(jnp.int32, (sub, size), 1)
                query_index = i * bq + c + lax.broadcasted_iota(jnp.int32, (sub, size), 0)
                allowed = (key_index >= wide(begin, size)) & (key_index <= query_index)
                probs = jnp.where(allowed, probs, 0.0)
            d_scores = (probs * (d_probs - wide(inner[rows, h * PAIR:(h + 1) * PAIR], size))).astype(BF16)
            dvt_acc[lanes, where] += mm(cout_t[lanes, rows], probs.astype(BF16))
            dkt_acc[lanes, where] += mm(query_t[lanes, rows], d_scores)
            dq_acc[rows, :] += mm(d_scores, head_masks(k_ref[where, :])[h])

        ready = scores(0)
        for n in range(len(streams)):
            held = ready
            if n + 1 < len(streams):
                ready = scores(n + 1)
            absorb(n, held)

    low = sched[2 + i]
    mid = jnp.minimum(sched[2 + blocks + i], i * (bq // bk))

    @pl.loop(low, mid)
    def _(j):
        visit(j, True, False)

    @pl.loop(jnp.maximum(low, mid), i * (bq // bk))
    def _(j):
        visit(j, False, False)

    visit(None, True, True)

    def unrotate(g, cosine, sine):
        return g * cosine - swap_halves(g) * sine

    here = pl.ds(pl.multiple_of(i * bq, bq), bq)
    dq = unrotate(dq_acc[...] * (HEAD ** -0.5), cos_ref[here, :], sin_ref[here, :])
    all_ref[here, 0:PAIR] = dq.astype(BF16)

    @pl.when(step == blocks - 1)
    def _():
        dk = unrotate(dkt_acc[...].T, cos_ref[...], sin_ref[...])
        all_ref[:, PAIR:2 * PAIR] = dk.astype(BF16)
        all_ref[:, 2 * PAIR:] = dvt_acc[...].T.astype(BF16)
        local = x_own_ref.shape[0]
        mine = pl.ds(pl.multiple_of(sched[0] * local, local), local)
        rest = pl.ds(pl.multiple_of((1 - sched[0]) * local, local), local)
        dw_ref[...] = (tdot(x_own_ref[...], all_ref[mine, :])
                       + tdot(x_oth_ref[...], all_ref[rest, :])).astype(BF16)


def attend_backward(sched, qkv, cosine, sine, start, lse, o_oth, o_own, g_oth, g_own, x_own, x_oth,
                    bq, bk, sub=256):
    slots, cols = qkv.shape[0], qkv.shape[1] // 3
    pairs, blocks = cols // PAIR, slots // bq
    local, width = x_own.shape
    place, half = placing(blocks)
    table = pl.BlockSpec((slots, PAIR), lambda p, n, s: (0, 0), pipeline_mode=pl.Buffered(1))
    rows = pl.BlockSpec((local, width), lambda p, n, s: (0, 0), pipeline_mode=pl.Buffered(1))
    oth = pl.BlockSpec((bq, PAIR), lambda p, n, s: (jnp.minimum(n, half - 1), p))
    own = pl.BlockSpec((bq, PAIR), lambda p, n, s: (jnp.maximum(n - half, 0), p))
    return pl.pallas_call(
        partial(backward_kernel, bq=bq, bk=bk, sub=sub, blocks=blocks),
        grid_spec=pltpu.PrefetchScalarGridSpec(
            num_scalar_prefetch=1,
            grid=(pairs, blocks),
            in_specs=[
                pl.BlockSpec((bq, PAIR), lambda p, n, s: (place(n, s), 3 * p)),
                pl.BlockSpec((slots, PAIR), lambda p, n, s: (0, 3 * p + 1)),
                pl.BlockSpec((slots, PAIR), lambda p, n, s: (0, 3 * p + 2)),
                table, table,
                pl.BlockSpec((1, bq), lambda p, n, s: (0, place(n, s))),
                pl.BlockSpec((None, 2, bq), lambda p, n, s: (p, 0, place(n, s))),
                oth, own, oth, own, rows, rows,
            ],
            out_specs=[pl.BlockSpec((slots, 3 * PAIR), lambda p, n, s: (0, p)),
                       pl.BlockSpec((width, 3 * PAIR), lambda p, n, s: (0, p))],
            scratch_shapes=[
                pltpu.VMEM((bq, PAIR), F32),
                pltpu.VMEM((PAIR, slots), F32),
                pltpu.VMEM((PAIR, slots), F32),
            ],
        ),
        out_shape=[jax.ShapeDtypeStruct((slots, 3 * cols), BF16),
                   jax.ShapeDtypeStruct((width, 3 * cols), BF16)],
        compiler_params=params(dims=2),
        cost_estimate=cost(10 * slots * slots * cols + 6 * slots * width * cols,
                           20 * slots * cols, slots * slots * 6),
        name="attend_backward",
    )(sched, qkv, qkv, qkv, cosine, sine, start, lse, o_oth, o_own, g_oth, g_own, x_own, x_oth)


def feed_kernel(sched, x_ref, own_ref, oth_ref, dy_ref, w_hbm, ga_ref, gf_ref,
                out_ref, dfirst_ref, gown_ref, goth_ref, grads_ref, gains_ref,
                w_ref, keep_a, keep_b, hidden_s, dgate_s, dup_s, normed_s, dffn_s, dattn_s, mixed_s,
                sems, *, block, sub, chunk, local, hid, head_cols, parts, share):
    step = pl.program_id(0)
    me = sched[0]
    steps = local // block
    outs = slice(3 * hid, 3 * hid + head_cols)
    pieces = [(slice(3 * hid, w_ref.shape[2]), None), (slice(0, 2 * hid), 0), (slice(0, 2 * hid), 1),
              (slice(2 * hid, 3 * hid), None)]

    def piece(n):
        cols, t = pieces[n]
        at = (slice(None), slice(None), cols) if t is None else (t, slice(None), cols)
        return pltpu.make_async_copy(w_hbm.at[at], w_ref.at[at], sems.at[n])

    @pl.when(step == 0)
    def _():
        for n in range(len(pieces)):
            piece(n).start()
        gains_ref[...] = jnp.zeros_like(gains_ref)

    def arrive(n):
        @pl.when(step == 0)
        def _():
            piece(n).wait()

    chunks = [(t, c) for t in range(2) for c in range(0, hid, chunk)]

    @pl.when(step < steps)
    def _():
        subs = list(range(0, block, sub))
        base = pl.multiple_of(step * block, block)
        arrive(0)
        first, rms1, unit1, normed, normed_b, ffn = {}, {}, {}, {}, {}, {}
        attn = {}
        for r in subs:
            rows = slice(r, r + sub)
            attn[r] = rdot(own_ref[rows, :], w_ref[me, :, outs]) + rdot(oth_ref[rows, :], w_ref[1 - me, :, outs])
        for r in subs:
            rows = slice(r, r + sub)
            here = pl.ds(base + r, sub)
            first = x_ref[rows, :].astype(F32) + attn[r]
            rms1[r] = lax.rsqrt(jnp.mean(first * first, axis=-1, keepdims=True) + EPS)
            unit1[r] = first * rms1[r]
            normed[r] = unit1[r] * ga_ref[...]
            normed_b[r] = normed[r].astype(BF16)
            normed_s[here, :] = normed_b[r]
            mixed_s[here, :] = jnp.concatenate([own_ref[rows, :], oth_ref[rows, :]], axis=1)
        for n, (t, c) in enumerate(chunks):
            if n == 0:
                arrive(1)
            if t == 1 and c == 0:
                arrive(2)
            at = t * hid + c
            cols = slice(at, at + chunk)
            hid_b = {}
            for r in subs:
                rows = slice(r, r + sub)
                here = pl.ds(base + r, sub)
                gate = mm(normed_b[r], w_ref[t, :, c:c + chunk])
                upper = mm(normed_b[r], w_ref[t, :, hid + c:hid + c + chunk])
                sigma = 1.0 / (1.0 + jnp.exp(-gate))
                silu = gate * sigma
                hid_b[r] = (silu * upper).astype(BF16)
                keep_a[rows, cols] = silu
                keep_b[rows, cols] = upper * (sigma + silu * (1.0 - sigma))
                hidden_s[here, cols] = hid_b[r]
            if n == 0:
                arrive(3)
            for r in subs:
                part = rdot(hid_b[r], w_ref[t, :, 2 * hid + c:2 * hid + c + chunk])
                ffn[r] = part if n == 0 else ffn[r] + part
        d_second, d_ffn, dn = {}, {}, {}
        for r in subs:
            rows = slice(r, r + sub)
            here = pl.ds(base + r, sub)
            second = normed[r] + ffn[r]
            rms2 = lax.rsqrt(jnp.mean(second * second, axis=-1, keepdims=True) + EPS)
            unit2 = second * rms2
            slot = me * local + base + r + lax.broadcasted_iota(jnp.int32, (sub, 1), 0)
            valid = slot < sched[1]
            out_ref[rows, :] = jnp.where(valid, unit2 * gf_ref[...], 0.0).astype(BF16)
            dy = jnp.where(valid, dy_ref[rows, :].astype(F32), 0.0)
            gains_ref[1:2, :] += jnp.sum(dy * unit2, axis=0, keepdims=True)
            scaled = dy * gf_ref[...]
            d_second[r] = rms2 * (scaled - unit2 * jnp.mean(scaled * unit2, axis=-1, keepdims=True))
            d_ffn[r] = d_second[r].astype(BF16)
            dffn_s[here, :] = d_ffn[r]
            dn[r] = d_second[r]
        for t, c in chunks:
            at = t * hid + c
            cols = slice(at, at + chunk)
            dg, du = {}, {}
            for r in subs:
                rows = slice(r, r + sub)
                here = pl.ds(base + r, sub)
                d_hidden = mm(d_ffn[r], w_ref[t, :, 2 * hid + c:2 * hid + c + chunk])
                dg[r] = (d_hidden * keep_b[rows, cols]).astype(BF16)
                du[r] = (d_hidden * keep_a[rows, cols]).astype(BF16)
                dgate_s[here, cols] = dg[r]
                dup_s[here, cols] = du[r]
            for r in subs:
                dn[r] = dn[r] + rdot(dg[r], w_ref[t, :, c:c + chunk]) + rdot(du[r], w_ref[t, :, hid + c:hid + c + chunk])
        for r in subs:
            rows = slice(r, r + sub)
            here = pl.ds(base + r, sub)
            gains_ref[0:1, :] += jnp.sum(dn[r] * unit1[r], axis=0, keepdims=True)
            scaled = dn[r] * ga_ref[...]
            d_first = rms1[r] * (scaled - unit1[r] * jnp.mean(scaled * unit1[r], axis=-1, keepdims=True))
            dfirst_ref[rows, :] = d_first
            d_attn = d_first.astype(BF16)
            dattn_s[here, :] = d_attn
            gown_ref[rows, :] = mm(d_attn, w_ref[me, :, outs]).astype(BF16)
            goth_ref[rows, :] = mm(d_attn, w_ref[1 - me, :, outs]).astype(BF16)

    @pl.when(step >= steps)
    def _():
        tile = step - steps
        t, part = lax.div(tile, parts), lax.rem(tile, parts)
        size = dattn_s.shape[1] // parts
        rows = pl.ds(pl.multiple_of(part * size, size), size)
        cols = pl.ds(pl.multiple_of(t * hid, hid), hid)
        mixed = jnp.where(t == me, mixed_s[:, :head_cols], mixed_s[:, head_cols:])
        for at, left, right in ((0, normed_s, dgate_s[:, cols]), (hid, normed_s, dup_s[:, cols]),
                                (2 * hid, dffn_s, hidden_s[:, cols]), (3 * hid, dattn_s, mixed)):
            value = tdot(left[:, rows], right).astype(BF16)
            there = slice(at, at + right.shape[1])
            if share is None:
                grads_ref[0, :, there] = value
            else:
                near = grads_ref.shape[1]
                for n in range(size // share):
                    grads_ref[0, n % near, n // near, :, there] = value[n * share:(n + 1) * share]


def feed(sched, x, own, oth, dy, weights, gain_attn, gain_ffn, hid, share, near,
         block=512, sub=256, chunk=512, parts=2):
    local, width = x.shape
    head_cols = own.shape[1]
    total = weights.shape[2]
    steps = local // block
    packed = share % 16 == 0

    def at(s):
        return jnp.minimum(s, steps - 1)

    rows = pl.BlockSpec((block, width), lambda s, sched: (at(s), 0))
    heads = pl.BlockSpec((block, head_cols), lambda s, sched: (at(s), 0))
    gain = pl.BlockSpec((1, width), lambda s, sched: (0, 0))

    def tile(s, sched):
        n = jnp.maximum(s - steps, 0)
        if packed:
            return (lax.div(n, parts), 0, lax.rem(n, parts), 0, 0)
        return (lax.div(n, parts), lax.rem(n, parts), 0)

    if packed:
        grads_shape = (2, near, width // (near * share), share, total)
        grads_block = (1, near, width // (near * share * parts), share, total)
    else:
        grads_shape, grads_block = (2, width, total), (1, width // parts, total)

    def shape(cols, dtype):
        return jax.ShapeDtypeStruct((local, cols), dtype)

    results = pl.pallas_call(
        partial(feed_kernel, block=block, sub=sub, chunk=chunk, local=local, hid=hid,
                head_cols=head_cols, parts=parts, share=share if packed else None),
        grid_spec=pltpu.PrefetchScalarGridSpec(
            num_scalar_prefetch=1,
            grid=(steps + 2 * parts,),
            in_specs=[rows, heads, heads, rows, pl.BlockSpec(memory_space=pl.ANY), gain, gain],
            out_specs=[rows, rows, heads, heads,
                       pl.BlockSpec(grads_block, tile),
                       pl.BlockSpec((16, width), lambda s, sched: (0, 0))],
            scratch_shapes=[pltpu.VMEM(weights.shape, BF16)]
            + [pltpu.VMEM((block, 2 * hid), F32)] * 2
            + [pltpu.VMEM((local, 2 * hid), BF16)] * 3
            + [pltpu.VMEM((local, width), BF16)] * 3
            + [pltpu.VMEM((local, 2 * head_cols), BF16), pltpu.SemaphoreType.DMA((4,))],
        ),
        out_shape=[
            shape(width, BF16), shape(width, F32), shape(head_cols, BF16), shape(head_cols, BF16),
            jax.ShapeDtypeStruct(grads_shape, BF16),
            jax.ShapeDtypeStruct((16, width), F32),
        ],
        compiler_params=params(60 * 1024 * 1024),
        cost_estimate=cost(12 * local * width * total, 30 * local * width),
        name="feed",
    )(sched, x, own, oth, dy, weights, gain_attn, gain_ffn)
    grads = results[4]
    if not packed:
        grads = grads.reshape(2, -1, near, share, total).swapaxes(1, 2)
    return (*results[:4], grads.reshape(-1, total), results[5])


def input_grad_kernel(sched, d_ref, w_ref, dfirst_ref, oth_ref, own_ref, *, half):
    step = pl.program_id(0)
    cols = d_ref.shape[1]
    order = [at + n * PAIR for n in range(3) for at in range(0, cols, 3 * PAIR)]
    part = rdot(jnp.concatenate([d_ref[:, at:at + PAIR] for at in order], axis=1), w_ref[...])

    @pl.when(step < half)
    def _():
        oth_ref[...] = part.astype(BF16)

    @pl.when(step >= half)
    def _():
        own_ref[...] = dfirst_ref[...] + part


def input_grads(sched, d_qkv, weights, d_first, block):
    local, width = d_first.shape
    cols = d_qkv.shape[1]
    half = local // block
    place, _ = placing(2 * half)
    own = pl.BlockSpec((block, width), lambda n, s: (jnp.maximum(n - half, 0), 0))
    return pl.pallas_call(
        partial(input_grad_kernel, half=half),
        grid_spec=pltpu.PrefetchScalarGridSpec(
            num_scalar_prefetch=1,
            grid=(2 * half,),
            in_specs=[pl.BlockSpec((block, cols), lambda n, s: (place(n, s), 0)),
                      pl.BlockSpec((width, cols), lambda n, s: (0, 0)), own],
            out_specs=[pl.BlockSpec((block, width), lambda n, s: (jnp.minimum(n, half - 1), 0)), own],
        ),
        out_shape=[jax.ShapeDtypeStruct((local, width), BF16),
                   jax.ShapeDtypeStruct((local, width), F32)],
        compiler_params=params(),
        cost_estimate=cost(4 * local * width * cols, 4 * local * (width + cols)),
        name="input_grads",
    )(sched, d_qkv, weights, d_first)


def finish_kernel(total_ref, gate_ref, up_ref, down_ref, out_ref):
    hid = gate_ref.shape[1]
    gate_ref[...] = total_ref[:, 0:hid].astype(F32)
    up_ref[...] = total_ref[:, hid:2 * hid].astype(F32)
    down_ref[...] = total_ref[:, 2 * hid:3 * hid].astype(F32)
    out_ref[...] = total_ref[:, 3 * hid:].astype(F32)


def finish(total, hid):
    share, cols = total.shape
    gate, up, down, out = pl.pallas_call(
        finish_kernel,
        out_shape=[jax.ShapeDtypeStruct((share, width), F32)
                   for width in (hid, hid, hid, cols - 3 * hid)],
        cost_estimate=cost(0, 6 * share * cols),
        name="finish",
    )(total)
    return gate, up, down.T, out.T


def exchange(value):
    return lax.ppermute(value, "tensor", [(0, 1), (1, 0)])


def flip(value, bit):
    count = lax.axis_size(DP)
    return lax.ppermute(value, DP, [(at, at ^ (1 << bit)) for at in range(count)])


def bit_orders(count):
    bits = count.bit_length() - 1
    low = list(range(min(2, bits)))
    high = list(range(min(2, bits), bits))
    return high[::-1] + low, high[::-1] + low[::-1]


def join(held, bit):
    other = flip(held, bit)
    mine = ((lax.axis_index(DP) >> bit) & 1) == 0
    return jnp.stack([jnp.where(mine, held, other), jnp.where(mine, other, held)])


def in_order(held, order):
    bits = len(order)
    rows, cols = held.shape[-2:]
    held = held.reshape((2,) * bits + (rows, cols))
    axes = [bits - 1 - order.index(bit) for bit in range(bits - 1, -1, -1)]
    return held.transpose(*axes, bits, bits + 1).reshape(-1, cols)


def gather_rows(piece, edge):
    fore, back = bit_orders(lax.axis_size(DP))
    high = len(fore) - min(2, len(fore))
    held = piece[None]
    for bit in fore[:high]:
        held = join(held, bit)
    parts = [held[..., :edge], held[..., edge:]]
    for one, two in zip(fore[high:], back[high:]):
        parts = [join(parts[0], one), join(parts[1], two)]
    return jnp.concatenate([in_order(parts[0], fore), in_order(parts[1], back)], axis=1)


def scatter_rows(total, order):
    me = lax.axis_index(DP)
    bits = len(order)
    rows, cols = total.shape[0] >> bits, total.shape[1]
    held = total.reshape((2,) * bits + (rows, cols))
    left = list(range(bits - 1, -1, -1))
    for bit in order:
        axis = left.index(bit)
        left.pop(axis)
        low = lax.index_in_dim(held, 0, axis, keepdims=False)
        high = lax.index_in_dim(held, 1, axis, keepdims=False)
        mine = ((me >> bit) & 1) == 0
        got = flip(jnp.where(mine, high, low), bit)
        held = (jnp.where(mine, low, high).astype(F32) + got.astype(F32)).astype(BF16)
    return held.reshape(rows, cols)


def local(tokens, w_query, w_key, w_value, w_out, w_gate, w_up, w_down, gain_attn, gain_ffn,
          lengths, cotangent):
    rows, width = tokens.shape
    slots = 2 * rows
    me = lax.axis_index("tensor")
    count = lax.axis_size(DP)
    cols, hid = w_query.shape[1], w_gate.shape[1]
    share = width // count
    edge = 5 * cols // 3
    bq, bk = rows, rows // 2
    blocks = slots // bq

    packed = jnp.concatenate([w_gate, w_up, w_down.T, w_out.T], axis=1)
    feed_w = lax.all_gather(packed, ("tensor",) + DP, axis=0, tiled=True)
    feed_w = feed_w.reshape(2, width, packed.shape[1])
    full_qkv = gather_rows(jnp.concatenate([w_query, w_key, w_value], axis=1), edge)
    other_x = exchange(tokens)

    index = jnp.arange(slots, dtype=jnp.int32)
    row = lengths[0]
    ends = jnp.cumsum(row)
    begins = jnp.sum(jnp.where(index[:, None] >= ends[None, :], row[None, :], 0), axis=1)
    position = (index - begins).astype(F32)
    lane = jnp.arange(PAIR, dtype=jnp.int32) % HEAD
    inverse = ROPE_BASE ** (-((lane % (HEAD // 2)).astype(F32) * 2.0 / HEAD))
    angle = position[:, None] * inverse[None, :]
    cosine = jnp.cos(angle)
    sine = jnp.where(lane[None, :] < HEAD // 2, -jnp.sin(angle), jnp.sin(angle))
    block_begin = begins.reshape(blocks, bq)
    sched = jnp.concatenate([
        jnp.stack([me.astype(jnp.int32), ends[-1]]),
        block_begin[:, 0] // bk,
        (block_begin[:, -1] + bk - 1) // bk,
    ])
    start = begins.reshape(1, slots)

    qkv, mixed_send, mixed_own, lse = attend_forward(
        sched, tokens, other_x, full_qkv, cosine, sine, start, bq, bk)
    mixed_oth = exchange(mixed_send)
    output, d_first, g_own, g_send, grads, gains = feed(
        sched, tokens, mixed_own, mixed_oth, cotangent, feed_w, gain_attn.reshape(1, width),
        gain_ffn.reshape(1, width), hid, share, lax.axis_size("near"))
    g_oth = exchange(g_send)
    reduced = lax.psum_scatter(grads, ("tensor", "near"), scatter_dimension=0, tiled=True)
    reduced = lax.psum_scatter(reduced, "far", scatter_dimension=0, tiled=True)
    gains = gains[:2] + exchange(gains[:2])
    d_qkv, dw = attend_backward(sched, qkv, cosine, sine, start, lse, mixed_send, mixed_own,
                                g_oth, g_own, tokens, other_x, bq, bk)
    dw, gains = lax.optimization_barrier((dw, gains))
    fore, back = bit_orders(count)
    for bit in fore[::-1]:
        gains = gains + flip(gains, bit)
    dw = jnp.concatenate([scatter_rows(dw[:, :edge], fore[::-1]),
                          scatter_rows(dw[:, edge:], back[::-1])], axis=1).astype(F32)
    dw = dw.reshape(share, cols // PAIR, 3, PAIR)
    x_send, x_own = input_grads(sched, d_qkv, full_qkv, d_first, 512)
    input_grad = (x_own + exchange(x_send).astype(F32)).astype(BF16)
    grad_gate, grad_up, grad_down, grad_out = finish(reduced, hid)
    return (
        output,
        input_grad,
        dw[:, :, 0].reshape(share, cols),
        dw[:, :, 1].reshape(share, cols),
        dw[:, :, 2].reshape(share, cols),
        grad_out,
        grad_gate,
        grad_up,
        grad_down,
        gains[0],
        gains[1],
    )


def solution(mesh):
    count, pair = mesh.shape["dp"], mesh.shape["tensor"]
    near = min(4, count)
    mesh = Mesh(mesh.devices.reshape(count // near, near, pair), DP + ("tensor",))
    split = P(DP, "tensor")
    turned = P("tensor", DP)
    slots = P(DP + ("tensor",), None)
    return jax.shard_map(
        local,
        mesh=mesh,
        in_specs=(slots, split, split, split, turned, split, split, turned, P(), P(),
                  P(DP, None), slots),
        out_specs=(slots, slots, split, split, split, turned, split, split, turned, P(), P()),
        check_vma=False,
    )
```

time: 350 us -> 312 us (0.89); the launches traced: 353 us -> 308 us
  Pallas kernels: 183 us -> 154 us
  starting transfers between devices: 47.1 us -> 30.7 us
  other arithmetic: 15.1 us -> 18.8 us
    pallas_call x6 -> x4, Pallas kernels: 172 us -> 144 us  [the longest x1 56.3 us: feed(): pl.pallas_call(partial(feed_kernel, block=block, sub=sub, chunk=chunk, lo...]
    ppermute x24 -> x18, starting transfers between devices: 46.5 us -> 30 us  [flip(): return lax.ppermute(value, DP, [(at, at ^ 1 << bit) for at in range(count)])]
    all_gather x1, waiting for transfers between devices: 0.01 us -> 9.38 us  [local(): feed_w = lax.all_gather(packed, ('tensor',) + DP, axis=0, tiled=True)]
    reduce_scatter x1 -> x2, waiting for transfers between devices: 10.4 us -> 2.52 us  [the longest x1 2.52 us: local(): reduced = lax.psum_scatter(reduced, 'far', scatter_dimension=0, tiled=True)]
    transpose x5 -> x2, local copies, waits for them, and re-layouts: 4.04 us -> 0.15 us  [in_order(): return held.transpose(*axes, bits, bits + 1).reshape(-1, cols)]
    ppermute x24 -> x18, waiting for transfers between devices: 65.7 us -> 62.9 us  [flip(): return lax.ppermute(value, DP, [(at, at ^ 1 << bit) for at in range(count)])]
  transfers between devices with their start and end apart: 31 -> 26, of which waited for: 19 -> 14; matrix products, arithmetic and copies ran while one was open for 6% -> 9% of each run, Pallas kernels for 35% -> 31%
where the time goes in v2:
time: 312 us; the launch traced here: 308 us
  Pallas kernels  154 us (49%)
  waiting for transfers between devices  77.2 us (25%)
  starting transfers between devices  30.7 us (10%)
  other arithmetic  18.8 us (6%)
  between operations  14.5 us (5%)
  local copies, waits for them, and re-layouts  12.5 us (4%)
    ppermute x18, waiting for transfers between devices, flip(): return lax.ppermute(value, DP, [(at, at ^ 1 << bit) for at in range(count)])  62.9 us
    pallas_call x1, Pallas kernels, feed(): pl.pallas_call(partial(feed_kernel, block=block, sub=sub, chunk=chunk, lo...  56.3 us
    pallas_call x1, Pallas kernels, attend_backward(): pl.pallas_call(partial(backward_kernel, bq=bq, bk=bk, sub=sub, blocks=blo...  52.1 us
    pallas_call x1, Pallas kernels, attend_forward(): pl.pallas_call(partial(forward_kernel, bq=bq, bk=bk, sub=sub, chunk=chunk...  33.6 us
    ppermute x18, starting transfers between devices, flip(): return lax.ppermute(value, DP, [(at, at ^ 1 << bit) for at in range(count)])  30 us
    pallas_call x1, Pallas kernels, input_grads(): pl.pallas_call(partial(input_grad_kernel, half=half), grid_spec=pltpu.Pre...  10.4 us
    all_gather x1, waiting for transfers between devices, local(): feed_w = lax.all_gather(packed, ('tensor',) + DP, axis=0, tiled=True)  9.38 us
  transfers between devices with their start and end apart: 26, of which 14 were waited for; matrix products, arithmetic and copies ran while one was open for 9% of the time, Pallas kernels for 31%

profile of v2, /device:TPU:0, one launch (start us, length us, event | category | flops | bytes accessed | tf_op | source)
XLA Modules:
  0.0 307.8 jit_solution(5482976302690657816)
XLA Ops:
  7.3 1.8 pad_maximum_fusion.3
  9.9 4.1 %collective-permute-start.1 = (bf16[1,48,1152]{2,1,0:T(8,128)(2,1)S(1)}, bf16[1,48,1152]{2,1,0:T(8,128)(2,1)S(1)}, u32[]{:S(2)}, u32[]{:S(2)}) collective-permute-start(bf16[1,48,1152]{2,1,0:T(8,128)(2,1)S(1)} %maximum_bitcast_fusion.2), channel_id=1, source_target_pairs={{0,16},{2,18},{4,20},{6,22},{8,24},{10,26},{12,28},{14,30},{16,0},... | collective-permute-start | bytes 331784 | tf_op jit(solution)/shard_map/ppermute | solution.py:590
  16.2 5.6 %negate_select_fusion = (f32[2048,128]{1,0:T(8,128)}, f32[2048,128]{1,0:T(8,128)}) fusion(f32[128]{0:T(128)S(1)} %fusion.28, f32[2048]{0:T(1024)S(1)} %subtract_convert_fusion, pred[128]{0:T(512)(128)(4,1)S(1)} %broadcast_compare_fusion), kind=kLoop, calls=%fused_computation.2 | loop fusion | flops 786432 | bytes 2105984 | tf_op jit(solution)/shard_map/jit(_where)/select_n | solution.py:670
  22.2 1.6 collective-permute-start.2
  23.8 12.0 %collective-permute-done.2 = bf16[2,1,48,1152]{3,2,0,1:T(8,128)(2,1)S(1)} collective-permute-done((bf16[2,1,48,1152]{3,2,0,1:T(8,128)(2,1)S(1)}, bf16[2,1,48,1152]{3,2,0,1:T(8,128)(2,1)S(1)}, u32[]{:S(2)}, u32[]{:S(2)}) %collective-permute-start.2) | collective-permute-done | bytes 221216 | tf_op jit(solution)/shard_map/ppermute | solution.py:590
  39.5 2.2 collective-permute-done.5
  42.9 6.3 %collective-permute-done.3 = bf16[2,2,1,48,640]{4,3,1,0,2:T(8,128)(2,1)S(1)} collective-permute-done((bf16[2,2,1,48,640]{4,3,1,0,2:T(8,128)(2,1)S(1)}, bf16[2,2,1,48,640]{4,3,1,0,2:T(8,128)(2,1)S(1)}, u32[]{:S(2)}, u32[]{:S(2)}) %collective-permute-start.3) | collective-permute-done | bytes 245792 | tf_op jit(solution)/shard_map/ppermute | solution.py:590
  49.5 13.2 %collective-permute-done.6 = bf16[2,2,2,1,48,512]{5,4,2,1,0,3:T(8,128)(2,1)S(1)} collective-permute-done((bf16[2,2,2,1,48,512]{5,4,2,1,0,3:T(8,128)(2,1)S(1)}, bf16[2,2,2,1,48,512]{5,4,2,1,0,3:T(8,128)(2,1)S(1)}, u32[]{:S(2)}, u32[]{:S(2)}) %collective-permute-start.6) | collective-permute-done | bytes 393248 | tf_op jit(solution)/shard_map/ppermute | solution.py:590
  65.9 33.6 %attend_forward.1 = (bf16[2048,1152]{1,0:T(8,128)(2,1)}, bf16[1024,384]{1,0:T(8,128)(2,1)}, bf16[1024,384]{1,0:T(8,128)(2,1)}, f32[3,2,2048]{2,1,0:T(2,128)}) custom-call(s32[6]{0:T(128)} %pad_add_fusion.sched, bf16[1024,768]{1,0:T(8,128)(2,1)} %x_own_ref.1, bf16[1024,768]{1,0:T(8,128)(2,1)} %copy-done.7, ...), custom_call_target="tpu_custom_call" | custom-call | flops 10066329600 | bytes 12582912 | tf_op jit(solution)/shard_map/attend_forward/pallas_call | solution.py:153
  102.0 9.4 %all-gather.2.cloned.1.call-done = bf16[1536,3456]{1,0:T(8,128)(2,1)} async-done(((bf16[48,3456]{1,0:T(8,128)(2,1)}), bf16[1536,3456]{1,0:T(8,128)(2,1)}) %all-gather.2.cloned.1.call-update) | async-done | bytes 10616848 | tf_op jit(solution)/shard_map/all_gather | solution.py:656
  111.4 56.3 %feed.1 = (bf16[1024,768]{1,0:T(8,128)(2,1)}, f32[1024,768]{1,0:T(8,128)}, bf16[1024,384]{1,0:T(8,128)(2,1)}, bf16[1024,384]{1,0:T(8,128)(2,1)}, bf16[2,4,4,48,3...) custom-call(s32[6]{0:T(128)} %pad_add_fusion.sched, bf16[1024,768]{1,0:T(8,128)(2,1)} %x_own_ref.1, ...), custom_call_target="tpu_custom_call" | custom-call | flops 32614907904 | bytes 23592960 | tf_op jit(solution)/shard_map/feed/pallas_call | solution.py:495
  172.8 52.1 %attend_backward.1 = (bf16[2048,1152]{1,0:T(8,128)(2,1)}, bf16[768,1152]{1,0:T(8,128)(2,1)}) custom-call(s32[6]{0:T(128)} %pad_add_fusion.sched, bf16[2048,1152]{1,0:T(8,128)(2,1)} %get-tuple-element.34.q_ref.k_ref.v_ref, bf16[2048,1152]{1,0:T(8,128)(2,1)} %get-tuple-element.34.q_ref.k_ref.v_ref, bf16[2048,1152]{1,0:T(8,128)(2,1)} %get-tuple-element.34.q_ref.k_ref.v_ref, ...), custom_call_target="tpu_custom_call" | custom-call | flops 19730006016 | bytes 15728640 | tf_op jit(solution)/shard_map/attend_backward/pallas_call | solution.py:298
  224.9 10.5 %collective-permute-start.19 = (f32[2,768]{1,0:T(2,128)S(1)}, f32[2,768]{1,0:T(2,128)S(1)}, u32[]{:S(2)}, u32[]{:S(2)}) collective-permute-start(f32[2,768]{1,0:T(2,128)S(1)} %slice_add_fusion.1), channel_id=1, source_target_pairs={{0,4},{2,6},{4,0},{6,2},{8,12},{10,14},{12,8},{14,10},{16,20},{18,... | collective-permute-start | bytes 18440 | tf_op jit(solution)/shard_map/ppermute | solution.py:590
  240.2 1.6 collective-permute-done.20
  245.4 1.4 collective-permute-start.22
  246.9 10.4 %input_grads.1 = (bf16[1024,768]{1,0:T(8,128)(2,1)}, f32[1024,768]{1,0:T(8,128)}) custom-call(s32[6]{0:T(128)} %pad_add_fusion.sched, bf16[2048,1152]{1,0:T(8,128)(2,1)} %get-tuple-element.38.d_ref, bf16[768,1152]{1,0:T(8,128)(2,1)} %pad_maximum_fusion.wq_ref.wk_ref.wv_ref.w_ref, f32[1024,768]{1,0:T(8,128)} %get-tuple-element.39.dfirst_ref), custom_call_target="tpu_custom_call" | custom-call | flops 3623878656 | bytes 7864320 | tf_op jit(solution)/shard_map/input_grads/pallas_call | solution.py:547
  259.2 5.6 %collective-permute-done.16 = bf16[2,2,48,512]{3,2,1,0:T(8,128)(2,1)S(1)} collective-permute-done((bf16[2,2,48,512]{3,2,1,0:T(8,128)(2,1)S(1)}, bf16[2,2,48,512]{3,2,1,0:T(8,128)(2,1)S(1)}, u32[]{:S(2)}, u32[]{:S(2)}) %collective-permute-start.16) | collective-permute-done | bytes 196640 | tf_op jit(solution)/shard_map/ppermute | solution.py:590
  265.7 3.9 %collective-permute-done.17 = bf16[2,48,512]{2,1,0:T(8,128)(2,1)S(1)} collective-permute-done((bf16[2,48,512]{2,1,0:T(8,128)(2,1)S(1)}, bf16[2,48,512]{2,1,0:T(8,128)(2,1)S(1)}, u32[]{:S(2)}, u32[]{:S(2)}) %collective-permute-start.17) | collective-permute-done | bytes 98336 | tf_op jit(solution)/shard_map/ppermute | solution.py:590
  269.9 2.6 collective-permute-start.18
  272.6 7.3 %collective-permute-done.13 = bf16[2,48,640]{2,1,0:T(8,128)(2,1)S(1)} collective-permute-done((bf16[2,48,640]{2,1,0:T(8,128)(2,1)S(1)}, bf16[2,48,640]{2,1,0:T(8,128)(2,1)S(1)}, u32[]{:S(2)}, u32[]{:S(2)}) %collective-permute-start.13) | collective-permute-done | bytes 122912 | tf_op jit(solution)/shard_map/ppermute | solution.py:590
  280.0 9.5 %collective-permute-done.14 = bf16[48,640]{1,0:T(8,128)(2,1)S(1)} collective-permute-done((bf16[48,640]{1,0:T(8,128)(2,1)S(1)}, bf16[48,640]{1,0:T(8,128)(2,1)S(1)}, u32[]{:S(2)}, u32[]{:S(2)}) %collective-permute-start.14) | collective-permute-done | bytes 61472 | tf_op jit(solution)/shard_map/ppermute | solution.py:590
  293.9 2.9 add_convert_fusion
  296.7 2.5 reduce-scatter.5.cloned.1.call-done.total_ref
  299.3 1.8 finish.1
  (127 shorter events, 35.2 us)
Async XLA Ops:
  7.2 104.2 %all-gather.2.cloned.1.call-start = ((), (), s32[]{:S(2)}) async-start(), calls=%async_computation.2 | async-start | bytes 10948608 | tf_op jit(solution)/shard_map/all_gather | solution.py:656
  9.0 256.0 %reduce-scatter.3.cloned.1.call-start = ((), (), s32[]{:S(2)}) async-start(), calls=%async_computation.3 | async-start | bytes 11943936 | tf_op jit(solution)/shard_map/reduce_scatter | solution.py:686
  9.9 12.1 %collective-permute-start.1 = (bf16[1,48,1152]{2,1,0:T(8,128)(2,1)S(1)}, bf16[1,48,1152]{2,1,0:T(8,128)(2,1)S(1)}, u32[]{:S(2)}, u32[]{:S(2)}) collective-permute-start(bf16[1,48,1152]{2,1,0:T(8,128)(2,1)S(1)} %maximum_bitcast_fusion.2), channel_id=1, source_target_pairs={{0,16},{2,18},{4,20},{6,22},{8,24},{10,26},{12,28},{14,30},{16,0},... | collective-permute-start | bytes 331784 | tf_op jit(solution)/shard_map/ppermute | solution.py:590
  14.0 50.7 %collective-permute-start = (bf16[1024,768]{1,0:T(8,128)(2,1)}, bf16[1024,768]{1,0:T(8,128)(2,1)S(1)}, u32[]{:S(2)}, u32[]{:S(2)}) collective-permute-start(bf16[1024,768]{1,0:T(8,128)(2,1)} %x_own_ref.1), channel_id=1, source_target_pairs={{0,1},{1,0},{2,3},{3,2},{4,5},{5,4},{6,7},{7,6},{8,9},{9,8},{10,11... | collective-permute-start | bytes 4718600 | tf_op jit(solution)/shard_map/ppermute | solution.py:585
  22.2 13.6 %collective-permute-start.2 = (bf16[2,1,48,1152]{3,2,0,1:T(8,128)(2,1)S(1)}, bf16[2,1,48,1152]{3,2,0,1:T(8,128)(2,1)S(1)}, u32[]{:S(2)}, u32[]{:S(2)}) collective-permute-start(bf16[2,1,48,1152]{3,2,0,1:T(8,128)(2,1)S(1)} %fusion.16), channel_id=1, source_target_pairs={{0,8},{2,10},{4,12},{6,14},{8,0},{10,2},{12,4},{14,6},{16,24},{18,... | collective-permute-start | bytes 663560 | tf_op jit(solution)/shard_map/ppermute | solution.py:590
  35.9 5.7 %collective-permute-start.5 = (bf16[2,2,1,48,512]{4,3,1,0,2:T(8,128)(2,1)S(1)}, bf16[2,2,1,48,512]{4,3,1,0,2:T(8,128)(2,1)S(1)}, u32[]{:S(2)}, u32[]{:S(2)}) collective-permute-start(bf16[2,2,1,48,512]{4,3,1,0,2:T(8,128)(2,1)S(1)} %fusion.23), channel_id=1, source_target_pairs={{0,4},{2,6},{4,0},{6,2},{8,12},{10,14},{12,8},{14,10},{16,20},{18,... | collective-permute-start | bytes 589832 | tf_op jit(solution)/shard_map/ppermute | solution.py:590
  38.5 10.7 %collective-permute-start.3 = (bf16[2,2,1,48,640]{4,3,1,0,2:T(8,128)(2,1)S(1)}, bf16[2,2,1,48,640]{4,3,1,0,2:T(8,128)(2,1)S(1)}, u32[]{:S(2)}, u32[]{:S(2)}) collective-permute-start(bf16[2,2,1,48,640]{4,3,1,0,2:T(8,128)(2,1)S(1)} %fusion.30), channel_id=1, source_target_pairs={{0,2},{2,0},{4,6},{6,4},{8,10},{10,8},{12,14},{14,12},{16,18},{18,... | collective-permute-start | bytes 737288 | tf_op jit(solution)/shard_map/ppermute | solution.py:590
  41.8 20.8 %collective-permute-start.6 = (bf16[2,2,2,1,48,512]{5,4,2,1,0,3:T(8,128)(2,1)S(1)}, bf16[2,2,2,1,48,512]{5,4,2,1,0,3:T(8,128)(2,1)S(1)}, u32[]{:S(2)}, u32[]{:S(2)}) collective-permute-start(bf16[2,2,2,1,48,512]{5,4,2,1,0,3:T(8,128)(2,1)S(1)} %fusion.7), channel_id=1, source_target_pairs={{0,2},{2,0},{4,6},{6,4},{8,10},{10,8},{12,14},{14,12},{16,18},{18,... | collective-permute-start | bytes 1179656 | tf_op jit(solution)/shard_map/ppermute | solution.py:590
  49.4 13.6 %collective-permute-start.4 = (bf16[2,2,2,1,48,640]{5,4,2,1,0,3:T(8,128)(2,1)S(1)}, bf16[2,2,2,1,48,640]{5,4,2,1,0,3:T(8,128)(2,1)S(1)}, u32[]{:S(2)}, u32[]{:S(2)}) collective-permute-start(bf16[2,2,2,1,48,640]{5,4,2,1,0,3:T(8,128)(2,1)S(1)} %fusion.6), channel_id=1, source_target_pairs={{0,4},{2,6},{4,0},{6,2},{8,12},{10,14},{12,8},{14,10},{16,20},{18,... | collective-permute-start | bytes 1474568 | tf_op jit(solution)/shard_map/ppermute | solution.py:590
  167.7 131.5 %reduce-scatter.5.cloned.1.call-start = ((), (), s32[]{:S(2)}) async-start(), calls=%async_computation.4 | async-start | bytes 1658880 | tf_op jit(solution)/shard_map/reduce_scatter | solution.py:687
  168.8 3.1 collective-permute-start.8
  224.9 13.1 %collective-permute-start.19 = (f32[2,768]{1,0:T(2,128)S(1)}, f32[2,768]{1,0:T(2,128)S(1)}, u32[]{:S(2)}, u32[]{:S(2)}) collective-permute-start(f32[2,768]{1,0:T(2,128)S(1)} %slice_add_fusion.1), channel_id=1, source_target_pairs={{0,4},{2,6},{4,0},{6,2},{8,12},{10,14},{12,8},{14,10},{16,20},{18,... | collective-permute-start | bytes 18440 | tf_op jit(solution)/shard_map/ppermute | solution.py:590
  237.9 3.9 %collective-permute-start.20 = (f32[2,768]{1,0:T(2,128)S(1)}, f32[2,768]{1,0:T(2,128)S(1)}, u32[]{:S(2)}, u32[]{:S(2)}) collective-permute-start(f32[2,768]{1,0:T(2,128)S(1)} %add.99), channel_id=1, source_target_pairs={{0,2},{2,0},{4,6},{6,4},{8,10},{10,8},{12,14},{14,12},{16,18},{18,... | collective-permute-start | bytes 18440 | tf_op jit(solution)/shard_map/ppermute | solution.py:590
  239.1 18.2 %collective-permute-start.15 = (bf16[2,2,2,48,512]{4,3,2,1,0:T(8,128)(2,1)S(1)}, bf16[2,2,2,48,512]{4,3,2,1,0:T(8,128)(2,1)S(1)}, u32[]{:S(2)}, u32[]{:S(2)}) collective-permute-start(bf16[2,2,2,48,512]{4,3,2,1,0:T(8,128)(2,1)S(1)} %select_bitcast_fusion.2), channel_id=1, source_target_pairs={{0,2},{2,0},{4,6},{6,4},{8,10},{10,8},{12,14},{14,12},{16,18},{18,... | collective-permute-start | bytes 1179656 | tf_op jit(solution)/shard_map/ppermute | solution.py:590
  241.8 3.6 %collective-permute-start.21 = (f32[2,768]{1,0:T(2,128)S(1)}, f32[2,768]{1,0:T(2,128)S(1)}, u32[]{:S(2)}, u32[]{:S(2)}) collective-permute-start(f32[2,768]{1,0:T(2,128)S(1)} %add.100), channel_id=1, source_target_pairs={{0,8},{2,10},{4,12},{6,14},{8,0},{10,2},{12,4},{14,6},{16,24},{18,... | collective-permute-start | bytes 18440 | tf_op jit(solution)/shard_map/ppermute | solution.py:590
  243.0 15.5 %collective-permute-start.11 = (bf16[2,2,2,48,640]{4,3,1,0,2:T(8,128)(2,1)S(1)}, bf16[2,2,2,48,640]{4,3,1,0,2:T(8,128)(2,1)S(1)}, u32[]{:S(2)}, u32[]{:S(2)}) collective-permute-start(bf16[2,2,2,48,640]{4,3,1,0,2:T(8,128)(2,1)S(1)} %select_bitcast_fusion), channel_id=1, source_target_pairs={{0,4},{2,6},{4,0},{6,2},{8,12},{10,14},{12,8},{14,10},{16,20},{18,... | collective-permute-start | bytes 1474568 | tf_op jit(solution)/shard_map/ppermute | solution.py:590
  245.4 11.8 %collective-permute-start.22 = (f32[2,768]{1,0:T(2,128)S(1)}, f32[2,768]{1,0:T(2,128)S(1)}, u32[]{:S(2)}, u32[]{:S(2)}) collective-permute-start(f32[2,768]{1,0:T(2,128)S(1)} %add.101), channel_id=1, source_target_pairs={{0,16},{2,18},{4,20},{6,22},{8,24},{10,26},{12,28},{14,30},{16,0},... | collective-permute-start | bytes 18440 | tf_op jit(solution)/shard_map/ppermute | solution.py:590
  257.2 36.7 %collective-permute-start.9 = (bf16[1024,768]{1,0:T(8,128)(2,1)}, bf16[1024,768]{1,0:T(8,128)(2,1)}, u32[]{:S(2)}, u32[]{:S(2)}) collective-permute-start(bf16[1024,768]{1,0:T(8,128)(2,1)} %get-tuple-element.41), channel_id=1, source_target_pairs={{0,1},{1,0},{2,3},{3,2},{4,5},{5,4},{6,7},{7,6},{8,9},{9,8},{10,11... | collective-permute-start | bytes 4718600 | tf_op jit(solution)/shard_map/ppermute | solution.py:585
  257.4 7.4 %collective-permute-start.16 = (bf16[2,2,48,512]{3,2,1,0:T(8,128)(2,1)S(1)}, bf16[2,2,48,512]{3,2,1,0:T(8,128)(2,1)S(1)}, u32[]{:S(2)}, u32[]{:S(2)}) collective-permute-start(bf16[2,2,48,512]{3,2,1,0:T(8,128)(2,1)S(1)} %fusion.13), channel_id=1, source_target_pairs={{0,4},{2,6},{4,0},{6,2},{8,12},{10,14},{12,8},{14,10},{16,20},{18,... | collective-permute-start | bytes 589832 | tf_op jit(solution)/shard_map/ppermute | solution.py:590
  258.8 10.9 %collective-permute-start.12 = (bf16[2,2,48,640]{3,2,1,0:T(8,128)(2,1)S(1)}, bf16[2,2,48,640]{3,2,1,0:T(8,128)(2,1)S(1)}, u32[]{:S(2)}, u32[]{:S(2)}) collective-permute-start(bf16[2,2,48,640]{3,2,1,0:T(8,128)(2,1)S(1)} %select_bitcast_fusion.4), channel_id=1, source_target_pairs={{0,2},{2,0},{4,6},{6,4},{8,10},{10,8},{12,14},{14,12},{16,18},{18,... | collective-permute-start | bytes 737288 | tf_op jit(solution)/shard_map/ppermute | solution.py:590
  264.9 4.7 %collective-permute-start.17 = (bf16[2,48,512]{2,1,0:T(8,128)(2,1)S(1)}, bf16[2,48,512]{2,1,0:T(8,128)(2,1)S(1)}, u32[]{:S(2)}, u32[]{:S(2)}) collective-permute-start(bf16[2,48,512]{2,1,0:T(8,128)(2,1)S(1)} %fusion.20), channel_id=1, source_target_pairs={{0,8},{2,10},{4,12},{6,14},{8,0},{10,2},{12,4},{14,6},{16,24},{18,... | collective-permute-start | bytes 294920 | tf_op jit(solution)/shard_map/ppermute | solution.py:590
  269.8 10.1 %collective-permute-start.13 = (bf16[2,48,640]{2,1,0:T(8,128)(2,1)S(1)}, bf16[2,48,640]{2,1,0:T(8,128)(2,1)S(1)}, u32[]{:S(2)}, u32[]{:S(2)}) collective-permute-start(bf16[2,48,640]{2,1,0:T(8,128)(2,1)S(1)} %fusion.17), channel_id=1, source_target_pairs={{0,8},{2,10},{4,12},{6,14},{8,0},{10,2},{12,4},{14,6},{16,24},{18,... | collective-permute-start | bytes 368648 | tf_op jit(solution)/shard_map/ppermute | solution.py:590
  269.9 10.1 %collective-permute-start.18 = (bf16[48,512]{1,0:T(8,128)(2,1)S(1)}, bf16[48,512]{1,0:T(8,128)(2,1)S(1)}, u32[]{:S(2)}, u32[]{:S(2)}) collective-permute-start(bf16[48,512]{1,0:T(8,128)(2,1)S(1)} %select_bitcast_fusion.11), channel_id=1, source_target_pairs={{0,16},{2,18},{4,20},{6,22},{8,24},{10,26},{12,28},{14,30},{16,0},... | collective-permute-start | bytes 147464 | tf_op jit(solution)/shard_map/ppermute | solution.py:590
  279.9 9.6 %collective-permute-start.14 = (bf16[48,640]{1,0:T(8,128)(2,1)S(1)}, bf16[48,640]{1,0:T(8,128)(2,1)S(1)}, u32[]{:S(2)}, u32[]{:S(2)}) collective-permute-start(bf16[48,640]{1,0:T(8,128)(2,1)S(1)} %select_bitcast_fusion.10), channel_id=1, source_target_pairs={{0,16},{2,18},{4,20},{6,22},{8,24},{10,26},{12,28},{14,30},{16,0},... | collective-permute-start | bytes 184328 | tf_op jit(solution)/shard_map/ppermute | solution.py:590
  (13 other events, 172.7 us)
Sparse Core Ops, SparseCore 0:
  11.5 99.8 all-gather.1
  167.8 86.2 reduce-scatter.2
  265.2 34.0 reduce-scatter.4

commit v3 on v2

--- a/solution.py
+++ b/solution.py
@@ -51,9 +51,12 @@
 
 
 def head_masks(values):
+    return one_head(values, 0), one_head(values, 1)
+
+
+def one_head(values, h):
     lane = lax.broadcasted_iota(jnp.int32, (1, PAIR), 1)
-    low = (lane < HEAD).astype(values.dtype)
-    return (values * low, values * (1 - low))
+    return values * (lane // HEAD == h).astype(values.dtype)
 
 
 def forward_kernel(sched, own_x_ref, oth_x_ref, wq_ref, wk_ref, wv_ref, cos_ref, sin_ref, start_ref,
@@ -68,8 +71,7 @@
         weights = jnp.concatenate([wq_ref[...], wk_ref[...], wv_ref[...]], axis=1)
         for x_ref, side in ((own_x_ref, sched[0]), (oth_x_ref, 1 - sched[0])):
             for r in range(0, local, chunk):
-                at = pl.multiple_of(side * local + r, chunk)
-                here = pl.ds(at, chunk)
+                here = pl.ds(pl.multiple_of(side * local + r, chunk), chunk)
                 u = mm(x_ref[r:r + chunk, :], weights)
                 cosine, sine = cos_ref[here, :], sin_ref[here, :]
                 for n, scale in ((0, HEAD ** -0.5), (1, 1.0)):
@@ -80,49 +82,50 @@
                 qkv_ref[here, 2 * PAIR:] = v.astype(BF16)
                 vt_ref[:, here] = v.T.astype(BF16)
 
-    queries = head_masks(qkv_ref[pl.ds(pl.multiple_of(i * bq, bq), bq), 0:PAIR])
     start = start_ref[...]
     acc_ref[...] = jnp.zeros_like(acc_ref)
-    streams = [(h, c) for h in range(2) for c in range(0, bq, sub)]
-
-    def visit(j, carry, masked, last):
-        at = pl.multiple_of(i * bq if last else j * bk, bk)
-        scores, out = [], []
-        for h, c in streams:
-            size = c + sub if last else bk
-            s = rdot(qkv_ref[pl.ds(at, size), PAIR:2 * PAIR], queries[h][c:c + sub])
-            if masked:
-                key_index = at + lax.broadcasted_iota(jnp.int32, (size, sub), 0)
-                query_index = i * bq + c + lax.broadcasted_iota(jnp.int32, (size, sub), 1)
-                allowed = (key_index >= start[:, c:c + sub]) & (key_index <= query_index)
-                s = jnp.where(allowed, s, NEGATIVE)
-            scores.append(s)
-        for n, (h, c) in enumerate(streams):
-            size = c + sub if last else bk
+    streams = list(range(0, bq, sub))
+
+    @pl.loop(0, 2)
+    def _(h):
+        queries = one_head(qkv_ref[pl.ds(pl.multiple_of(i * bq, bq), bq), 0:PAIR], h)
+        rows = pl.ds(pl.multiple_of(h * HEAD, HEAD), HEAD)
+
+        def visit(j, carry, last):
+            at = pl.multiple_of(i * bq if last else j * bk, bk)
+            scores, out = [], []
+            for c in streams:
+                size = c + sub if last else bk
+                s = rdot(qkv_ref[pl.ds(at, size), PAIR:2 * PAIR], queries[c:c + sub])
+                key_index = lax.broadcasted_iota(jnp.int32, (size, sub), 0)
+                allowed = key_index >= start[:, c:c + sub] - at
+                if last:
+                    query_index = c + lax.broadcasted_iota(jnp.int32, (size, sub), 1)
+                    allowed = allowed & (key_index <= query_index)
+                scores.append(jnp.where(allowed, s, NEGATIVE))
+            for n, c in enumerate(streams):
+                size = c + sub if last else bk
+                peak, total = carry[2 * n], carry[2 * n + 1]
+                new_peak = jnp.maximum(peak, jnp.max(scores[n], axis=0, keepdims=True))
+                fade = jnp.exp(peak - new_peak)
+                expo = jnp.exp(scores[n] - new_peak)
+                total = total * fade + jnp.sum(expo, axis=0, keepdims=True)
+                cols = slice(c, c + sub)
+                acc_ref[rows, cols] = acc_ref[rows, cols] * fade + mm(
+                    vt_ref[rows, pl.ds(at, size)], expo.astype(BF16)
+                )
+                out += [new_peak, total]
+            return tuple(out)
+
+        carry = (jnp.full((1, sub), NEGATIVE, F32), jnp.zeros((1, sub), F32)) * len(streams)
+        carry = lax.fori_loop(sched[2 + i], i * (bq // bk), lambda j, c: visit(j, c, False), carry)
+        carry = visit(None, carry, True)
+        for n, c in enumerate(streams):
             peak, total = carry[2 * n], carry[2 * n + 1]
-            new_peak = jnp.maximum(peak, jnp.max(scores[n], axis=0, keepdims=True))
-            fade = jnp.exp(peak - new_peak)
-            expo = jnp.exp(scores[n] - new_peak)
-            total = total * fade + jnp.sum(expo, axis=0, keepdims=True)
-            rows, cols = pl.ds(h * HEAD, HEAD), slice(c, c + sub)
-            acc_ref[rows, cols] = acc_ref[rows, cols] * fade + mm(
-                vt_ref[rows, pl.ds(at, size)], expo.astype(BF16)
-            )
-            out += [new_peak, total]
-        return tuple(out)
-
-    low = sched[2 + i]
-    top = i * (bq // bk)
-    mid = jnp.minimum(sched[2 + blocks + i], top)
-    carry = (jnp.full((1, sub), NEGATIVE, F32), jnp.zeros((1, sub), F32)) * len(streams)
-    carry = lax.fori_loop(low, mid, lambda j, c: visit(j, c, True, False), carry)
-    carry = lax.fori_loop(jnp.maximum(low, mid), top, lambda j, c: visit(j, c, False, False), carry)
-    carry = visit(None, carry, True, True)
-    for n, (h, c) in enumerate(streams):
-        peak, total = carry[2 * n], carry[2 * n + 1]
-        rows, cols = slice(h * HEAD, (h + 1) * HEAD), slice(c, c + sub)
-        acc_ref[rows, cols] = acc_ref[rows, cols] / total
-        lse_ref[h:h + 1, cols] = peak + jnp.log(total)
+            cols = slice(c, c + sub)
+            acc_ref[rows, cols] = acc_ref[rows, cols] / total
+            lse_ref[pl.ds(h, 1), cols] = peak + jnp.log(total)
+
     mixed = acc_ref[...].T.astype(BF16)
 
     @pl.when(step < half)
@@ -202,7 +205,7 @@
     couts = head_masks(grads)
     query_t = q_ref[...].astype(F32).T.astype(BF16)
     cout_t = grads.astype(F32).T.astype(BF16)
-    start = start_ref[...]
+    begin = jnp.broadcast_to(start_ref[...], (PAIR, bq)).T
     product = grads.astype(F32) * mixed.astype(F32)
     big = product.astype(BF16)
     small = (product - big.astype(F32)).astype(BF16)
@@ -216,7 +219,7 @@
     def wide(value, size):
         return jnp.concatenate([value] * (size // PAIR), axis=1)
 
-    def visit(j, masked, last):
+    def visit(j, last):
         at = pl.multiple_of(i * bq if last else j * bk, bk)
         streams = [(c, h) for c in range(0, bq, sub) for h in range(2)]
 
@@ -235,12 +238,12 @@
             rows = slice(c, c + sub)
             lanes = slice(h * HEAD, (h + 1) * HEAD)
             probs = jnp.exp(raw - wide(lse[h][rows], size))
-            if masked:
-                begin = jnp.broadcast_to(start[:, rows], (PAIR, sub)).T
-                key_index = at + lax.broadcasted_iota(jnp.int32, (sub, size), 1)
-                query_index = i * bq + c + lax.broadcasted_iota(jnp.int32, (sub, size), 0)
-                allowed = (key_index >= wide(begin, size)) & (key_index <= query_index)
-                probs = jnp.where(allowed, probs, 0.0)
+            key_index = lax.broadcasted_iota(jnp.int32, (sub, size), 1)
+            allowed = key_index >= wide(begin[rows], size) - at
+            if last:
+                query_index = c + lax.broadcasted_iota(jnp.int32, (sub, size), 0)
+                allowed = allowed & (key_index <= query_index)
+            probs = jnp.where(allowed, probs, 0.0)
             d_scores = (probs * (d_probs - wide(inner[rows, h * PAIR:(h + 1) * PAIR], size))).astype(BF16)
             dvt_acc[lanes, where] += mm(cout_t[lanes, rows], probs.astype(BF16))
             dkt_acc[lanes, where] += mm(query_t[lanes, rows], d_scores)
@@ -253,18 +256,11 @@
                 ready = scores(n + 1)
             absorb(n, held)
 
-    low = sched[2 + i]
-    mid = jnp.minimum(sched[2 + blocks + i], i * (bq // bk))
-
-    @pl.loop(low, mid)
+    @pl.loop(sched[2 + blocks + i], i * (bq // bk))
     def _(j):
-        visit(j, True, False)
-
-    @pl.loop(jnp.maximum(low, mid), i * (bq // bk))
-    def _(j):
-        visit(j, False, False)
-
-    visit(None, True, True)
+        visit(j, False)
+
+    visit(None, True)
 
     def unrotate(g, cosine, sine):
         return g * cosine - swap_halves(g) * sine
@@ -328,7 +324,7 @@
 
 def feed_kernel(sched, x_ref, own_ref, oth_ref, dy_ref, w_hbm, ga_ref, gf_ref,
                 out_ref, dfirst_ref, gown_ref, goth_ref, grads_ref, gains_ref,
-                w_ref, keep_a, keep_b, hidden_s, dgate_s, dup_s, normed_s, dffn_s, dattn_s, mixed_s,
+                w_ref, keep_a, keep_b, total_s, right_s, left_s, dattn_s, mixed_s,
                 sems, *, block, sub, chunk, local, hid, head_cols, parts, share):
     step = pl.program_id(0)
     me = sched[0]
@@ -353,15 +349,12 @@
         def _():
             piece(n).wait()
 
-    chunks = [(t, c) for t in range(2) for c in range(0, hid, chunk)]
-
     @pl.when(step < steps)
     def _():
         subs = list(range(0, block, sub))
         base = pl.multiple_of(step * block, block)
         arrive(0)
-        first, rms1, unit1, normed, normed_b, ffn = {}, {}, {}, {}, {}, {}
-        attn = {}
+        attn, rms1, unit1, normed, normed_b = {}, {}, {}, {}, {}
         for r in subs:
             rows = slice(r, r + sub)
             attn[r] = rdot(own_ref[rows, :], w_ref[me, :, outs]) + rdot(oth_ref[rows, :], w_ref[1 - me, :, outs])
@@ -373,37 +366,38 @@
             unit1[r] = first * rms1[r]
             normed[r] = unit1[r] * ga_ref[...]
             normed_b[r] = normed[r].astype(BF16)
-            normed_s[here, :] = normed_b[r]
+            left_s[0, here, :] = normed_b[r]
             mixed_s[here, :] = jnp.concatenate([own_ref[rows, :], oth_ref[rows, :]], axis=1)
-        for n, (t, c) in enumerate(chunks):
-            if n == 0:
-                arrive(1)
-            if t == 1 and c == 0:
-                arrive(2)
-            at = t * hid + c
-            cols = slice(at, at + chunk)
-            hid_b = {}
-            for r in subs:
-                rows = slice(r, r + sub)
-                here = pl.ds(base + r, sub)
-                gate = mm(normed_b[r], w_ref[t, :, c:c + chunk])
-                upper = mm(normed_b[r], w_ref[t, :, hid + c:hid + c + chunk])
-                sigma = 1.0 / (1.0 + jnp.exp(-gate))
-                silu = gate * sigma
-                hid_b[r] = (silu * upper).astype(BF16)
-                keep_a[rows, cols] = silu
-                keep_b[rows, cols] = upper * (sigma + silu * (1.0 - sigma))
-                hidden_s[here, cols] = hid_b[r]
-            if n == 0:
-                arrive(3)
-            for r in subs:
-                part = rdot(hid_b[r], w_ref[t, :, 2 * hid + c:2 * hid + c + chunk])
-                ffn[r] = part if n == 0 else ffn[r] + part
-        d_second, d_ffn, dn = {}, {}, {}
+        total_s[...] = jnp.zeros_like(total_s)
+
+        @pl.loop(0, 2)
+        def _(t):
+            for at, count in ((0, 1), (0, 3), (1, 2)):
+                @pl.when((step == 0) & (t == at))
+                def _():
+                    piece(count).wait()
+
+            for c in range(0, hid, chunk):
+                cols = pl.ds(pl.multiple_of(t * hid + c, chunk), chunk)
+                hid_b = {}
+                for r in subs:
+                    rows = slice(r, r + sub)
+                    gate = mm(normed_b[r], w_ref[t, :, c:c + chunk])
+                    upper = mm(normed_b[r], w_ref[t, :, hid + c:hid + c + chunk])
+                    sigma = 1.0 / (1.0 + jnp.exp(-gate))
+                    silu = gate * sigma
+                    hid_b[r] = (silu * upper).astype(BF16)
+                    keep_a[rows, cols] = silu
+                    keep_b[rows, cols] = upper * (sigma + silu * (1.0 - sigma))
+                    right_s[2, pl.ds(base + r, sub), cols] = hid_b[r]
+                for r in subs:
+                    total_s[r:r + sub, :] += rdot(hid_b[r], w_ref[t, :, 2 * hid + c:2 * hid + c + chunk])
+
+        d_second, d_ffn = {}, {}
         for r in subs:
             rows = slice(r, r + sub)
             here = pl.ds(base + r, sub)
-            second = normed[r] + ffn[r]
+            second = normed[r] + total_s[rows, :]
             rms2 = lax.rsqrt(jnp.mean(second * second, axis=-1, keepdims=True) + EPS)
             unit2 = second * rms2
             slot = me * local + base + r + lax.broadcasted_iota(jnp.int32, (sub, 1), 0)
@@ -414,27 +408,31 @@
             scaled = dy * gf_ref[...]
             d_second[r] = rms2 * (scaled - unit2 * jnp.mean(scaled * unit2, axis=-1, keepdims=True))
             d_ffn[r] = d_second[r].astype(BF16)
-            dffn_s[here, :] = d_ffn[r]
-            dn[r] = d_second[r]
-        for t, c in chunks:
-            at = t * hid + c
-            cols = slice(at, at + chunk)
-            dg, du = {}, {}
-            for r in subs:
-                rows = slice(r, r + sub)
-                here = pl.ds(base + r, sub)
-                d_hidden = mm(d_ffn[r], w_ref[t, :, 2 * hid + c:2 * hid + c + chunk])
-                dg[r] = (d_hidden * keep_b[rows, cols]).astype(BF16)
-                du[r] = (d_hidden * keep_a[rows, cols]).astype(BF16)
-                dgate_s[here, cols] = dg[r]
-                dup_s[here, cols] = du[r]
-            for r in subs:
-                dn[r] = dn[r] + rdot(dg[r], w_ref[t, :, c:c + chunk]) + rdot(du[r], w_ref[t, :, hid + c:hid + c + chunk])
+            left_s[1, here, :] = d_ffn[r]
+            total_s[rows, :] = d_second[r]
+
+        @pl.loop(0, 2)
+        def _(t):
+            for c in range(0, hid, chunk):
+                cols = pl.ds(pl.multiple_of(t * hid + c, chunk), chunk)
+                dg, du = {}, {}
+                for r in subs:
+                    rows, here = slice(r, r + sub), pl.ds(base + r, sub)
+                    d_hidden = mm(d_ffn[r], w_ref[t, :, 2 * hid + c:2 * hid + c + chunk])
+                    dg[r] = (d_hidden * keep_b[rows, cols]).astype(BF16)
+                    du[r] = (d_hidden * keep_a[rows, cols]).astype(BF16)
+                    right_s[0, here, cols] = dg[r]
+                    right_s[1, here, cols] = du[r]
+                for r in subs:
+                    total_s[r:r + sub, :] += rdot(dg[r], w_ref[t, :, c:c + chunk]) + rdot(
+                        du[r], w_ref[t, :, hid + c:hid + c + chunk])
+
         for r in subs:
             rows = slice(r, r + sub)
             here = pl.ds(base + r, sub)
-            gains_ref[0:1, :] += jnp.sum(dn[r] * unit1[r], axis=0, keepdims=True)
-            scaled = dn[r] * ga_ref[...]
+            d_normed = total_s[rows, :]
+            gains_ref[0:1, :] += jnp.sum(d_normed * unit1[r], axis=0, keepdims=True)
+            scaled = d_normed * ga_ref[...]
             d_first = rms1[r] * (scaled - unit1[r] * jnp.mean(scaled * unit1[r], axis=-1, keepdims=True))
             dfirst_ref[rows, :] = d_first
             d_attn = d_first.astype(BF16)
@@ -449,17 +447,21 @@
         size = dattn_s.shape[1] // parts
         rows = pl.ds(pl.multiple_of(part * size, size), size)
         cols = pl.ds(pl.multiple_of(t * hid, hid), hid)
-        mixed = jnp.where(t == me, mixed_s[:, :head_cols], mixed_s[:, head_cols:])
-        for at, left, right in ((0, normed_s, dgate_s[:, cols]), (hid, normed_s, dup_s[:, cols]),
-                                (2 * hid, dffn_s, hidden_s[:, cols]), (3 * hid, dattn_s, mixed)):
-            value = tdot(left[:, rows], right).astype(BF16)
-            there = slice(at, at + right.shape[1])
+
+        def store(value, there):
             if share is None:
                 grads_ref[0, :, there] = value
             else:
                 near = grads_ref.shape[1]
                 for n in range(size // share):
                     grads_ref[0, n % near, n // near, :, there] = value[n * share:(n + 1) * share]
+
+        for n in range(3):
+            left = left_s[n // 2, :, rows]
+            store(tdot(left, right_s[n, :, cols]).astype(BF16), slice(n * hid, (n + 1) * hid))
+
+        mixed = jnp.where(t == me, mixed_s[:, :head_cols], mixed_s[:, head_cols:])
+        store(tdot(dattn_s[:, rows], mixed).astype(BF16), slice(3 * hid, 3 * hid + head_cols))
 
 
 def feed(sched, x, own, oth, dy, weights, gain_attn, gain_ffn, hid, share, near,
@@ -504,8 +506,9 @@
                        pl.BlockSpec((16, width), lambda s, sched: (0, 0))],
             scratch_shapes=[pltpu.VMEM(weights.shape, BF16)]
             + [pltpu.VMEM((block, 2 * hid), F32)] * 2
-            + [pltpu.VMEM((local, 2 * hid), BF16)] * 3
-            + [pltpu.VMEM((local, width), BF16)] * 3
+            + [pltpu.VMEM((block, width), F32)]
+            + [pltpu.VMEM((3, local, 2 * hid), BF16), pltpu.VMEM((2, local, width), BF16)]
+            + [pltpu.VMEM((local, width), BF16)]
             + [pltpu.VMEM((local, 2 * head_cols), BF16), pltpu.SemaphoreType.DMA((4,))],
         ),
         out_shape=[
@@ -668,11 +671,10 @@
     angle = position[:, None] * inverse[None, :]
     cosine = jnp.cos(angle)
     sine = jnp.where(lane[None, :] < HEAD // 2, -jnp.sin(angle), jnp.sin(angle))
-    block_begin = begins.reshape(blocks, bq)
     sched = jnp.concatenate([
         jnp.stack([me.astype(jnp.int32), ends[-1]]),
-        block_begin[:, 0] // bk,
-        (block_begin[:, -1] + bk - 1) // bk,
+        begins[::bq] // bk,
+        begins[::bq] // (bk // 2),
     ])
     start = begins.reshape(1, slots)
 
@@ -687,7 +689,7 @@
     reduced = lax.psum_scatter(reduced, "far", scatter_dimension=0, tiled=True)
     gains = gains[:2] + exchange(gains[:2])
     d_qkv, dw = attend_backward(sched, qkv, cosine, sine, start, lse, mixed_send, mixed_own,
-                                g_oth, g_own, tokens, other_x, bq, bk)
+                                g_oth, g_own, tokens, other_x, bq, bk // 2)
     dw, gains = lax.optimization_barrier((dw, gains))
     fore, back = bit_orders(count)
     for bit in fore[::-1]:

time: 312 us -> 301 us (0.965); the launches traced: 308 us -> 300 us
  Pallas kernels: 154 us -> 164 us
  starting transfers between devices: 30.7 us -> 22.4 us
  waiting for transfers between devices: 77.2 us -> 69.5 us
    pallas_call x1, Pallas kernels: 52.1 us -> 60.8 us  [attend_backward(): pl.pallas_call(partial(backward_kernel, bq=bq, bk=bk, sub=sub, blocks=blo...]
    ppermute x18, starting transfers between devices: 30 us -> 21.7 us  [flip(): return lax.ppermute(value, DP, [(at, at ^ 1 << bit) for at in range(count)])]
    pallas_call x1, Pallas kernels: 33.6 us -> 40.9 us  [attend_forward(): pl.pallas_call(partial(forward_kernel, bq=bq, bk=bk, sub=sub, chunk=chunk...]
    all_gather x1, waiting for transfers between devices: 9.38 us -> 2.31 us  [local(): feed_w = lax.all_gather(packed, ('tensor',) + DP, axis=0, tiled=True)]
    pallas_call x1, Pallas kernels: 56.3 us -> 49.9 us  [feed(): pl.pallas_call(partial(feed_kernel, block=block, sub=sub, chunk=chunk, lo...]
  transfers between devices with their start and end apart: 26 -> 26, of which waited for: 14 -> 15; matrix products, arithmetic and copies ran while one was open for 9% -> 9% of each run, Pallas kernels for 31% -> 37%
where the time goes in v3:
time: 301 us; the launch traced here: 300 us
  Pallas kernels  164 us (54%)
  waiting for transfers between devices  69.5 us (23%)
  starting transfers between devices  22.4 us (7%)
  other arithmetic  18.6 us (6%)
  between operations  14.2 us (5%)
  local copies, waits for them, and re-layouts  12 us (4%)
    ppermute x18, waiting for transfers between devices, flip(): return lax.ppermute(value, DP, [(at, at ^ 1 << bit) for at in range(count)])  61.5 us
    pallas_call x1, Pallas kernels, attend_backward(): pl.pallas_call(partial(backward_kernel, bq=bq, bk=bk, sub=sub, blocks=blo...  60.8 us
    pallas_call x1, Pallas kernels, feed(): pl.pallas_call(partial(feed_kernel, block=block, sub=sub, chunk=chunk, lo...  49.9 us
    pallas_call x1, Pallas kernels, attend_forward(): pl.pallas_call(partial(forward_kernel, bq=bq, bk=bk, sub=sub, chunk=chunk...  40.9 us
    ppermute x18, starting transfers between devices, flip(): return lax.ppermute(value, DP, [(at, at ^ 1 << bit) for at in range(count)])  21.7 us
    pallas_call x1, Pallas kernels, input_grads(): pl.pallas_call(partial(input_grad_kernel, half=half), grid_spec=pltpu.Pre...  10.4 us
  transfers between devices with their start and end apart: 26, of which 15 were waited for; matrix products, arithmetic and copies ran while one was open for 9% of the time, Pallas kernels for 37%

profile of v3, /device:TPU:0, one launch (start us, length us, event | category | flops | bytes accessed | tf_op | source)
XLA Modules:
  0.0 300.5 jit_solution(13255412850487127844)
XLA Ops:
  7.3 1.8 pad_maximum_fusion.3
  9.9 4.1 %collective-permute-start.1 = (bf16[1,48,1152]{2,1,0:T(8,128)(2,1)S(1)}, bf16[1,48,1152]{2,1,0:T(8,128)(2,1)S(1)}, u32[]{:S(2)}, u32[]{:S(2)}) collective-permute-start(bf16[1,48,1152]{2,1,0:T(8,128)(2,1)S(1)} %maximum_bitcast_fusion.2), channel_id=1, source_target_pairs={{0,16},{2,18},{4,20},{6,22},{8,24},{10,26},{12,28},{14,30},{16,0},... | collective-permute-start | bytes 331784 | tf_op jit(solution)/shard_map/ppermute | solution.py:593
  15.6 5.6 %negate_select_fusion = (f32[2048,128]{1,0:T(8,128)}, f32[2048,128]{1,0:T(8,128)}) fusion(f32[128]{0:T(128)S(1)} %fusion.27, f32[2048]{0:T(1024)S(1)} %subtract_convert_fusion, pred[128]{0:T(512)(128)(4,1)S(1)} %broadcast_compare_fusion), kind=kLoop, calls=%fused_computation.2 | loop fusion | flops 786432 | bytes 2105984 | tf_op jit(solution)/shard_map/jit(_where)/select_n | solution.py:673
  22.0 1.6 collective-permute-start.2
  23.7 11.5 %collective-permute-done.2 = bf16[2,1,48,1152]{3,2,0,1:T(8,128)(2,1)S(1)} collective-permute-done((bf16[2,1,48,1152]{3,2,0,1:T(8,128)(2,1)S(1)}, bf16[2,1,48,1152]{3,2,0,1:T(8,128)(2,1)S(1)}, u32[]{:S(2)}, u32[]{:S(2)}) %collective-permute-start.2) | collective-permute-done | bytes 221216 | tf_op jit(solution)/shard_map/ppermute | solution.py:593
  39.2 1.9 collective-permute-done.5
  41.2 1.8 collective-permute-start.6
  43.0 4.7 %collective-permute-done.3 = bf16[2,2,1,48,640]{4,3,1,0,2:T(8,128)(2,1)S(1)} collective-permute-done((bf16[2,2,1,48,640]{4,3,1,0,2:T(8,128)(2,1)S(1)}, bf16[2,2,1,48,640]{4,3,1,0,2:T(8,128)(2,1)S(1)}, u32[]{:S(2)}, u32[]{:S(2)}) %collective-permute-start.3) | collective-permute-done | bytes 245792 | tf_op jit(solution)/shard_map/ppermute | solution.py:593
  47.9 14.2 %collective-permute-done.6 = bf16[2,2,2,1,48,512]{5,4,2,1,0,3:T(8,128)(2,1)S(1)} collective-permute-done((bf16[2,2,2,1,48,512]{5,4,2,1,0,3:T(8,128)(2,1)S(1)}, bf16[2,2,2,1,48,512]{5,4,2,1,0,3:T(8,128)(2,1)S(1)}, u32[]{:S(2)}, u32[]{:S(2)}) %collective-permute-start.6) | collective-permute-done | bytes 393248 | tf_op jit(solution)/shard_map/ppermute | solution.py:593
  65.3 40.9 %attend_forward.1 = (bf16[2048,1152]{1,0:T(8,128)(2,1)}, bf16[1024,384]{1,0:T(8,128)(2,1)}, bf16[1024,384]{1,0:T(8,128)(2,1)}, f32[3,2,2048]{2,1,0:T(2,128)}) custom-call(s32[6]{0:T(128)} %pad_add_fusion.sched, bf16[1024,768]{1,0:T(8,128)(2,1)} %x_own_ref.1, bf16[1024,768]{1,0:T(8,128)(2,1)} %copy-done.7, ...), custom_call_target="tpu_custom_call" | custom-call | flops 10066329600 | bytes 12582912 | tf_op jit(solution)/shard_map/attend_forward/pallas_call | solution.py:156
  109.1 2.3 all-gather.2.cloned.1.call-done
  111.4 49.9 %feed.1 = (bf16[1024,768]{1,0:T(8,128)(2,1)}, f32[1024,768]{1,0:T(8,128)}, bf16[1024,384]{1,0:T(8,128)(2,1)}, bf16[1024,384]{1,0:T(8,128)(2,1)}, bf16[2,4,4,48,3...) custom-call(s32[6]{0:T(128)} %pad_add_fusion.sched, bf16[1024,768]{1,0:T(8,128)(2,1)} %x_own_ref.1, ...), custom_call_target="tpu_custom_call" | custom-call | flops 32614907904 | bytes 23592960 | tf_op jit(solution)/shard_map/feed/pallas_call | solution.py:497
  166.4 60.8 %attend_backward.1 = (bf16[2048,1152]{1,0:T(8,128)(2,1)}, bf16[768,1152]{1,0:T(8,128)(2,1)}) custom-call(s32[6]{0:T(128)} %pad_add_fusion.sched, bf16[2048,1152]{1,0:T(8,128)(2,1)} %get-tuple-element.34.q_ref.k_ref.v_ref, bf16[2048,1152]{1,0:T(8,128)(2,1)} %get-tuple-element.34.q_ref.k_ref.v_ref, bf16[2048,1152]{1,0:T(8,128)(2,1)} %get-tuple-element.34.q_ref.k_ref.v_ref, ...), custom_call_target="tpu_custom_call" | custom-call | flops 19730006016 | bytes 15728640 | tf_op jit(solution)/shard_map/attend_backward/pallas_call | solution.py:294
  231.4 1.7 collective-permute-start.15
  238.4 1.8 collective-permute-start.22
  240.2 10.4 %input_grads.1 = (bf16[1024,768]{1,0:T(8,128)(2,1)}, f32[1024,768]{1,0:T(8,128)}) custom-call(s32[6]{0:T(128)} %pad_add_fusion.sched, bf16[2048,1152]{1,0:T(8,128)(2,1)} %get-tuple-element.38.d_ref, bf16[768,1152]{1,0:T(8,128)(2,1)} %pad_maximum_fusion.wq_ref.wk_ref.wv_ref.w_ref, f32[1024,768]{1,0:T(8,128)} %get-tuple-element.39.dfirst_ref), custom_call_target="tpu_custom_call" | custom-call | flops 3623878656 | bytes 7864320 | tf_op jit(solution)/shard_map/input_grads/pallas_call | solution.py:550
  253.1 5.0 %collective-permute-done.16 = bf16[2,2,48,512]{3,2,1,0:T(8,128)(2,1)S(1)} collective-permute-done((bf16[2,2,48,512]{3,2,1,0:T(8,128)(2,1)S(1)}, bf16[2,2,48,512]{3,2,1,0:T(8,128)(2,1)S(1)}, u32[]{:S(2)}, u32[]{:S(2)}) %collective-permute-start.16) | collective-permute-done | bytes 196640 | tf_op jit(solution)/shard_map/ppermute | solution.py:593
  258.9 4.0 %collective-permute-done.17 = bf16[2,48,512]{2,1,0:T(8,128)(2,1)S(1)} collective-permute-done((bf16[2,48,512]{2,1,0:T(8,128)(2,1)S(1)}, bf16[2,48,512]{2,1,0:T(8,128)(2,1)S(1)}, u32[]{:S(2)}, u32[]{:S(2)}) %collective-permute-start.17) | collective-permute-done | bytes 98336 | tf_op jit(solution)/shard_map/ppermute | solution.py:593
  263.3 2.5 collective-permute-start.18
  265.8 7.4 %collective-permute-done.13 = bf16[2,48,640]{2,1,0:T(8,128)(2,1)S(1)} collective-permute-done((bf16[2,48,640]{2,1,0:T(8,128)(2,1)S(1)}, bf16[2,48,640]{2,1,0:T(8,128)(2,1)S(1)}, u32[]{:S(2)}, u32[]{:S(2)}) %collective-permute-start.13) | collective-permute-done | bytes 122912 | tf_op jit(solution)/shard_map/ppermute | solution.py:593
  273.4 9.1 %collective-permute-done.14 = bf16[48,640]{1,0:T(8,128)(2,1)S(1)} collective-permute-done((bf16[48,640]{1,0:T(8,128)(2,1)S(1)}, bf16[48,640]{1,0:T(8,128)(2,1)S(1)}, u32[]{:S(2)}, u32[]{:S(2)}) %collective-permute-start.14) | collective-permute-done | bytes 61472 | tf_op jit(solution)/shard_map/ppermute | solution.py:593
  286.2 2.9 add_convert_fusion
  289.1 3.1 %reduce-scatter.5.cloned.1.call-done.total_ref = bf16[48,3456]{1,0:T(8,128)(2,1)} async-done(((bf16[192,3456]{1,0:T(8,128)(2,1)}), bf16[48,3456]{1,0:T(8,128)(2,1)}) %reduce-scatter.5.cloned.1.call-update) | async-done | bytes 331792 | tf_op jit(solution)/shard_map/reduce_scatter | solution.py:689
  292.1 1.8 finish.1
  (125 shorter events, 35.6 us)
Async XLA Ops:
  7.2 104.2 %all-gather.2.cloned.1.call-start = ((), (), s32[]{:S(2)}) async-start(), calls=%async_computation.2 | async-start | bytes 10948608 | tf_op jit(solution)/shard_map/all_gather | solution.py:659
  9.0 249.9 %reduce-scatter.3.cloned.1.call-start = ((), (), s32[]{:S(2)}) async-start(), calls=%async_computation.3 | async-start | bytes 11943936 | tf_op jit(solution)/shard_map/reduce_scatter | solution.py:688
  9.9 12.0 %collective-permute-start.1 = (bf16[1,48,1152]{2,1,0:T(8,128)(2,1)S(1)}, bf16[1,48,1152]{2,1,0:T(8,128)(2,1)S(1)}, u32[]{:S(2)}, u32[]{:S(2)}) collective-permute-start(bf16[1,48,1152]{2,1,0:T(8,128)(2,1)S(1)} %maximum_bitcast_fusion.2), channel_id=1, source_target_pairs={{0,16},{2,18},{4,20},{6,22},{8,24},{10,26},{12,28},{14,30},{16,0},... | collective-permute-start | bytes 331784 | tf_op jit(solution)/shard_map/ppermute | solution.py:593
  14.0 50.2 %collective-permute-start = (bf16[1024,768]{1,0:T(8,128)(2,1)}, bf16[1024,768]{1,0:T(8,128)(2,1)S(1)}, u32[]{:S(2)}, u32[]{:S(2)}) collective-permute-start(bf16[1024,768]{1,0:T(8,128)(2,1)} %x_own_ref.1), channel_id=1, source_target_pairs={{0,1},{1,0},{2,3},{3,2},{4,5},{5,4},{6,7},{7,6},{8,9},{9,8},{10,11... | collective-permute-start | bytes 4718600 | tf_op jit(solution)/shard_map/ppermute | solution.py:588
  22.0 13.2 %collective-permute-start.2 = (bf16[2,1,48,1152]{3,2,0,1:T(8,128)(2,1)S(1)}, bf16[2,1,48,1152]{3,2,0,1:T(8,128)(2,1)S(1)}, u32[]{:S(2)}, u32[]{:S(2)}) collective-permute-start(bf16[2,1,48,1152]{3,2,0,1:T(8,128)(2,1)S(1)} %fusion.16), channel_id=1, source_target_pairs={{0,8},{2,10},{4,12},{6,14},{8,0},{10,2},{12,4},{14,6},{16,24},{18,... | collective-permute-start | bytes 663560 | tf_op jit(solution)/shard_map/ppermute | solution.py:593
  35.3 5.7 %collective-permute-start.5 = (bf16[2,2,1,48,512]{4,3,1,0,2:T(8,128)(2,1)S(1)}, bf16[2,2,1,48,512]{4,3,1,0,2:T(8,128)(2,1)S(1)}, u32[]{:S(2)}, u32[]{:S(2)}) collective-permute-start(bf16[2,2,1,48,512]{4,3,1,0,2:T(8,128)(2,1)S(1)} %fusion.23), channel_id=1, source_target_pairs={{0,4},{2,6},{4,0},{6,2},{8,12},{10,14},{12,8},{14,10},{16,20},{18,... | collective-permute-start | bytes 589832 | tf_op jit(solution)/shard_map/ppermute | solution.py:593
  37.8 9.9 %collective-permute-start.3 = (bf16[2,2,1,48,640]{4,3,1,0,2:T(8,128)(2,1)S(1)}, bf16[2,2,1,48,640]{4,3,1,0,2:T(8,128)(2,1)S(1)}, u32[]{:S(2)}, u32[]{:S(2)}) collective-permute-start(bf16[2,2,1,48,640]{4,3,1,0,2:T(8,128)(2,1)S(1)} %fusion.29), channel_id=1, source_target_pairs={{0,2},{2,0},{4,6},{6,4},{8,10},{10,8},{12,14},{14,12},{16,18},{18,... | collective-permute-start | bytes 737288 | tf_op jit(solution)/shard_map/ppermute | solution.py:593
  41.2 20.9 %collective-permute-start.6 = (bf16[2,2,2,1,48,512]{5,4,2,1,0,3:T(8,128)(2,1)S(1)}, bf16[2,2,2,1,48,512]{5,4,2,1,0,3:T(8,128)(2,1)S(1)}, u32[]{:S(2)}, u32[]{:S(2)}) collective-permute-start(bf16[2,2,2,1,48,512]{5,4,2,1,0,3:T(8,128)(2,1)S(1)} %fusion.7), channel_id=1, source_target_pairs={{0,2},{2,0},{4,6},{6,4},{8,10},{10,8},{12,14},{14,12},{16,18},{18,... | collective-permute-start | bytes 1179656 | tf_op jit(solution)/shard_map/ppermute | solution.py:593
  47.8 14.6 %collective-permute-start.4 = (bf16[2,2,2,1,48,640]{5,4,2,1,0,3:T(8,128)(2,1)S(1)}, bf16[2,2,2,1,48,640]{5,4,2,1,0,3:T(8,128)(2,1)S(1)}, u32[]{:S(2)}, u32[]{:S(2)}) collective-permute-start(bf16[2,2,2,1,48,640]{5,4,2,1,0,3:T(8,128)(2,1)S(1)} %fusion.6), channel_id=1, source_target_pairs={{0,4},{2,6},{4,0},{6,2},{8,12},{10,14},{12,8},{14,10},{16,20},{18,... | collective-permute-start | bytes 1474568 | tf_op jit(solution)/shard_map/ppermute | solution.py:593
  161.3 130.8 %reduce-scatter.5.cloned.1.call-start = ((), (), s32[]{:S(2)}) async-start(), calls=%async_computation.4 | async-start | bytes 1658880 | tf_op jit(solution)/shard_map/reduce_scatter | solution.py:689
  162.4 3.1 %collective-permute-start.8 = (bf16[1024,384]{1,0:T(8,128)(2,1)S(1)}, bf16[1024,384]{1,0:T(8,128)(2,1)S(1)}, u32[]{:S(2)}, u32[]{:S(2)}) collective-permute-start(bf16[1024,384]{1,0:T(8,128)(2,1)S(1)} %copy-done.8), channel_id=1, source_target_pairs={{0,1},{1,0},{2,3},{3,2},{4,5},{5,4},{6,7},{7,6},{8,9},{9,8},{10,11... | collective-permute-start | bytes 2359304 | tf_op jit(solution)/shard_map/ppermute | solution.py:588
  227.2 3.8 %collective-permute-start.19 = (f32[2,768]{1,0:T(2,128)S(1)}, f32[2,768]{1,0:T(2,128)S(1)}, u32[]{:S(2)}, u32[]{:S(2)}) collective-permute-start(f32[2,768]{1,0:T(2,128)S(1)} %slice_add_fusion), channel_id=1, source_target_pairs={{0,4},{2,6},{4,0},{6,2},{8,12},{10,14},{12,8},{14,10},{16,20},{18,... | collective-permute-start | bytes 18440 | tf_op jit(solution)/shard_map/ppermute | solution.py:593
  231.0 3.8 %collective-permute-start.20 = (f32[2,768]{1,0:T(2,128)S(1)}, f32[2,768]{1,0:T(2,128)S(1)}, u32[]{:S(2)}, u32[]{:S(2)}) collective-permute-start(f32[2,768]{1,0:T(2,128)S(1)} %add.94), channel_id=1, source_target_pairs={{0,2},{2,0},{4,6},{6,4},{8,10},{10,8},{12,14},{14,12},{16,18},{18,... | collective-permute-start | bytes 18440 | tf_op jit(solution)/shard_map/ppermute | solution.py:593
  231.4 19.2 %collective-permute-start.15 = (bf16[2,2,2,48,512]{4,3,2,1,0:T(8,128)(2,1)S(1)}, bf16[2,2,2,48,512]{4,3,2,1,0:T(8,128)(2,1)S(1)}, u32[]{:S(2)}, u32[]{:S(2)}) collective-permute-start(bf16[2,2,2,48,512]{4,3,2,1,0:T(8,128)(2,1)S(1)} %select_bitcast_fusion.2), channel_id=1, source_target_pairs={{0,2},{2,0},{4,6},{6,4},{8,10},{10,8},{12,14},{14,12},{16,18},{18,... | collective-permute-start | bytes 1179656 | tf_op jit(solution)/shard_map/ppermute | solution.py:593
  234.7 3.6 %collective-permute-start.21 = (f32[2,768]{1,0:T(2,128)S(1)}, f32[2,768]{1,0:T(2,128)S(1)}, u32[]{:S(2)}, u32[]{:S(2)}) collective-permute-start(f32[2,768]{1,0:T(2,128)S(1)} %add.95), channel_id=1, source_target_pairs={{0,8},{2,10},{4,12},{6,14},{8,0},{10,2},{12,4},{14,6},{16,24},{18,... | collective-permute-start | bytes 18440 | tf_op jit(solution)/shard_map/ppermute | solution.py:593
  236.3 15.6 %collective-permute-start.11 = (bf16[2,2,2,48,640]{4,3,1,0,2:T(8,128)(2,1)S(1)}, bf16[2,2,2,48,640]{4,3,1,0,2:T(8,128)(2,1)S(1)}, u32[]{:S(2)}, u32[]{:S(2)}) collective-permute-start(bf16[2,2,2,48,640]{4,3,1,0,2:T(8,128)(2,1)S(1)} %select_bitcast_fusion), channel_id=1, source_target_pairs={{0,4},{2,6},{4,0},{6,2},{8,12},{10,14},{12,8},{14,10},{16,20},{18,... | collective-permute-start | bytes 1474568 | tf_op jit(solution)/shard_map/ppermute | solution.py:593
  238.4 12.2 %collective-permute-start.22 = (f32[2,768]{1,0:T(2,128)S(1)}, f32[2,768]{1,0:T(2,128)S(1)}, u32[]{:S(2)}, u32[]{:S(2)}) collective-permute-start(f32[2,768]{1,0:T(2,128)S(1)} %add.96), channel_id=1, source_target_pairs={{0,16},{2,18},{4,20},{6,22},{8,24},{10,26},{12,28},{14,30},{16,0},... | collective-permute-start | bytes 18440 | tf_op jit(solution)/shard_map/ppermute | solution.py:593
  250.5 35.6 %collective-permute-start.9 = (bf16[1024,768]{1,0:T(8,128)(2,1)}, bf16[1024,768]{1,0:T(8,128)(2,1)}, u32[]{:S(2)}, u32[]{:S(2)}) collective-permute-start(bf16[1024,768]{1,0:T(8,128)(2,1)} %get-tuple-element.41), channel_id=1, source_target_pairs={{0,1},{1,0},{2,3},{3,2},{4,5},{5,4},{6,7},{7,6},{8,9},{9,8},{10,11... | collective-permute-start | bytes 4718600 | tf_op jit(solution)/shard_map/ppermute | solution.py:588
  250.8 7.4 %collective-permute-start.16 = (bf16[2,2,48,512]{3,2,1,0:T(8,128)(2,1)S(1)}, bf16[2,2,48,512]{3,2,1,0:T(8,128)(2,1)S(1)}, u32[]{:S(2)}, u32[]{:S(2)}) collective-permute-start(bf16[2,2,48,512]{3,2,1,0:T(8,128)(2,1)S(1)} %fusion.13), channel_id=1, source_target_pairs={{0,4},{2,6},{4,0},{6,2},{8,12},{10,14},{12,8},{14,10},{16,20},{18,... | collective-permute-start | bytes 589832 | tf_op jit(solution)/shard_map/ppermute | solution.py:593
  252.1 10.8 %collective-permute-start.12 = (bf16[2,2,48,640]{3,2,1,0:T(8,128)(2,1)S(1)}, bf16[2,2,48,640]{3,2,1,0:T(8,128)(2,1)S(1)}, u32[]{:S(2)}, u32[]{:S(2)}) collective-permute-start(bf16[2,2,48,640]{3,2,1,0:T(8,128)(2,1)S(1)} %select_bitcast_fusion.4), channel_id=1, source_target_pairs={{0,2},{2,0},{4,6},{6,4},{8,10},{10,8},{12,14},{14,12},{16,18},{18,... | collective-permute-start | bytes 737288 | tf_op jit(solution)/shard_map/ppermute | solution.py:593
  258.2 4.7 %collective-permute-start.17 = (bf16[2,48,512]{2,1,0:T(8,128)(2,1)S(1)}, bf16[2,48,512]{2,1,0:T(8,128)(2,1)S(1)}, u32[]{:S(2)}, u32[]{:S(2)}) collective-permute-start(bf16[2,48,512]{2,1,0:T(8,128)(2,1)S(1)} %fusion.20), channel_id=1, source_target_pairs={{0,8},{2,10},{4,12},{6,14},{8,0},{10,2},{12,4},{14,6},{16,24},{18,... | collective-permute-start | bytes 294920 | tf_op jit(solution)/shard_map/ppermute | solution.py:593
  263.1 10.1 %collective-permute-start.13 = (bf16[2,48,640]{2,1,0:T(8,128)(2,1)S(1)}, bf16[2,48,640]{2,1,0:T(8,128)(2,1)S(1)}, u32[]{:S(2)}, u32[]{:S(2)}) collective-permute-start(bf16[2,48,640]{2,1,0:T(8,128)(2,1)S(1)} %fusion.17), channel_id=1, source_target_pairs={{0,8},{2,10},{4,12},{6,14},{8,0},{10,2},{12,4},{14,6},{16,24},{18,... | collective-permute-start | bytes 368648 | tf_op jit(solution)/shard_map/ppermute | solution.py:593
  263.3 10.1 %collective-permute-start.18 = (bf16[48,512]{1,0:T(8,128)(2,1)S(1)}, bf16[48,512]{1,0:T(8,128)(2,1)S(1)}, u32[]{:S(2)}, u32[]{:S(2)}) collective-permute-start(bf16[48,512]{1,0:T(8,128)(2,1)S(1)} %select_bitcast_fusion.11), channel_id=1, source_target_pairs={{0,16},{2,18},{4,20},{6,22},{8,24},{10,26},{12,28},{14,30},{16,0},... | collective-permute-start | bytes 147464 | tf_op jit(solution)/shard_map/ppermute | solution.py:593
  273.3 9.2 %collective-permute-start.14 = (bf16[48,640]{1,0:T(8,128)(2,1)S(1)}, bf16[48,640]{1,0:T(8,128)(2,1)S(1)}, u32[]{:S(2)}, u32[]{:S(2)}) collective-permute-start(bf16[48,640]{1,0:T(8,128)(2,1)S(1)} %select_bitcast_fusion.10), channel_id=1, source_target_pairs={{0,16},{2,18},{4,20},{6,22},{8,24},{10,26},{12,28},{14,30},{16,0},... | collective-permute-start | bytes 184328 | tf_op jit(solution)/shard_map/ppermute | solution.py:593
  (13 other events, 179.2 us)
Sparse Core Ops, SparseCore 0:
  11.5 99.8 all-gather.1
  161.4 87.2 reduce-scatter.2
  259.1 33.0 reduce-scatter.4

commit v4 on v3

--- a/solution.py
+++ b/solution.py
@@ -17,6 +17,8 @@
 BF16 = jnp.bfloat16
 VMEM_LIMIT = 56 * 1024 * 1024
 DP = ("far", "near")
+EXTRA = 16
+SIDE, TOTAL, BIT_X, BIT_Y, FAR, LOWS = range(6)
 
 
 def mm(left, right):
@@ -118,7 +120,7 @@
             return tuple(out)
 
         carry = (jnp.full((1, sub), NEGATIVE, F32), jnp.zeros((1, sub), F32)) * len(streams)
-        carry = lax.fori_loop(sched[2 + i], i * (bq // bk), lambda j, c: visit(j, c, False), carry)
+        carry = lax.fori_loop(sched[LOWS + i], i * (bq // bk), lambda j, c: visit(j, c, False), carry)
         carry = visit(None, carry, True)
         for n, c in enumerate(streams):
             peak, total = carry[2 * n], carry[2 * n + 1]
@@ -188,10 +190,12 @@
 
 def backward_kernel(sched, q_ref, k_ref, v_ref, cos_ref, sin_ref, start_ref, lse_ref,
                     o_oth_ref, o_own_ref, g_oth_ref, g_own_ref, x_own_ref, x_oth_ref,
-                    all_ref, dw_ref, dq_acc, dkt_acc, dvt_acc, *, bq, bk, sub, blocks):
+                    gains_ref, all_ref, *rest, bq, bk, sub, blocks, share):
     step = pl.program_id(1)
     half = blocks // 2
     i = lax.rem(step + (1 - sched[0]) * half, blocks)
+
+    dw_refs, (dq_acc, dkt_acc, dvt_acc) = rest[:-3], rest[-3:]
 
     @pl.when(step == 0)
     def _():
@@ -256,7 +260,7 @@
                 ready = scores(n + 1)
             absorb(n, held)
 
-    @pl.loop(sched[2 + blocks + i], i * (bq // bk))
+    @pl.loop(sched[LOWS + blocks + i], i * (bq // bk))
     def _(j):
         visit(j, False)
 
@@ -276,13 +280,49 @@
         all_ref[:, 2 * PAIR:] = dvt_acc[...].T.astype(BF16)
         local = x_own_ref.shape[0]
         mine = pl.ds(pl.multiple_of(sched[0] * local, local), local)
-        rest = pl.ds(pl.multiple_of((1 - sched[0]) * local, local), local)
-        dw_ref[...] = (tdot(x_own_ref[...], all_ref[mine, :])
-                       + tdot(x_oth_ref[...], all_ref[rest, :])).astype(BF16)
+        other = pl.ds(pl.multiple_of((1 - sched[0]) * local, local), local)
+        total = (tdot(x_own_ref[...], all_ref[mine, :])
+                 + tdot(x_oth_ref[...], all_ref[other, :])).astype(BF16)
+        if share is None:
+            dw_refs[0][...] = total
+        else:
+            part_rows(total, gains_ref[...], sched[BIT_X], sched[BIT_Y], *dw_refs, share)
+
+
+def encode(value):
+    high = value.astype(BF16)
+    rest = value - high.astype(F32)
+    middle = rest.astype(BF16)
+    low = (rest - middle.astype(F32)).astype(BF16)
+    rows, cols = value.shape
+    pieces = [piece.astype(F32) for piece in (high, middle, low)]
+    return jnp.concatenate(pieces + [jnp.zeros((EXTRA - 3 * rows, cols), F32)], axis=0).astype(BF16)
+
+
+def decode(rows, count=2):
+    wide = rows.astype(F32)
+    return wide[0:count] + wide[count:2 * count] + wide[2 * count:3 * count]
+
+
+def part_rows(total, gains, bit_x, bit_y, keep_a, send_a, keep_b, send_b, share):
+    def block(z, y, x):
+        at = (4 * z + 2 * y + x) * share
+        return total[at:at + share]
+
+    pieces = keep_a.shape[0] // share
+    for n in range(pieces):
+        z, side, here = 2 * (n // 2), n % 2, slice(n * share, (n + 1) * share)
+        zero, one = block(z, side, 0), block(z, side, 1)
+        keep_a[here] = jnp.where(bit_x == 0, zero, one)
+        send_a[here] = jnp.where(bit_x == 0, one, zero)
+        zero, one = block(z + 1, 0, side), block(z + 1, 1, side)
+        keep_b[here] = jnp.where(bit_y == 0, zero, one)
+        send_b[here] = jnp.where(bit_y == 0, one, zero)
+    send_a[pieces * share:] = encode(gains)
 
 
 def attend_backward(sched, qkv, cosine, sine, start, lse, o_oth, o_own, g_oth, g_own, x_own, x_oth,
-                    bq, bk, sub=256):
+                    gains, bq, bk, share, sub=256):
     slots, cols = qkv.shape[0], qkv.shape[1] // 3
     pairs, blocks = cols // PAIR, slots // bq
     local, width = x_own.shape
@@ -291,8 +331,15 @@
     rows = pl.BlockSpec((local, width), lambda p, n, s: (0, 0), pipeline_mode=pl.Buffered(1))
     oth = pl.BlockSpec((bq, PAIR), lambda p, n, s: (jnp.minimum(n, half - 1), p))
     own = pl.BlockSpec((bq, PAIR), lambda p, n, s: (jnp.maximum(n - half, 0), p))
+    if share is None:
+        dw_specs = [pl.BlockSpec((width, 3 * PAIR), lambda p, n, s: (0, p))]
+        dw_shapes = [(width, 3 * cols)]
+    else:
+        rows_out = [width // 4, width // 4 + EXTRA, width // 4, width // 4]
+        dw_specs = [pl.BlockSpec((size, 3 * PAIR), lambda p, n, s: (0, p)) for size in rows_out]
+        dw_shapes = [(size, 3 * cols) for size in rows_out]
     return pl.pallas_call(
-        partial(backward_kernel, bq=bq, bk=bk, sub=sub, blocks=blocks),
+        partial(backward_kernel, bq=bq, bk=bk, sub=sub, blocks=blocks, share=share),
         grid_spec=pltpu.PrefetchScalarGridSpec(
             num_scalar_prefetch=1,
             grid=(pairs, blocks),
@@ -304,22 +351,21 @@
                 pl.BlockSpec((1, bq), lambda p, n, s: (0, place(n, s))),
                 pl.BlockSpec((None, 2, bq), lambda p, n, s: (p, 0, place(n, s))),
                 oth, own, oth, own, rows, rows,
+                pl.BlockSpec((2, 3 * PAIR), lambda p, n, s: (0, p)),
             ],
-            out_specs=[pl.BlockSpec((slots, 3 * PAIR), lambda p, n, s: (0, p)),
-                       pl.BlockSpec((width, 3 * PAIR), lambda p, n, s: (0, p))],
+            out_specs=[pl.BlockSpec((slots, 3 * PAIR), lambda p, n, s: (0, p)), *dw_specs],
             scratch_shapes=[
                 pltpu.VMEM((bq, PAIR), F32),
                 pltpu.VMEM((PAIR, slots), F32),
                 pltpu.VMEM((PAIR, slots), F32),
             ],
         ),
-        out_shape=[jax.ShapeDtypeStruct((slots, 3 * cols), BF16),
-                   jax.ShapeDtypeStruct((width, 3 * cols), BF16)],
+        out_shape=[jax.ShapeDtypeStruct(shape, BF16) for shape in [(slots, 3 * cols), *dw_shapes]],
         compiler_params=params(dims=2),
         cost_estimate=cost(10 * slots * slots * cols + 6 * slots * width * cols,
                            20 * slots * cols, slots * slots * 6),
         name="attend_backward",
-    )(sched, qkv, qkv, qkv, cosine, sine, start, lse, o_oth, o_own, g_oth, g_own, x_own, x_oth)
+    )(sched, qkv, qkv, qkv, cosine, sine, start, lse, o_oth, o_own, g_oth, g_own, x_own, x_oth, gains)
 
 
 def feed_kernel(sched, x_ref, own_ref, oth_ref, dy_ref, w_hbm, ga_ref, gf_ref,
@@ -584,6 +630,103 @@
     return gate, up, down.T, out.T
 
 
+def whole_call(kernel, name, sched, values, shapes):
+    whole = pl.BlockSpec(memory_space=pltpu.VMEM)
+    size = 4 * sum(value.size for value in values)
+    return pl.pallas_call(
+        kernel,
+        in_specs=[pl.BlockSpec(memory_space=pltpu.SMEM)] + [whole] * len(values),
+        out_specs=[whole] * len(shapes),
+        out_shape=[jax.ShapeDtypeStruct(shape, dtype) for shape, dtype in shapes],
+        compiler_params=pltpu.CompilerParams(vmem_limit_bytes=32 * 1024 * 1024),
+        cost_estimate=cost(0, size),
+        name=name,
+    )(sched, *values)
+
+
+def add(left, right):
+    return left.astype(F32) + right.astype(F32)
+
+
+def near_kernel(sched, keep_a, got_a, keep_b, got_b, gains, next_a, send_a, next_b, send_b, total,
+                *, share):
+    size = next_a.shape[0]
+    for held, got, bit, stay, go in ((keep_a, got_a, sched[BIT_Y], next_a, send_a),
+                                     (keep_b, got_b, sched[BIT_X], next_b, send_b)):
+        for n in range(size // share):
+            here = slice(n * share, (n + 1) * share)
+            mine = pl.ds(pl.multiple_of((2 * n + bit) * share, share), share)
+            other = pl.ds(pl.multiple_of((2 * n + 1 - bit) * share, share), share)
+            stay[here] = add(held[mine], got[mine]).astype(BF16)
+            go[here] = add(held[other], got[other]).astype(BF16)
+    total[...] = gains[...] + decode(got_a[2 * size:])
+    send_a[size:] = encode(total[...])
+
+
+def far_kernel(sched, keep_a, got_a, keep_b, got_b, gains, own, total, *sends):
+    far, share = 1 + len(sends), own.shape[0]
+    sums = []
+    for n in range(far // 2):
+        here = slice(n * share, (n + 1) * share)
+        sums += [add(keep_a[here], got_a[here]), add(keep_b[here], got_b[here])]
+    total[...] = gains[...] + decode(got_a[keep_a.shape[0]:])
+    for shift in range(far):
+        at = lax.rem(sched[FAR] + shift, far)
+        value = sums[0]
+        for n in range(1, far):
+            value = jnp.where(at == n, sums[n], value)
+        if shift == 0:
+            own[...] = value
+        else:
+            sends[shift - 1][:share] = value.astype(BF16)
+            sends[shift - 1][share:] = encode(total[...])
+
+
+def last_kernel(sched, own, gains, *rest):
+    got, outs, total = rest[:-4], rest[-4:-1], rest[-1]
+    value, share, far = own[...], own.shape[0], 1 + len(rest[:-4])
+    arrived = [gains[...]]
+    for piece in got:
+        value = value + piece[:share].astype(F32)
+        arrived.append(decode(piece[share:]))
+    for at in range(0, value.shape[1], PAIR):
+        pair, part = at // PAIR // 3, at // PAIR % 3
+        outs[part][:, pair * PAIR:(pair + 1) * PAIR] = value[:, at:at + PAIR]
+    summed = None
+    for n in range(far):
+        shift = lax.rem(sched[FAR] - n + far, far)
+        term = arrived[0]
+        for k in range(1, far):
+            term = jnp.where(shift == k, arrived[k], term)
+        summed = term if summed is None else summed + term
+    total[...] = summed
+
+
+def shifted(value, shift):
+    far = lax.axis_size("far")
+    return lax.ppermute(value, "far", [(at, (at + shift) % far) for at in range(far)])
+
+
+def sum_parts(sched, share, keep_a, send_a, keep_b, send_b, gains, beside, late):
+    size, width = keep_a.shape
+    far = lax.axis_size("far")
+    send_a, send_b, beside, late = lax.optimization_barrier((send_a, send_b, beside, late))
+    got_a, got_b = flip(send_a, 0), flip(send_b, 1)
+    sizes = [size // 2, size // 2 + EXTRA, size // 2, size // 2]
+    keep_a, send_a, keep_b, send_b, gains = whole_call(
+        partial(near_kernel, share=share), "near_sums", sched,
+        (keep_a, got_a, keep_b, got_b, gains),
+        [((rows, width), BF16) for rows in sizes] + [(gains.shape, F32)])
+    got_a, got_b = flip(send_a, 1), flip(send_b, 0)
+    own, gains, *sends = whole_call(
+        far_kernel, "far_sums", sched, (keep_a, got_a, keep_b, got_b, gains),
+        [((share, width), F32), (gains.shape, F32)] + [((share + EXTRA, width), BF16)] * (far - 1))
+    got = [shifted(value, shift + 1) for shift, value in enumerate(sends)]
+    *dw, gains = whole_call(last_kernel, "last_sums", sched, (own, gains, *got),
+                            [((share, width // 3), F32)] * 3 + [(gains.shape, F32)])
+    return dw, gains, beside, late
+
+
 def exchange(value):
     return lax.ppermute(value, "tensor", [(0, 1), (1, 0)])
 
@@ -661,6 +804,7 @@
     full_qkv = gather_rows(jnp.concatenate([w_query, w_key, w_value], axis=1), edge)
     other_x = exchange(tokens)
 
+    near_at = lax.axis_index("near")
     index = jnp.arange(slots, dtype=jnp.int32)
     row = lengths[0]
     ends = jnp.cumsum(row)
@@ -672,7 +816,7 @@
     cosine = jnp.cos(angle)
     sine = jnp.where(lane[None, :] < HEAD // 2, -jnp.sin(angle), jnp.sin(angle))
     sched = jnp.concatenate([
-        jnp.stack([me.astype(jnp.int32), ends[-1]]),
+        jnp.stack([me, ends[-1], near_at % 2, near_at // 2, lax.axis_index("far")]).astype(jnp.int32),
         begins[::bq] // bk,
         begins[::bq] // (bk // 2),
     ])
@@ -686,32 +830,37 @@
         gain_ffn.reshape(1, width), hid, share, lax.axis_size("near"))
     g_oth = exchange(g_send)
     reduced = lax.psum_scatter(grads, ("tensor", "near"), scatter_dimension=0, tiled=True)
+    gains = gains[:2] + exchange(gains[:2])
+    parted = share % 16 == 0 and lax.axis_size("near") == 4 and lax.axis_size("far") % 2 == 0
+    gains = jnp.pad(gains, ((0, 0), (0, 3 * cols - width)))
+    d_qkv, *dw = attend_backward(sched, qkv, cosine, sine, start, lse, mixed_send, mixed_own,
+                                 g_oth, g_own, tokens, other_x, gains, bq, bk // 2,
+                                 share if parted else None)
+    x_send, x_own = input_grads(sched, d_qkv, full_qkv, d_first, 512)
+    if parted:
+        dw, gains, x_own, reduced = sum_parts(sched, share, *dw, gains, x_own, reduced)
+    else:
+        fore, back = bit_orders(count)
+        dw = jnp.concatenate([scatter_rows(dw[0][:, :edge], fore[::-1]),
+                              scatter_rows(dw[0][:, edge:], back[::-1])], axis=1).astype(F32)
+        dw = dw.reshape(share, cols // PAIR, 3, PAIR).transpose(2, 0, 1, 3).reshape(3, share, cols)
+        for bit in range(count.bit_length() - 1):
+            gains = gains + flip(gains, bit)
     reduced = lax.psum_scatter(reduced, "far", scatter_dimension=0, tiled=True)
-    gains = gains[:2] + exchange(gains[:2])
-    d_qkv, dw = attend_backward(sched, qkv, cosine, sine, start, lse, mixed_send, mixed_own,
-                                g_oth, g_own, tokens, other_x, bq, bk // 2)
-    dw, gains = lax.optimization_barrier((dw, gains))
-    fore, back = bit_orders(count)
-    for bit in fore[::-1]:
-        gains = gains + flip(gains, bit)
-    dw = jnp.concatenate([scatter_rows(dw[:, :edge], fore[::-1]),
-                          scatter_rows(dw[:, edge:], back[::-1])], axis=1).astype(F32)
-    dw = dw.reshape(share, cols // PAIR, 3, PAIR)
-    x_send, x_own = input_grads(sched, d_qkv, full_qkv, d_first, 512)
     input_grad = (x_own + exchange(x_send).astype(F32)).astype(BF16)
     grad_gate, grad_up, grad_down, grad_out = finish(reduced, hid)
     return (
         output,
         input_grad,
-        dw[:, :, 0].reshape(share, cols),
-        dw[:, :, 1].reshape(share, cols),
-        dw[:, :, 2].reshape(share, cols),
+        dw[0],
+        dw[1],
+        dw[2],
         grad_out,
         grad_gate,
         grad_up,
         grad_down,
-        gains[0],
-        gains[1],
+        gains[0, :width],
+        gains[1, :width],
     )
 
 

time: 301 us -> 293 us (0.973)
  waiting for transfers between devices: 69.5 us -> 65.1 us
  local copies, waits for them, and re-layouts: 12 us -> 8.33 us
    ppermute x18 -> x10, waiting for transfers between devices: 61.5 us -> 41.7 us  [flip(): return lax.ppermute(value, DP, [(at, at ^ 1 << bit) for at in range(count)])]
    ppermute x0 -> x3, waiting for transfers between devices: none -> 10.1 us  [shifted(): lax.ppermute(value, 'far', [(at, (at + shift) % far) for at in range(far)])]
    ppermute x18 -> x10, starting transfers between devices: 21.7 us -> 14 us  [flip(): return lax.ppermute(value, DP, [(at, at ^ 1 << bit) for at in range(count)])]
    ppermute x0 -> x3, starting transfers between devices: none -> 5.4 us  [shifted(): lax.ppermute(value, 'far', [(at, (at + shift) % far) for at in range(far)])]
    all_gather x1, waiting for transfers between devices: 2.31 us -> 7.3 us  [local(): feed_w = lax.all_gather(packed, ('tensor',) + DP, axis=0, tiled=True)]
    reduce_scatter x1, waiting for transfers between devices: 0.01 us -> 3.61 us  [local(): lax.psum_scatter(grads, ('tensor', 'near'), scatter_dimension=0, tiled=True)]
    slice x5 -> x1, local copies, waits for them, and re-layouts: 3.81 us -> 0.61 us  [local(): gains[1, :width]]
    reduce_scatter x1, waiting for transfers between devices: 3.06 us -> 0.01 us  [local(): reduced = lax.psum_scatter(reduced, 'far', scatter_dimension=0, tiled=True)]
  transfers between devices with their start and end apart: 26 -> 21, of which waited for: 15 -> 14; matrix products, arithmetic and copies ran while one was open for 9% -> 7% of each run, Pallas kernels for 37% -> 40%
where the time goes in v4:
time: 293 us; the launch traced here: 292 us
  Pallas kernels  167 us (57%)
  waiting for transfers between devices  65.1 us (22%)
  starting transfers between devices  20.2 us (7%)
  other arithmetic  17.2 us (6%)
  between operations  14.1 us (5%)
  local copies, waits for them, and re-layouts  8.33 us (3%)
    pallas_call x1, Pallas kernels, attend_backward(): pl.pallas_call(partial(backward_kernel, bq=bq, bk=bk, sub=sub, blocks=blo...  61 us
    pallas_call x1, Pallas kernels, feed(): pl.pallas_call(partial(feed_kernel, block=block, sub=sub, chunk=chunk, lo...  49.9 us
    ppermute x10, waiting for transfers between devices, flip(): return lax.ppermute(value, DP, [(at, at ^ 1 << bit) for at in range(count)])  41.7 us
    pallas_call x1, Pallas kernels, attend_forward(): pl.pallas_call(partial(forward_kernel, bq=bq, bk=bk, sub=sub, chunk=chunk...  40.9 us
    ppermute x10, starting transfers between devices, flip(): return lax.ppermute(value, DP, [(at, at ^ 1 << bit) for at in range(count)])  14 us
    pallas_call x1, Pallas kernels, input_grads(): pl.pallas_call(partial(input_grad_kernel, half=half), grid_spec=pltpu.Pre...  10.5 us
    ppermute x3, waiting for transfers between devices, shifted(): lax.ppermute(value, 'far', [(at, (at + shift) % far) for at in range(far)])  10.1 us
    all_gather x1, waiting for transfers between devices, local(): feed_w = lax.all_gather(packed, ('tensor',) + DP, axis=0, tiled=True)  7.3 us
  transfers between devices with their start and end apart: 21, of which 14 were waited for; matrix products, arithmetic and copies ran while one was open for 7% of the time, Pallas kernels for 40%

profile of v4, /device:TPU:0, one launch (start us, length us, event | category | flops | bytes accessed | tf_op | source)
XLA Modules:
  0.0 291.9 jit_solution(3195237513163296723)
XLA Ops:
  7.2 1.8 pad_maximum_fusion.3
  9.9 4.1 %collective-permute-start.1 = (bf16[1,48,1152]{2,1,0:T(8,128)(2,1)S(1)}, bf16[1,48,1152]{2,1,0:T(8,128)(2,1)S(1)}, u32[]{:S(2)}, u32[]{:S(2)}) collective-permute-start(bf16[1,48,1152]{2,1,0:T(8,128)(2,1)S(1)} %maximum_bitcast_fusion.2), channel_id=1, source_target_pairs={{0,16},{2,18},{4,20},{6,22},{8,24},{10,26},{12,28},{14,30},{16,0},... | collective-permute-start | bytes 331784 | tf_op jit(solution)/shard_map/ppermute | solution.py:736
  15.6 3.8 %collective-permute-done.1 = bf16[1,48,1152]{2,1,0:T(8,128)(2,1)S(1)} collective-permute-done((bf16[1,48,1152]{2,1,0:T(8,128)(2,1)S(1)}, bf16[1,48,1152]{2,1,0:T(8,128)(2,1)S(1)}, u32[]{:S(2)}, u32[]{:S(2)}) %collective-permute-start.1) | collective-permute-done | bytes 110624 | tf_op jit(solution)/shard_map/ppermute | solution.py:736
  21.1 5.6 %negate_select_fusion = (f32[2048,128]{1,0:T(8,128)}, f32[2048,128]{1,0:T(8,128)}) fusion(f32[128]{0:T(128)S(1)} %fusion.13, f32[2048]{0:T(1024)S(1)} %subtract_convert_fusion, pred[128]{0:T(512)(128)(4,1)S(1)} %broadcast_compare_fusion), kind=kLoop, calls=%fused_computation.2 | loop fusion | flops 786432 | bytes 2105984 | tf_op jit(solution)/shard_map/jit(_where)/select_n | solution.py:817
  26.8 2.6 collective-permute-done.2
  32.7 1.6 collective-permute-start.3
  36.7 5.0 %collective-permute-done.3 = bf16[2,2,1,48,640]{4,3,1,0,2:T(8,128)(2,1)S(1)} collective-permute-done((bf16[2,2,1,48,640]{4,3,1,0,2:T(8,128)(2,1)S(1)}, bf16[2,2,1,48,640]{4,3,1,0,2:T(8,128)(2,1)S(1)}, u32[]{:S(2)}, u32[]{:S(2)}) %collective-permute-start.3) | collective-permute-done | bytes 245792 | tf_op jit(solution)/shard_map/ppermute | solution.py:736
  42.6 7.5 %collective-permute-done.6 = bf16[2,2,2,1,48,512]{5,4,2,1,0,3:T(8,128)(2,1)S(1)} collective-permute-done((bf16[2,2,2,1,48,512]{5,4,2,1,0,3:T(8,128)(2,1)S(1)}, bf16[2,2,2,1,48,512]{5,4,2,1,0,3:T(8,128)(2,1)S(1)}, u32[]{:S(2)}, u32[]{:S(2)}) %collective-permute-start.6) | collective-permute-done | bytes 393248 | tf_op jit(solution)/shard_map/ppermute | solution.py:736
  50.3 4.5 %collective-permute-done.4 = bf16[2,2,2,1,48,640]{5,4,2,1,0,3:T(8,128)(2,1)S(1)} collective-permute-done((bf16[2,2,2,1,48,640]{5,4,2,1,0,3:T(8,128)(2,1)S(1)}, bf16[2,2,2,1,48,640]{5,4,2,1,0,3:T(8,128)(2,1)S(1)}, u32[]{:S(2)}, u32[]{:S(2)}) %collective-permute-start.4) | collective-permute-done | bytes 491552 | tf_op jit(solution)/shard_map/ppermute | solution.py:736
  57.7 40.9 %attend_forward.1 = (bf16[2048,1152]{1,0:T(8,128)(2,1)}, bf16[1024,384]{1,0:T(8,128)(2,1)}, bf16[1024,384]{1,0:T(8,128)(2,1)}, f32[3,2,2048]{2,1,0:T(2,128)}) custom-call(s32[9]{0:T(128)} %concatenate.12.sched, bf16[1024,768]{1,0:T(8,128)(2,1)} %x_own_ref.1, bf16[1024,768]{1,0:T(8,128)(2,1)} %copy-done.7, ...), custom_call_target="tpu_custom_call" | custom-call | flops 10066329600 | bytes 12582912 | tf_op jit(solution)/shard_map/attend_forward/pallas_call | solution.py:158
  101.3 7.3 %all-gather.2.cloned.1.call-done = bf16[1536,3456]{1,0:T(8,128)(2,1)} async-done(((bf16[48,3456]{1,0:T(8,128)(2,1)}), bf16[1536,3456]{1,0:T(8,128)(2,1)}) %all-gather.2.cloned.1.call-update) | async-done | bytes 10616848 | tf_op jit(solution)/shard_map/all_gather | solution.py:802
  108.6 49.9 %feed.1 = (bf16[1024,768]{1,0:T(8,128)(2,1)}, f32[1024,768]{1,0:T(8,128)}, bf16[1024,384]{1,0:T(8,128)(2,1)}, bf16[1024,384]{1,0:T(8,128)(2,1)}, bf16[2,4,4,48,3...) custom-call(s32[9]{0:T(128)} %concatenate.12.sched, bf16[1024,768]{1,0:T(8,128)(2,1)} %x_own_ref.1, ...), custom_call_target="tpu_custom_call" | custom-call | flops 32614907904 | bytes 23592960 | tf_op jit(solution)/shard_map/feed/pallas_call | solution.py:543
  164.2 61.0 %attend_backward.1 = (bf16[2048,1152]{1,0:T(8,128)(2,1)}, bf16[192,1152]{1,0:T(8,128)(2,1)}, bf16[208,1152]{1,0:T(8,128)(2,1)}, bf16[192,1152]{1,0:T(8,128)(2,1)}, bf16[192,1152]{1,0:T(8,128)(2,1)}) custom-call(s32[9]{0:T(128)} %concatenate.12.sched, bf16[2048,1152]{1,0:T(8,128)(2,1)} %get-tuple-element.53.q_ref.k_ref.v_ref, ...), custom_call_target="tpu_custom_call" | custom-call | flops 19730006016 | bytes 15728640 | tf_op jit(solution)/shard_map/attend_backward/pallas_call | solution.py:341
  225.2 10.5 %input_grads.1 = (bf16[1024,768]{1,0:T(8,128)(2,1)}, f32[1024,768]{1,0:T(8,128)}) custom-call(s32[9]{0:T(128)} %concatenate.12.sched, bf16[2048,1152]{1,0:T(8,128)(2,1)} %get-tuple-element.60.d_ref, bf16[768,1152]{1,0:T(8,128)(2,1)} %pad_maximum_fusion.wq_ref.wk_ref.wv_ref.w_ref, f32[1024,768]{1,0:T(8,128)} %get-tuple-element.61.dfirst_ref), custom_call_target="tpu_custom_call" | custom-call | flops 3623878656 | bytes 7864320 | tf_op jit(solution)/shard_map/input_grads/pallas_call | solution.py:596
  235.7 3.6 %reduce-scatter.3.cloned.1.call-done = bf16[192,3456]{1,0:T(8,128)(2,1)} async-done(((bf16[1536,3456]{1,0:T(8,128)(2,1)}), bf16[192,3456]{1,0:T(8,128)(2,1)}) %reduce-scatter.3.cloned.1.call-update) | async-done | bytes 1327120 | tf_op jit(solution)/shard_map/reduce_scatter | solution.py:832
  241.5 11.5 %collective-permute-done.12.got_b = bf16[192,1152]{1,0:T(8,128)(2,1)S(1)} collective-permute-done((bf16[192,1152]{1,0:T(8,128)(2,1)S(1)}, bf16[192,1152]{1,0:T(8,128)(2,1)S(1)}, u32[]{:S(2)}, u32[]{:S(2)}) %collective-permute-start.12) | collective-permute-done | bytes 442400 | tf_op jit(solution)/shard_map/ppermute | solution.py:736
  256.0 5.8 %collective-permute-done.14.got_b = bf16[96,1152]{1,0:T(8,128)(2,1)S(1)} collective-permute-done((bf16[96,1152]{1,0:T(8,128)(2,1)S(1)}, bf16[96,1152]{1,0:T(8,128)(2,1)S(1)}, u32[]{:S(2)}, u32[]{:S(2)}) %collective-permute-start.14) | collective-permute-done | bytes 221216 | tf_op jit(solution)/shard_map/ppermute | solution.py:736
  262.7 1.5 collective-permute-start.15
  264.3 2.4 collective-permute-start.16
  266.7 1.5 collective-permute-start.17
  268.2 3.5 %add_convert_fusion = bf16[1024,768]{1,0:T(8,128)(2,1)} fusion(f32[1024,768]{1,0:T(8,128)} %get-tuple-element.64, bf16[1024,768]{1,0:T(8,128)(2,1)S(1)} %collective-permute-done.10), kind=kLoop, calls=%fused_computation | loop fusion | flops 2359296 | bytes 6291456 | tf_op jit(solution)/shard_map/convert_element_type | solution.py:850
  271.7 3.0 %collective-permute-done.15.rest_0_ = bf16[64,1152]{1,0:T(8,128)(2,1)S(1)} collective-permute-done((bf16[64,1152]{1,0:T(8,128)(2,1)S(1)}, bf16[64,1152]{1,0:T(8,128)(2,1)S(1)}, u32[]{:S(2)}, u32[]{:S(2)}) %collective-permute-start.15) | collective-permute-done | bytes 147488 | tf_op jit(solution)/shard_map/ppermute | solution.py:707
  274.7 7.1 %collective-permute-done.16.rest_1_ = bf16[64,1152]{1,0:T(8,128)(2,1)S(1)} collective-permute-done((bf16[64,1152]{1,0:T(8,128)(2,1)S(1)}, bf16[64,1152]{1,0:T(8,128)(2,1)S(1)}, u32[]{:S(2)}, u32[]{:S(2)}) %collective-permute-start.16) | collective-permute-done | bytes 147488 | tf_op jit(solution)/shard_map/ppermute | solution.py:707
  283.6 1.8 finish.1
  (95 shorter events, 30.2 us)
Async XLA Ops:
  7.2 101.4 %all-gather.2.cloned.1.call-start = ((), (), s32[]{:S(2)}) async-start(), calls=%async_computation.2 | async-start | bytes 10948608 | tf_op jit(solution)/shard_map/all_gather | solution.py:802
  9.0 230.3 %reduce-scatter.3.cloned.1.call-start = ((), (), s32[]{:S(2)}) async-start(), calls=%async_computation.3 | async-start | bytes 11943936 | tf_op jit(solution)/shard_map/reduce_scatter | solution.py:832
  9.9 9.5 %collective-permute-start.1 = (bf16[1,48,1152]{2,1,0:T(8,128)(2,1)S(1)}, bf16[1,48,1152]{2,1,0:T(8,128)(2,1)S(1)}, u32[]{:S(2)}, u32[]{:S(2)}) collective-permute-start(bf16[1,48,1152]{2,1,0:T(8,128)(2,1)S(1)} %maximum_bitcast_fusion.2), channel_id=1, source_target_pairs={{0,16},{2,18},{4,20},{6,22},{8,24},{10,26},{12,28},{14,30},{16,0},... | collective-permute-start | bytes 331784 | tf_op jit(solution)/shard_map/ppermute | solution.py:736
  14.0 42.6 %collective-permute-start = (bf16[1024,768]{1,0:T(8,128)(2,1)}, bf16[1024,768]{1,0:T(8,128)(2,1)S(1)}, u32[]{:S(2)}, u32[]{:S(2)}) collective-permute-start(bf16[1024,768]{1,0:T(8,128)(2,1)} %x_own_ref.1), channel_id=1, source_target_pairs={{0,1},{1,0},{2,3},{3,2},{4,5},{5,4},{6,7},{7,6},{8,9},{9,8},{10,11... | collective-permute-start | bytes 4718600 | tf_op jit(solution)/shard_map/ppermute | solution.py:731
  20.3 9.1 %collective-permute-start.2 = (bf16[2,1,48,1152]{3,2,0,1:T(8,128)(2,1)S(1)}, bf16[2,1,48,1152]{3,2,0,1:T(8,128)(2,1)S(1)}, u32[]{:S(2)}, u32[]{:S(2)}) collective-permute-start(bf16[2,1,48,1152]{3,2,0,1:T(8,128)(2,1)S(1)} %fusion.8), channel_id=1, source_target_pairs={{0,8},{2,10},{4,12},{6,14},{8,0},{10,2},{12,4},{14,6},{16,24},{18,... | collective-permute-start | bytes 663560 | tf_op jit(solution)/shard_map/ppermute | solution.py:736
  29.5 5.7 %collective-permute-start.5 = (bf16[2,2,1,48,512]{4,3,1,0,2:T(8,128)(2,1)S(1)}, bf16[2,2,1,48,512]{4,3,1,0,2:T(8,128)(2,1)S(1)}, u32[]{:S(2)}, u32[]{:S(2)}) collective-permute-start(bf16[2,2,1,48,512]{4,3,1,0,2:T(8,128)(2,1)S(1)} %fusion.9), channel_id=1, source_target_pairs={{0,4},{2,6},{4,0},{6,2},{8,12},{10,14},{12,8},{14,10},{16,20},{18,... | collective-permute-start | bytes 589832 | tf_op jit(solution)/shard_map/ppermute | solution.py:736
  32.7 9.0 %collective-permute-start.3 = (bf16[2,2,1,48,640]{4,3,1,0,2:T(8,128)(2,1)S(1)}, bf16[2,2,1,48,640]{4,3,1,0,2:T(8,128)(2,1)S(1)}, u32[]{:S(2)}, u32[]{:S(2)}) collective-permute-start(bf16[2,2,1,48,640]{4,3,1,0,2:T(8,128)(2,1)S(1)} %fusion.15), channel_id=1, source_target_pairs={{0,2},{2,0},{4,6},{6,4},{8,10},{10,8},{12,14},{14,12},{16,18},{18,... | collective-permute-start | bytes 737288 | tf_op jit(solution)/shard_map/ppermute | solution.py:736
  35.4 14.7 %collective-permute-start.6 = (bf16[2,2,2,1,48,512]{5,4,2,1,0,3:T(8,128)(2,1)S(1)}, bf16[2,2,2,1,48,512]{5,4,2,1,0,3:T(8,128)(2,1)S(1)}, u32[]{:S(2)}, u32[]{:S(2)}) collective-permute-start(bf16[2,2,2,1,48,512]{5,4,2,1,0,3:T(8,128)(2,1)S(1)} %fusion.3), channel_id=1, source_target_pairs={{0,2},{2,0},{4,6},{6,4},{8,10},{10,8},{12,14},{14,12},{16,18},{18,... | collective-permute-start | bytes 1179656 | tf_op jit(solution)/shard_map/ppermute | solution.py:736
  41.8 13.0 %collective-permute-start.4 = (bf16[2,2,2,1,48,640]{5,4,2,1,0,3:T(8,128)(2,1)S(1)}, bf16[2,2,2,1,48,640]{5,4,2,1,0,3:T(8,128)(2,1)S(1)}, u32[]{:S(2)}, u32[]{:S(2)}) collective-permute-start(bf16[2,2,2,1,48,640]{5,4,2,1,0,3:T(8,128)(2,1)S(1)} %fusion.2), channel_id=1, source_target_pairs={{0,4},{2,6},{4,0},{6,2},{8,12},{10,14},{12,8},{14,10},{16,20},{18,... | collective-permute-start | bytes 1474568 | tf_op jit(solution)/shard_map/ppermute | solution.py:736
  57.7 41.0 %copy-start.5 = (f32[768]{0:T(1024)S(1)}, f32[768]{0:T(1024)}, u32[]{:S(2)}) copy-start(f32[768]{0:T(1024)} %param.20) | copy-start | bytes 9220
  57.7 41.6 %copy-start.6 = (f32[768]{0:T(1024)S(1)}, f32[768]{0:T(1024)}, u32[]{:S(2)}) copy-start(f32[768]{0:T(1024)} %param.21) | copy-start | bytes 9220
  98.7 2.6 collective-permute-start.7
  158.5 125.1 %reduce-scatter.5.cloned.1.call-start = ((), (), s32[]{:S(2)}) async-start(), calls=%async_computation.4 | async-start | bytes 1658880 | tf_op jit(solution)/shard_map/reduce_scatter | solution.py:849
  159.6 3.7 %collective-permute-start.8 = (bf16[1024,384]{1,0:T(8,128)(2,1)S(1)}, bf16[1024,384]{1,0:T(8,128)(2,1)S(1)}, u32[]{:S(2)}, u32[]{:S(2)}) collective-permute-start(bf16[1024,384]{1,0:T(8,128)(2,1)S(1)} %copy-done.8), channel_id=1, source_target_pairs={{0,1},{1,0},{2,3},{3,2},{4,5},{5,4},{6,7},{7,6},{8,9},{9,8},{10,11... | collective-permute-start | bytes 2359304 | tf_op jit(solution)/shard_map/ppermute | solution.py:731
  160.6 1.3 collective-permute-start.9
  225.1 27.9 %copy-start = (bf16[192,1152]{1,0:T(8,128)(2,1)S(1)}, bf16[192,1152]{1,0:T(8,128)(2,1)}, u32[]{:S(2)}) copy-start(bf16[192,1152]{1,0:T(8,128)(2,1)} %get-tuple-element.66.keep_a) | copy-start | bytes 1327108
  239.3 28.8 %collective-permute-start.10 = (bf16[1024,768]{1,0:T(8,128)(2,1)}, bf16[1024,768]{1,0:T(8,128)(2,1)S(1)}, u32[]{:S(2)}, u32[]{:S(2)}) collective-permute-start(bf16[1024,768]{1,0:T(8,128)(2,1)} %get-tuple-element.65), channel_id=1, source_target_pairs={{0,1},{1,0},{2,3},{3,2},{4,5},{5,4},{6,7},{7,6},{8,9},{9,8},{10,11... | collective-permute-start | bytes 4718600 | tf_op jit(solution)/shard_map/ppermute | solution.py:731
  239.4 13.7 %collective-permute-start.11 = (bf16[208,1152]{1,0:T(8,128)(2,1)S(1)}, bf16[208,1152]{1,0:T(8,128)(2,1)S(1)}, u32[]{:S(2)}, u32[]{:S(2)}) collective-permute-start(bf16[208,1152]{1,0:T(8,128)(2,1)S(1)} %copy-done.11), channel_id=1, source_target_pairs={{0,2},{2,0},{4,6},{6,4},{8,10},{10,8},{12,14},{14,12},{16,18},{18,... | collective-permute-start | bytes 1437704 | tf_op jit(solution)/shard_map/ppermute | solution.py:736
  240.8 12.2 %collective-permute-start.12 = (bf16[192,1152]{1,0:T(8,128)(2,1)S(1)}, bf16[192,1152]{1,0:T(8,128)(2,1)S(1)}, u32[]{:S(2)}, u32[]{:S(2)}) collective-permute-start(bf16[192,1152]{1,0:T(8,128)(2,1)S(1)} %copy-done.12), channel_id=1, source_target_pairs={{0,4},{2,6},{4,0},{6,2},{8,12},{10,14},{12,8},{14,10},{16,20},{18,... | collective-permute-start | bytes 1327112 | tf_op jit(solution)/shard_map/ppermute | solution.py:736
  253.9 7.9 %collective-permute-start.13 = (bf16[112,1152]{1,0:T(8,128)(2,1)S(1)}, bf16[112,1152]{1,0:T(8,128)(2,1)S(1)}, u32[]{:S(2)}, u32[]{:S(2)}) collective-permute-start(bf16[112,1152]{1,0:T(8,128)(2,1)S(1)} %get-tuple-element.71), channel_id=1, source_target_pairs={{0,4},{2,6},{4,0},{6,2},{8,12},{10,14},{12,8},{14,10},{16,20},{18,... | collective-permute-start | bytes 774152 | tf_op jit(solution)/shard_map/ppermute | solution.py:736
  255.1 6.8 %collective-permute-start.14 = (bf16[96,1152]{1,0:T(8,128)(2,1)S(1)}, bf16[96,1152]{1,0:T(8,128)(2,1)S(1)}, u32[]{:S(2)}, u32[]{:S(2)}) collective-permute-start(bf16[96,1152]{1,0:T(8,128)(2,1)S(1)} %get-tuple-element.73), channel_id=1, source_target_pairs={{0,2},{2,0},{4,6},{6,4},{8,10},{10,8},{12,14},{14,12},{16,18},{18,... | collective-permute-start | bytes 663560 | tf_op jit(solution)/shard_map/ppermute | solution.py:736
  262.7 11.9 %collective-permute-start.15 = (bf16[64,1152]{1,0:T(8,128)(2,1)S(1)}, bf16[64,1152]{1,0:T(8,128)(2,1)S(1)}, u32[]{:S(2)}, u32[]{:S(2)}) collective-permute-start(bf16[64,1152]{1,0:T(8,128)(2,1)S(1)} %get-tuple-element.77), channel_id=1, source_target_pairs={{0,8},{8,16},{16,24},{24,0},{1,9},{9,17},{17,25},{25,1},{2,10},{10... | collective-permute-start | bytes 442376 | tf_op jit(solution)/shard_map/ppermute | solution.py:707
  264.3 17.4 %collective-permute-start.16 = (bf16[64,1152]{1,0:T(8,128)(2,1)S(1)}, bf16[64,1152]{1,0:T(8,128)(2,1)S(1)}, u32[]{:S(2)}, u32[]{:S(2)}) collective-permute-start(bf16[64,1152]{1,0:T(8,128)(2,1)S(1)} %get-tuple-element.78), channel_id=1, source_target_pairs={{0,16},{8,24},{16,0},{24,8},{1,17},{9,25},{17,1},{25,9},{2,18},{10... | collective-permute-start | bytes 442376 | tf_op jit(solution)/shard_map/ppermute | solution.py:707
  266.7 15.0 %collective-permute-start.17 = (bf16[64,1152]{1,0:T(8,128)(2,1)S(1)}, bf16[64,1152]{1,0:T(8,128)(2,1)S(1)}, u32[]{:S(2)}, u32[]{:S(2)}) collective-permute-start(bf16[64,1152]{1,0:T(8,128)(2,1)S(1)} %get-tuple-element.79), channel_id=1, source_target_pairs={{0,24},{8,0},{16,8},{24,16},{1,25},{9,1},{17,9},{25,17},{2,26},{10... | collective-permute-start | bytes 442376 | tf_op jit(solution)/shard_map/ppermute | solution.py:707
  (10 other events, 138.0 us)
Sparse Core Ops, SparseCore 0:
  11.5 97.0 all-gather.1
  158.6 80.6 reduce-scatter.2
  241.6 37.1 reduce-scatter.4

commit v5 on v4

--- a/solution.py
+++ b/solution.py
@@ -286,7 +286,7 @@
         if share is None:
             dw_refs[0][...] = total
         else:
-            part_rows(total, gains_ref[...], sched[BIT_X], sched[BIT_Y], *dw_refs, share)
+            part_rows(total, gains_ref[0:2, :], sched[BIT_X], sched[BIT_Y], *dw_refs, share)
 
 
 def encode(value):
@@ -351,7 +351,7 @@
                 pl.BlockSpec((1, bq), lambda p, n, s: (0, place(n, s))),
                 pl.BlockSpec((None, 2, bq), lambda p, n, s: (p, 0, place(n, s))),
                 oth, own, oth, own, rows, rows,
-                pl.BlockSpec((2, 3 * PAIR), lambda p, n, s: (0, p)),
+                pl.BlockSpec((8, 3 * PAIR), lambda p, n, s: (0, p)),
             ],
             out_specs=[pl.BlockSpec((slots, 3 * PAIR), lambda p, n, s: (0, p)), *dw_specs],
             scratch_shapes=[
@@ -370,6 +370,7 @@
 
 def feed_kernel(sched, x_ref, own_ref, oth_ref, dy_ref, w_hbm, ga_ref, gf_ref,
                 out_ref, dfirst_ref, gown_ref, goth_ref, grads_ref, gains_ref,
+                right_hbm, left_hbm, dattn_hbm,
                 w_ref, keep_a, keep_b, total_s, right_s, left_s, dattn_s, mixed_s,
                 sems, *, block, sub, chunk, local, hid, head_cols, parts, share):
     step = pl.program_id(0)
@@ -413,7 +414,7 @@
             normed[r] = unit1[r] * ga_ref[...]
             normed_b[r] = normed[r].astype(BF16)
             left_s[0, here, :] = normed_b[r]
-            mixed_s[here, :] = jnp.concatenate([own_ref[rows, :], oth_ref[rows, :]], axis=1)
+            mixed_s[here, :] = oth_ref[rows, :]
         total_s[...] = jnp.zeros_like(total_s)
 
         @pl.loop(0, 2)
@@ -450,7 +451,7 @@
             valid = slot < sched[1]
             out_ref[rows, :] = jnp.where(valid, unit2 * gf_ref[...], 0.0).astype(BF16)
             dy = jnp.where(valid, dy_ref[rows, :].astype(F32), 0.0)
-            gains_ref[1:2, :] += jnp.sum(dy * unit2, axis=0, keepdims=True)
+            gains_ref[1:2, 0:dy.shape[1]] += jnp.sum(dy * unit2, axis=0, keepdims=True)
             scaled = dy * gf_ref[...]
             d_second[r] = rms2 * (scaled - unit2 * jnp.mean(scaled * unit2, axis=-1, keepdims=True))
             d_ffn[r] = d_second[r].astype(BF16)
@@ -477,7 +478,7 @@
             rows = slice(r, r + sub)
             here = pl.ds(base + r, sub)
             d_normed = total_s[rows, :]
-            gains_ref[0:1, :] += jnp.sum(d_normed * unit1[r], axis=0, keepdims=True)
+            gains_ref[0:1, 0:d_normed.shape[1]] += jnp.sum(d_normed * unit1[r], axis=0, keepdims=True)
             scaled = d_normed * ga_ref[...]
             d_first = rms1[r] * (scaled - unit1[r] * jnp.mean(scaled * unit1[r], axis=-1, keepdims=True))
             dfirst_ref[rows, :] = d_first
@@ -486,28 +487,106 @@
             gown_ref[rows, :] = mm(d_attn, w_ref[me, :, outs]).astype(BF16)
             goth_ref[rows, :] = mm(d_attn, w_ref[1 - me, :, outs]).astype(BF16)
 
+    mine = pl.ds(pl.multiple_of(me * hid, hid), hid)
+    outgoing = [
+        pltpu.make_async_copy(right_s.at[:, :, mine], right_hbm, sems.at[len(pieces)]),
+        pltpu.make_async_copy(left_s, left_hbm, sems.at[len(pieces) + 1]),
+        pltpu.make_async_copy(dattn_s, dattn_hbm, sems.at[len(pieces) + 2]),
+    ]
+
+    @pl.when(step == steps)
+    def _():
+        for copy in outgoing:
+            copy.start()
+
     @pl.when(step >= steps)
     def _():
-        tile = step - steps
-        t, part = lax.div(tile, parts), lax.rem(tile, parts)
         size = dattn_s.shape[1] // parts
-        rows = pl.ds(pl.multiple_of(part * size, size), size)
-        cols = pl.ds(pl.multiple_of(t * hid, hid), hid)
-
-        def store(value, there):
-            if share is None:
-                grads_ref[0, :, there] = value
-            else:
-                near = grads_ref.shape[1]
-                for n in range(size // share):
-                    grads_ref[0, n % near, n // near, :, there] = value[n * share:(n + 1) * share]
-
+        rows = pl.ds(pl.multiple_of((step - steps) * size, size), size)
+        cols = pl.ds(pl.multiple_of((1 - me) * hid, hid), hid)
         for n in range(3):
             left = left_s[n // 2, :, rows]
-            store(tdot(left, right_s[n, :, cols]).astype(BF16), slice(n * hid, (n + 1) * hid))
-
-        mixed = jnp.where(t == me, mixed_s[:, :head_cols], mixed_s[:, head_cols:])
-        store(tdot(dattn_s[:, rows], mixed).astype(BF16), slice(3 * hid, 3 * hid + head_cols))
+            store_rows(grads_ref, tdot(left, right_s[n, :, cols]), slice(n * hid, (n + 1) * hid), share)
+        store_rows(grads_ref, tdot(dattn_s[:, rows], mixed_s[...]),
+                   slice(3 * hid, 3 * hid + head_cols), share)
+
+    @pl.when(step == steps + parts - 1)
+    def _():
+        for copy in outgoing:
+            copy.wait()
+
+
+def store_rows(ref, value, cols, share, part=0):
+    value = value.astype(BF16)
+    rows = value.shape[0]
+    if share is None:
+        ref[pl.ds(pl.multiple_of(part * rows, rows), rows), cols] = value
+    else:
+        near = ref.shape[0]
+        for n in range(rows // share):
+            far = part * (rows // (share * near)) + n // near
+            ref[n % near, far, :, cols] = value[n * share:(n + 1) * share]
+
+
+def own_grads_kernel(left_ref, right_ref, dattn_ref, mixed_ref, out_ref, *, tiles, share):
+    step = pl.program_id(0)
+
+    size = left_ref.shape[1] // 2
+
+    @pl.loop(0, 2)
+    def _(part):
+        rows = pl.ds(pl.multiple_of(part * size, size), size)
+
+        @pl.when(step < tiles)
+        def _():
+            store_rows(out_ref, tdot(left_ref[:, rows], right_ref[...]), slice(None), share, part)
+
+        @pl.when(step == tiles)
+        def _():
+            store_rows(out_ref, tdot(dattn_ref[:, rows], mixed_ref[...]),
+                       slice(0, mixed_ref.shape[1]), share, part)
+
+
+def own_grads(left, right, d_attn, mixed, share, near, tile=512):
+    _, local, width = left.shape
+    hid, head_cols = right.shape[2], mixed.shape[1]
+    each = hid // tile
+    tiles = 3 * each
+    total = 3 * hid + head_cols
+    packed = share % 16 == 0
+    if packed:
+        shape = (near, width // (near * share), share)
+        out_spec = pl.BlockSpec((*shape, tile), lambda n: (0, 0, 0, n))
+    else:
+        shape = (width,)
+        out_spec = pl.BlockSpec((width, tile), lambda n: (0, n))
+
+    def kind(n):
+        return jnp.minimum(lax.div(n, each), 2)
+
+    grads = pl.pallas_call(
+        partial(own_grads_kernel, tiles=tiles, share=share if packed else None),
+        grid=(tiles + 1,),
+        in_specs=[
+            pl.BlockSpec((None, local, width), lambda n: (lax.div(kind(n), 2), 0, 0)),
+            pl.BlockSpec((None, local, tile), lambda n: (kind(n), 0, lax.rem(jnp.minimum(n, tiles - 1), each))),
+            pl.BlockSpec((local, width), lambda n: (0, 0)),
+            pl.BlockSpec((local, head_cols), lambda n: (0, 0)),
+        ],
+        out_specs=out_spec,
+        out_shape=jax.ShapeDtypeStruct((*shape, total), BF16),
+        compiler_params=params(),
+        cost_estimate=cost(2 * local * width * total, 2 * local * (4 * width + 3 * hid)),
+        name="own_grads",
+    )(left, right, d_attn, mixed)
+    return by_near(grads, share, near)
+
+
+def by_near(grads, share, near):
+    total = grads.shape[-1]
+    if share % 16:
+        grads = grads.reshape(-1, near, share, total).swapaxes(0, 1)
+    return grads.reshape(-1, total)
 
 
 def feed(sched, x, own, oth, dy, weights, gain_attn, gain_ffn, hid, share, near,
@@ -527,15 +606,13 @@
 
     def tile(s, sched):
         n = jnp.maximum(s - steps, 0)
-        if packed:
-            return (lax.div(n, parts), 0, lax.rem(n, parts), 0, 0)
-        return (lax.div(n, parts), lax.rem(n, parts), 0)
+        return (0, n, 0, 0) if packed else (n, 0)
 
     if packed:
-        grads_shape = (2, near, width // (near * share), share, total)
-        grads_block = (1, near, width // (near * share * parts), share, total)
+        grads_shape = (near, width // (near * share), share, total)
+        grads_block = (near, width // (near * share * parts), share, total)
     else:
-        grads_shape, grads_block = (2, width, total), (1, width // parts, total)
+        grads_shape, grads_block = (width, total), (width // parts, total)
 
     def shape(cols, dtype):
         return jax.ShapeDtypeStruct((local, cols), dtype)
@@ -545,31 +622,32 @@
                 head_cols=head_cols, parts=parts, share=share if packed else None),
         grid_spec=pltpu.PrefetchScalarGridSpec(
             num_scalar_prefetch=1,
-            grid=(steps + 2 * parts,),
+            grid=(steps + parts,),
             in_specs=[rows, heads, heads, rows, pl.BlockSpec(memory_space=pl.ANY), gain, gain],
             out_specs=[rows, rows, heads, heads,
                        pl.BlockSpec(grads_block, tile),
-                       pl.BlockSpec((16, width), lambda s, sched: (0, 0))],
+                       pl.BlockSpec((8, 3 * head_cols), lambda s, sched: (0, 0))]
+            + [pl.BlockSpec(memory_space=pl.ANY)] * 3,
             scratch_shapes=[pltpu.VMEM(weights.shape, BF16)]
             + [pltpu.VMEM((block, 2 * hid), F32)] * 2
             + [pltpu.VMEM((block, width), F32)]
             + [pltpu.VMEM((3, local, 2 * hid), BF16), pltpu.VMEM((2, local, width), BF16)]
             + [pltpu.VMEM((local, width), BF16)]
-            + [pltpu.VMEM((local, 2 * head_cols), BF16), pltpu.SemaphoreType.DMA((4,))],
+            + [pltpu.VMEM((local, head_cols), BF16), pltpu.SemaphoreType.DMA((7,))],
         ),
         out_shape=[
             shape(width, BF16), shape(width, F32), shape(head_cols, BF16), shape(head_cols, BF16),
             jax.ShapeDtypeStruct(grads_shape, BF16),
-            jax.ShapeDtypeStruct((16, width), F32),
+            jax.ShapeDtypeStruct((8, 3 * head_cols), F32),
+            jax.ShapeDtypeStruct((3, local, hid), BF16),
+            jax.ShapeDtypeStruct((2, local, width), BF16),
+            shape(width, BF16),
         ],
         compiler_params=params(60 * 1024 * 1024),
         cost_estimate=cost(12 * local * width * total, 30 * local * width),
         name="feed",
     )(sched, x, own, oth, dy, weights, gain_attn, gain_ffn)
-    grads = results[4]
-    if not packed:
-        grads = grads.reshape(2, -1, near, share, total).swapaxes(1, 2)
-    return (*results[:4], grads.reshape(-1, total), results[5])
+    return (*results[:4], by_near(results[4], share, near), *results[5:])
 
 
 def input_grad_kernel(sched, d_ref, w_ref, dfirst_ref, oth_ref, own_ref, *, half):
@@ -659,7 +737,7 @@
             other = pl.ds(pl.multiple_of((2 * n + 1 - bit) * share, share), share)
             stay[here] = add(held[mine], got[mine]).astype(BF16)
             go[here] = add(held[other], got[other]).astype(BF16)
-    total[...] = gains[...] + decode(got_a[2 * size:])
+    total[...] = gains[0:2, :] + decode(got_a[2 * size:])
     send_a[size:] = encode(total[...])
 
 
@@ -707,24 +785,30 @@
     return lax.ppermute(value, "far", [(at, (at + shift) % far) for at in range(far)])
 
 
-def sum_parts(sched, share, keep_a, send_a, keep_b, send_b, gains, beside, late):
+def sum_parts(sched, share, keep_a, send_a, keep_b, send_b, gains, meanwhile):
     size, width = keep_a.shape
     far = lax.axis_size("far")
-    send_a, send_b, beside, late = lax.optimization_barrier((send_a, send_b, beside, late))
     got_a, got_b = flip(send_a, 0), flip(send_b, 1)
+    beside = meanwhile()
+    got_a, got_b, beside = lax.optimization_barrier((got_a, got_b, beside))
     sizes = [size // 2, size // 2 + EXTRA, size // 2, size // 2]
     keep_a, send_a, keep_b, send_b, gains = whole_call(
         partial(near_kernel, share=share), "near_sums", sched,
         (keep_a, got_a, keep_b, got_b, gains),
-        [((rows, width), BF16) for rows in sizes] + [(gains.shape, F32)])
+        [((rows, width), BF16) for rows in sizes] + [((2, width), F32)])
     got_a, got_b = flip(send_a, 1), flip(send_b, 0)
     own, gains, *sends = whole_call(
         far_kernel, "far_sums", sched, (keep_a, got_a, keep_b, got_b, gains),
         [((share, width), F32), (gains.shape, F32)] + [((share + EXTRA, width), BF16)] * (far - 1))
     got = [shifted(value, shift + 1) for shift, value in enumerate(sends)]
+    return (own, gains, *got), beside
+
+
+def last_sums(sched, own, gains, *got):
+    share, width = own.shape
     *dw, gains = whole_call(last_kernel, "last_sums", sched, (own, gains, *got),
                             [((share, width // 3), F32)] * 3 + [(gains.shape, F32)])
-    return dw, gains, beside, late
+    return dw, gains
 
 
 def exchange(value):
@@ -825,21 +909,26 @@
     qkv, mixed_send, mixed_own, lse = attend_forward(
         sched, tokens, other_x, full_qkv, cosine, sine, start, bq, bk)
     mixed_oth = exchange(mixed_send)
-    output, d_first, g_own, g_send, grads, gains = feed(
+    output, d_first, g_own, g_send, grads, gains, right, left, d_attn = feed(
         sched, tokens, mixed_own, mixed_oth, cotangent, feed_w, gain_attn.reshape(1, width),
         gain_ffn.reshape(1, width), hid, share, lax.axis_size("near"))
     g_oth = exchange(g_send)
-    reduced = lax.psum_scatter(grads, ("tensor", "near"), scatter_dimension=0, tiled=True)
-    gains = gains[:2] + exchange(gains[:2])
+    other_grads = exchange(grads)
+    grads = own_grads(left, right, d_attn, mixed_own, share, lax.axis_size("near"))
+    grads = (grads.astype(F32) + other_grads.astype(F32)).astype(BF16)
+    grads, g_oth = lax.optimization_barrier((grads, g_oth))
+    reduced = lax.psum_scatter(grads, "near", scatter_dimension=0, tiled=True)
+    gains = gains + exchange(gains)
     parted = share % 16 == 0 and lax.axis_size("near") == 4 and lax.axis_size("far") % 2 == 0
-    gains = jnp.pad(gains, ((0, 0), (0, 3 * cols - width)))
     d_qkv, *dw = attend_backward(sched, qkv, cosine, sine, start, lse, mixed_send, mixed_own,
                                  g_oth, g_own, tokens, other_x, gains, bq, bk // 2,
                                  share if parted else None)
-    x_send, x_own = input_grads(sched, d_qkv, full_qkv, d_first, 512)
+    d_qkv, reduced, *dw = lax.optimization_barrier((d_qkv, reduced, *dw))
+    into_input = partial(input_grads, sched, d_qkv, full_qkv, d_first, 512)
     if parted:
-        dw, gains, x_own, reduced = sum_parts(sched, share, *dw, gains, x_own, reduced)
+        last, (x_send, x_own) = sum_parts(sched, share, *dw, gains, into_input)
     else:
+        x_send, x_own = into_input()
         fore, back = bit_orders(count)
         dw = jnp.concatenate([scatter_rows(dw[0][:, :edge], fore[::-1]),
                               scatter_rows(dw[0][:, edge:], back[::-1])], axis=1).astype(F32)
@@ -848,7 +937,11 @@
             gains = gains + flip(gains, bit)
     reduced = lax.psum_scatter(reduced, "far", scatter_dimension=0, tiled=True)
     input_grad = (x_own + exchange(x_send).astype(F32)).astype(BF16)
-    grad_gate, grad_up, grad_down, grad_out = finish(reduced, hid)
+    ready = (input_grad, *finish(reduced, hid))
+    if parted:
+        ready, last = lax.optimization_barrier((ready, last))
+        dw, gains = last_sums(sched, *last)
+    input_grad, grad_gate, grad_up, grad_down, grad_out = ready
     return (
         output,
         input_grad,

time: 293 us -> 285 us (0.973)
  Pallas kernels: 167 us -> 153 us
  other arithmetic: 17.2 us -> 23 us
    pallas_call x1, Pallas kernels: 61 us -> 46.3 us  [attend_backward(): pl.pallas_call(partial(backward_kernel, bq=bq, bk=bk, sub=sub, blocks=blo...]
    pallas_call x0 -> x1, Pallas kernels: none -> 13.1 us  [own_grads(): pl.pallas_call(partial(own_grads_kernel, tiles=tiles, share=share if pack...]
    ppermute x10, waiting for transfers between devices: 41.7 us -> 31.4 us  [flip(): return lax.ppermute(value, DP, [(at, at ^ 1 << bit) for at in range(count)])]
    reduce_scatter x1, waiting for transfers between devices: 3.61 us -> 11.8 us  [local(): reduced = lax.psum_scatter(grads, 'near', scatter_dimension=0, tiled=True)]
    ppermute x3, waiting for transfers between devices: 10.1 us -> 2.05 us  [shifted(): lax.ppermute(value, 'far', [(at, (at + shift) % far) for at in range(far)])]
    all_gather x1, waiting for transfers between devices: 7.3 us -> 13.7 us  [local(): feed_w = lax.all_gather(packed, ('tensor',) + DP, axis=0, tiled=True)]
    pallas_call x1, Pallas kernels: 49.9 us -> 43.6 us  [feed(): pl.pallas_call(partial(feed_kernel, block=block, sub=sub, chunk=chunk, lo...]
    convert_element_type x0 -> x1, other arithmetic: none -> 6.12 us  [local(): grads = (grads.astype(F32) + other_grads.astype(F32)).astype(BF16)]
  transfers between devices with their start and end apart: 21 -> 22, of which waited for: 14 -> 14; matrix products, arithmetic and copies ran while one was open for 7% -> 9% of each run, Pallas kernels for 40% -> 38%
where the time goes in v5:
time: 285 us; the launch traced here: 283 us
  Pallas kernels  153 us (54%)
  waiting for transfers between devices  66.7 us (23%)
  other arithmetic  23 us (8%)
  starting transfers between devices  21 us (7%)
  between operations  14 us (5%)
  local copies, waits for them, and re-layouts  5.7 us (2%)
    pallas_call x1, Pallas kernels, attend_backward(): pl.pallas_call(partial(backward_kernel, bq=bq, bk=bk, sub=sub, blocks=blo...  46.3 us
    pallas_call x1, Pallas kernels, feed(): pl.pallas_call(partial(feed_kernel, block=block, sub=sub, chunk=chunk, lo...  43.6 us
    pallas_call x1, Pallas kernels, attend_forward(): pl.pallas_call(partial(forward_kernel, bq=bq, bk=bk, sub=sub, chunk=chunk...  34.8 us
    ppermute x10, waiting for transfers between devices, flip(): return lax.ppermute(value, DP, [(at, at ^ 1 << bit) for at in range(count)])  31.4 us
    ppermute x10, starting transfers between devices, flip(): return lax.ppermute(value, DP, [(at, at ^ 1 << bit) for at in range(count)])  14 us
    all_gather x1, waiting for transfers between devices, local(): feed_w = lax.all_gather(packed, ('tensor',) + DP, axis=0, tiled=True)  13.7 us
    pallas_call x1, Pallas kernels, own_grads(): pl.pallas_call(partial(own_grads_kernel, tiles=tiles, share=share if pack...  13.1 us
    reduce_scatter x1, waiting for transfers between devices, local(): reduced = lax.psum_scatter(grads, 'near', scatter_dimension=0, tiled=True)  11.8 us
  transfers between devices with their start and end apart: 22, of which 14 were waited for; matrix products, arithmetic and copies ran while one was open for 9% of the time, Pallas kernels for 38%

profile of v5, /device:TPU:0, one launch (start us, length us, event | category | flops | bytes accessed | tf_op | source)
XLA Modules:
  0.0 283.4 jit_solution(855429278229679567)
XLA Ops:
  7.2 1.8 pad_maximum_fusion.3
  9.9 4.1 %collective-permute-start.1 = (bf16[1,48,1152]{2,1,0:T(8,128)(2,1)S(1)}, bf16[1,48,1152]{2,1,0:T(8,128)(2,1)S(1)}, u32[]{:S(2)}, u32[]{:S(2)}) collective-permute-start(bf16[1,48,1152]{2,1,0:T(8,128)(2,1)S(1)} %maximum_bitcast_fusion.2), channel_id=1, source_target_pairs={{0,16},{2,18},{4,20},{6,22},{8,24},{10,26},{12,28},{14,30},{16,0},... | collective-permute-start | bytes 331784 | tf_op jit(solution)/shard_map/ppermute | solution.py:820
  15.6 3.8 %collective-permute-done.1 = bf16[1,48,1152]{2,1,0:T(8,128)(2,1)S(1)} collective-permute-done((bf16[1,48,1152]{2,1,0:T(8,128)(2,1)S(1)}, bf16[1,48,1152]{2,1,0:T(8,128)(2,1)S(1)}, u32[]{:S(2)}, u32[]{:S(2)}) %collective-permute-start.1) | collective-permute-done | bytes 110624 | tf_op jit(solution)/shard_map/ppermute | solution.py:820
  21.1 5.6 %negate_select_fusion = (f32[2048,128]{1,0:T(8,128)}, f32[2048,128]{1,0:T(8,128)}) fusion(f32[128]{0:T(128)S(1)} %fusion.14, f32[2048]{0:T(1024)S(1)} %subtract_convert_fusion, pred[128]{0:T(512)(128)(4,1)S(1)} %broadcast_compare_fusion), kind=kLoop, calls=%fused_computation.4 | loop fusion | flops 786432 | bytes 2105984 | tf_op jit(solution)/shard_map/jit(_where)/select_n | solution.py:901
  26.7 2.6 collective-permute-done.2
  32.7 1.6 collective-permute-start.3
  36.7 5.0 %collective-permute-done.3 = bf16[2,2,1,48,640]{4,3,1,0,2:T(8,128)(2,1)S(1)} collective-permute-done((bf16[2,2,1,48,640]{4,3,1,0,2:T(8,128)(2,1)S(1)}, bf16[2,2,1,48,640]{4,3,1,0,2:T(8,128)(2,1)S(1)}, u32[]{:S(2)}, u32[]{:S(2)}) %collective-permute-start.3) | collective-permute-done | bytes 245792 | tf_op jit(solution)/shard_map/ppermute | solution.py:820
  42.6 7.9 %collective-permute-done.6 = bf16[2,2,2,1,48,512]{5,4,2,1,0,3:T(8,128)(2,1)S(1)} collective-permute-done((bf16[2,2,2,1,48,512]{5,4,2,1,0,3:T(8,128)(2,1)S(1)}, bf16[2,2,2,1,48,512]{5,4,2,1,0,3:T(8,128)(2,1)S(1)}, u32[]{:S(2)}, u32[]{:S(2)}) %collective-permute-start.6) | collective-permute-done | bytes 393248 | tf_op jit(solution)/shard_map/ppermute | solution.py:820
  50.7 3.9 %collective-permute-done.4 = bf16[2,2,2,1,48,640]{5,4,2,1,0,3:T(8,128)(2,1)S(1)} collective-permute-done((bf16[2,2,2,1,48,640]{5,4,2,1,0,3:T(8,128)(2,1)S(1)}, bf16[2,2,2,1,48,640]{5,4,2,1,0,3:T(8,128)(2,1)S(1)}, u32[]{:S(2)}, u32[]{:S(2)}) %collective-permute-start.4) | collective-permute-done | bytes 491552 | tf_op jit(solution)/shard_map/ppermute | solution.py:820
  57.4 34.8 %attend_forward.1 = (bf16[2048,1152]{1,0:T(8,128)(2,1)}, bf16[1024,384]{1,0:T(8,128)(2,1)}, bf16[1024,384]{1,0:T(8,128)(2,1)}, f32[3,2,2048]{2,1,0:T(2,128)}) custom-call(s32[9]{0:T(128)} %concatenate.12.sched, bf16[1024,768]{1,0:T(8,128)(2,1)} %x_own_ref.1, bf16[1024,768]{1,0:T(8,128)(2,1)} %copy-done.8, ...), custom_call_target="tpu_custom_call" | custom-call | flops 10066329600 | bytes 12582912 | tf_op jit(solution)/shard_map/attend_forward/pallas_call | solution.py:158
  94.8 13.7 %all-gather.2.cloned.1.call-done = bf16[1536,3456]{1,0:T(8,128)(2,1)} async-done(((bf16[48,3456]{1,0:T(8,128)(2,1)}), bf16[1536,3456]{1,0:T(8,128)(2,1)}) %all-gather.2.cloned.1.call-update) | async-done | bytes 10616848 | tf_op jit(solution)/shard_map/all_gather | solution.py:886
  108.5 43.6 %feed.1 = (bf16[1024,768]{1,0:T(8,128)(2,1)}, f32[1024,768]{1,0:T(8,128)}, bf16[1024,384]{1,0:T(8,128)(2,1)}, bf16[1024,384]{1,0:T(8,128)(2,1)}, bf16[4,4,48,345...) custom-call(s32[9]{0:T(128)} %concatenate.12.sched, ...), custom_call_target="tpu_custom_call" | custom-call | flops 32614907904 | bytes 23592960 | tf_op jit(solution)/shard_map/feed/pallas_call | solution.py:620
  152.7 13.1 %own_grads.1 = bf16[4,4,48,3456]{3,2,1,0:T(8,128)(2,1)} custom-call(bf16[2,1024,768]{2,1,0:T(8,128)(2,1)} %get-tuple-element.76.left_ref, bf16[3,1024,1024]{2,1,0:T(8,128)(2,1)} %get-tuple-element.77.right_ref, bf16[1024,768]{1,0:T(8,128)(2,1)} %get-tuple-element.78.dattn_ref, bf16[1024,384]{1,0:T(8,128)(2,1)} %get-tuple-element.71.own_ref.mixed_ref.o_own_ref), custom_call_target="tpu_custom_call" | custom-call | flops 5435817984 | bytes 12582912 | tf_op jit(solution)/shard_map/own_grads/pallas_call | solution.py:567
  165.8 6.1 %fusion = bf16[768,3456]{1,0:T(8,128)(2,1)} fusion(bf16[768,3456]{1,0:T(8,128)(2,1)S(1)} %collective-permute-done.8, bf16[4,4,48,3456]{3,2,1,0:T(8,128)(2,1)} %own_grads.1), kind=kLoop, calls=%fused_computation.1 | loop fusion | flops 10616832 | bytes 15925248 | tf_op jit(solution)/shard_map/convert_element_type | solution.py:918
  174.5 46.3 %attend_backward.1 = (bf16[2048,1152]{1,0:T(8,128)(2,1)}, bf16[192,1152]{1,0:T(8,128)(2,1)}, bf16[208,1152]{1,0:T(8,128)(2,1)}, bf16[192,1152]{1,0:T(8,128)(2,1)}, bf16[192,1152]{1,0:T(8,128)(2,1)}) custom-call(s32[9]{0:T(128)} %concatenate.12.sched, bf16[2048,1152]{1,0:T(8,128)(2,1)} %get-tuple-element.74.q_ref.k_ref.v_ref, ...), custom_call_target="tpu_custom_call" | custom-call | flops 19730006016 | bytes 15728640 | tf_op jit(solution)/shard_map/attend_backward/pallas_call | solution.py:341
  220.8 11.8 %reduce-scatter.3.cloned.1.call-done = bf16[192,3456]{1,0:T(8,128)(2,1)} async-done(((bf16[768,3456]{1,0:T(8,128)(2,1)}), bf16[192,3456]{1,0:T(8,128)(2,1)}) %reduce-scatter.3.cloned.1.call-update) | async-done | bytes 1327120 | tf_op jit(solution)/shard_map/reduce_scatter | solution.py:920
  234.8 10.4 %input_grads.1 = (bf16[1024,768]{1,0:T(8,128)(2,1)}, f32[1024,768]{1,0:T(8,128)}) custom-call(s32[9]{0:T(128)} %concatenate.12.sched, bf16[2048,1152]{1,0:T(8,128)(2,1)} %get-tuple-element.92.d_ref, bf16[768,1152]{1,0:T(8,128)(2,1)} %pad_maximum_fusion.wq_ref.wk_ref.wv_ref.w_ref, f32[1024,768]{1,0:T(8,128)} %get-tuple-element.93.dfirst_ref), custom_call_target="tpu_custom_call" | custom-call | flops 3623878656 | bytes 7864320 | tf_op jit(solution)/shard_map/input_grads/pallas_call | solution.py:674
  248.9 6.6 %collective-permute-done.15.got_b = bf16[96,1152]{1,0:T(8,128)(2,1)S(1)} collective-permute-done((bf16[96,1152]{1,0:T(8,128)(2,1)S(1)}, bf16[96,1152]{1,0:T(8,128)(2,1)S(1)}, u32[]{:S(2)}, u32[]{:S(2)}) %collective-permute-start.15) | collective-permute-done | bytes 221216 | tf_op jit(solution)/shard_map/ppermute | solution.py:820
  256.4 3.1 %collective-permute-start.16 = (bf16[64,1152]{1,0:T(8,128)(2,1)S(1)}, bf16[64,1152]{1,0:T(8,128)(2,1)S(1)}, u32[]{:S(2)}, u32[]{:S(2)}) collective-permute-start(bf16[64,1152]{1,0:T(8,128)(2,1)S(1)} %get-tuple-element.114), channel_id=1, source_target_pairs={{0,8},{8,16},{16,24},{24,0},{1,9},{9,17},{17,25},{25,1},{2,10},{10... | collective-permute-start | bytes 442376 | tf_op jit(solution)/shard_map/ppermute | solution.py:785
  260.3 2.0 collective-permute-start.18
  262.3 3.4 %add_convert_fusion = bf16[1024,768]{1,0:T(8,128)(2,1)} fusion(f32[1024,768]{1,0:T(8,128)} %get-tuple-element.96, bf16[1024,768]{1,0:T(8,128)(2,1)S(1)} %collective-permute-done.13), kind=kLoop, calls=%fused_computation.2 | loop fusion | flops 2359296 | bytes 6291456 | tf_op jit(solution)/shard_map/convert_element_type | solution.py:939
  265.7 5.5 %reduce-scatter.5.cloned.1.call-done.total_ref = bf16[48,3456]{1,0:T(8,128)(2,1)} async-done(((bf16[192,3456]{1,0:T(8,128)(2,1)}), bf16[48,3456]{1,0:T(8,128)(2,1)}) %reduce-scatter.5.cloned.1.call-update) | async-done | bytes 331792 | tf_op jit(solution)/shard_map/reduce_scatter | solution.py:938
  271.2 1.8 finish.1
  273.0 2.0 collective-permute-done.17.rest_1_
  (93 shorter events, 29.0 us)
Async XLA Ops:
  7.2 101.3 %all-gather.2.cloned.1.call-start = ((), (), s32[]{:S(2)}) async-start(), calls=%async_computation.2 | async-start | bytes 10948608 | tf_op jit(solution)/shard_map/all_gather | solution.py:886
  9.0 223.7 %reduce-scatter.3.cloned.1.call-start = ((), (), s32[]{:S(2)}) async-start(), calls=%async_computation.3 | async-start | bytes 6635520 | tf_op jit(solution)/shard_map/reduce_scatter | solution.py:920
  9.9 9.5 %collective-permute-start.1 = (bf16[1,48,1152]{2,1,0:T(8,128)(2,1)S(1)}, bf16[1,48,1152]{2,1,0:T(8,128)(2,1)S(1)}, u32[]{:S(2)}, u32[]{:S(2)}) collective-permute-start(bf16[1,48,1152]{2,1,0:T(8,128)(2,1)S(1)} %maximum_bitcast_fusion.2), channel_id=1, source_target_pairs={{0,16},{2,18},{4,20},{6,22},{8,24},{10,26},{12,28},{14,30},{16,0},... | collective-permute-start | bytes 331784 | tf_op jit(solution)/shard_map/ppermute | solution.py:820
  14.0 42.3 %collective-permute-start = (bf16[1024,768]{1,0:T(8,128)(2,1)}, bf16[1024,768]{1,0:T(8,128)(2,1)S(1)}, u32[]{:S(2)}, u32[]{:S(2)}) collective-permute-start(bf16[1024,768]{1,0:T(8,128)(2,1)} %x_own_ref.1), channel_id=1, source_target_pairs={{0,1},{1,0},{2,3},{3,2},{4,5},{5,4},{6,7},{7,6},{8,9},{9,8},{10,11... | collective-permute-start | bytes 4718600 | tf_op jit(solution)/shard_map/ppermute | solution.py:815
  20.3 9.1 %collective-permute-start.2 = (bf16[2,1,48,1152]{3,2,0,1:T(8,128)(2,1)S(1)}, bf16[2,1,48,1152]{3,2,0,1:T(8,128)(2,1)S(1)}, u32[]{:S(2)}, u32[]{:S(2)}) collective-permute-start(bf16[2,1,48,1152]{3,2,0,1:T(8,128)(2,1)S(1)} %fusion.9), channel_id=1, source_target_pairs={{0,8},{2,10},{4,12},{6,14},{8,0},{10,2},{12,4},{14,6},{16,24},{18,... | collective-permute-start | bytes 663560 | tf_op jit(solution)/shard_map/ppermute | solution.py:820
  29.5 5.7 %collective-permute-start.5 = (bf16[2,2,1,48,512]{4,3,1,0,2:T(8,128)(2,1)S(1)}, bf16[2,2,1,48,512]{4,3,1,0,2:T(8,128)(2,1)S(1)}, u32[]{:S(2)}, u32[]{:S(2)}) collective-permute-start(bf16[2,2,1,48,512]{4,3,1,0,2:T(8,128)(2,1)S(1)} %fusion.10), channel_id=1, source_target_pairs={{0,4},{2,6},{4,0},{6,2},{8,12},{10,14},{12,8},{14,10},{16,20},{18,... | collective-permute-start | bytes 589832 | tf_op jit(solution)/shard_map/ppermute | solution.py:820
  32.7 9.0 %collective-permute-start.3 = (bf16[2,2,1,48,640]{4,3,1,0,2:T(8,128)(2,1)S(1)}, bf16[2,2,1,48,640]{4,3,1,0,2:T(8,128)(2,1)S(1)}, u32[]{:S(2)}, u32[]{:S(2)}) collective-permute-start(bf16[2,2,1,48,640]{4,3,1,0,2:T(8,128)(2,1)S(1)} %fusion.16), channel_id=1, source_target_pairs={{0,2},{2,0},{4,6},{6,4},{8,10},{10,8},{12,14},{14,12},{16,18},{18,... | collective-permute-start | bytes 737288 | tf_op jit(solution)/shard_map/ppermute | solution.py:820
  35.4 15.1 %collective-permute-start.6 = (bf16[2,2,2,1,48,512]{5,4,2,1,0,3:T(8,128)(2,1)S(1)}, bf16[2,2,2,1,48,512]{5,4,2,1,0,3:T(8,128)(2,1)S(1)}, u32[]{:S(2)}, u32[]{:S(2)}) collective-permute-start(bf16[2,2,2,1,48,512]{5,4,2,1,0,3:T(8,128)(2,1)S(1)} %fusion.4), channel_id=1, source_target_pairs={{0,2},{2,0},{4,6},{6,4},{8,10},{10,8},{12,14},{14,12},{16,18},{18,... | collective-permute-start | bytes 1179656 | tf_op jit(solution)/shard_map/ppermute | solution.py:820
  41.8 12.8 %collective-permute-start.4 = (bf16[2,2,2,1,48,640]{5,4,2,1,0,3:T(8,128)(2,1)S(1)}, bf16[2,2,2,1,48,640]{5,4,2,1,0,3:T(8,128)(2,1)S(1)}, u32[]{:S(2)}, u32[]{:S(2)}) collective-permute-start(bf16[2,2,2,1,48,640]{5,4,2,1,0,3:T(8,128)(2,1)S(1)} %fusion.3), channel_id=1, source_target_pairs={{0,4},{2,6},{4,0},{6,2},{8,12},{10,14},{12,8},{14,10},{16,20},{18,... | collective-permute-start | bytes 1474568 | tf_op jit(solution)/shard_map/ppermute | solution.py:820
  57.4 34.9 %copy-start.6 = (f32[768]{0:T(1024)S(1)}, f32[768]{0:T(1024)}, u32[]{:S(2)}) copy-start(f32[768]{0:T(1024)} %param.20) | copy-start | bytes 9220
  57.4 35.5 %copy-start.7 = (f32[768]{0:T(1024)S(1)}, f32[768]{0:T(1024)}, u32[]{:S(2)}) copy-start(f32[768]{0:T(1024)} %param.21) | copy-start | bytes 9220
  92.3 2.6 collective-permute-start.7
  152.1 13.7 %collective-permute-start.8 = (bf16[768,3456]{1,0:T(8,128)(2,1)}, bf16[768,3456]{1,0:T(8,128)(2,1)S(1)}, u32[]{:S(2)}, u32[]{:S(2)}) collective-permute-start(bf16[768,3456]{1,0:T(8,128)(2,1)} %bitcast.117), channel_id=1, source_target_pairs={{0,1},{1,0},{2,3},{3,2},{4,5},{5,4},{6,7},{7,6},{8,9},{9,8},{10,11... | collective-permute-start | bytes 15925256 | tf_op jit(solution)/shard_map/ppermute | solution.py:815
  152.4 19.5 %collective-permute-start.9 = (bf16[1024,384]{1,0:T(8,128)(2,1)}, bf16[1024,384]{1,0:T(8,128)(2,1)S(1)}, u32[]{:S(2)}, u32[]{:S(2)}) collective-permute-start(bf16[1024,384]{1,0:T(8,128)(2,1)} %get-tuple-element.80), channel_id=1, source_target_pairs={{0,1},{1,0},{2,3},{3,2},{4,5},{5,4},{6,7},{7,6},{8,9},{9,8},{10,11... | collective-permute-start | bytes 2359304 | tf_op jit(solution)/shard_map/ppermute | solution.py:815
  171.9 99.3 %reduce-scatter.5.cloned.1.call-start = ((), (), s32[]{:S(2)}) async-start(), calls=%async_computation.4 | async-start | bytes 1658880 | tf_op jit(solution)/shard_map/reduce_scatter | solution.py:938
  172.7 1.2 collective-permute-start.10
  232.7 13.3 %collective-permute-start.11 = (bf16[208,1152]{1,0:T(8,128)(2,1)}, bf16[208,1152]{1,0:T(8,128)(2,1)S(1)}, u32[]{:S(2)}, u32[]{:S(2)}) collective-permute-start(bf16[208,1152]{1,0:T(8,128)(2,1)} %get-tuple-element.90), channel_id=1, source_target_pairs={{0,2},{2,0},{4,6},{6,4},{8,10},{10,8},{12,14},{14,12},{16,18},{18,... | collective-permute-start | bytes 1437704 | tf_op jit(solution)/shard_map/ppermute | solution.py:820
  234.1 11.8 %collective-permute-start.12 = (bf16[192,1152]{1,0:T(8,128)(2,1)}, bf16[192,1152]{1,0:T(8,128)(2,1)S(1)}, u32[]{:S(2)}, u32[]{:S(2)}) collective-permute-start(bf16[192,1152]{1,0:T(8,128)(2,1)} %get-tuple-element.91), channel_id=1, source_target_pairs={{0,4},{2,6},{4,0},{6,2},{8,12},{10,14},{12,8},{14,10},{16,20},{18,... | collective-permute-start | bytes 1327112 | tf_op jit(solution)/shard_map/ppermute | solution.py:820
  246.0 16.4 %collective-permute-start.13 = (bf16[1024,768]{1,0:T(8,128)(2,1)}, bf16[1024,768]{1,0:T(8,128)(2,1)S(1)}, u32[]{:S(2)}, u32[]{:S(2)}) collective-permute-start(bf16[1024,768]{1,0:T(8,128)(2,1)} %get-tuple-element.97), channel_id=1, source_target_pairs={{0,1},{1,0},{2,3},{3,2},{4,5},{5,4},{6,7},{7,6},{8,9},{9,8},{10,11... | collective-permute-start | bytes 4718600 | tf_op jit(solution)/shard_map/ppermute | solution.py:815
  246.9 8.7 %collective-permute-start.14 = (bf16[112,1152]{1,0:T(8,128)(2,1)S(1)}, bf16[112,1152]{1,0:T(8,128)(2,1)S(1)}, u32[]{:S(2)}, u32[]{:S(2)}) collective-permute-start(bf16[112,1152]{1,0:T(8,128)(2,1)S(1)} %get-tuple-element.108), channel_id=1, source_target_pairs={{0,4},{2,6},{4,0},{6,2},{8,12},{10,14},{12,8},{14,10},{16,20},{18,... | collective-permute-start | bytes 774152 | tf_op jit(solution)/shard_map/ppermute | solution.py:820
  248.0 7.5 %collective-permute-start.15 = (bf16[96,1152]{1,0:T(8,128)(2,1)S(1)}, bf16[96,1152]{1,0:T(8,128)(2,1)S(1)}, u32[]{:S(2)}, u32[]{:S(2)}) collective-permute-start(bf16[96,1152]{1,0:T(8,128)(2,1)S(1)} %get-tuple-element.110), channel_id=1, source_target_pairs={{0,2},{2,0},{4,6},{6,4},{8,10},{10,8},{12,14},{14,12},{16,18},{18,... | collective-permute-start | bytes 663560 | tf_op jit(solution)/shard_map/ppermute | solution.py:820
  256.4 16.6 %collective-permute-start.16 = (bf16[64,1152]{1,0:T(8,128)(2,1)S(1)}, bf16[64,1152]{1,0:T(8,128)(2,1)S(1)}, u32[]{:S(2)}, u32[]{:S(2)}) collective-permute-start(bf16[64,1152]{1,0:T(8,128)(2,1)S(1)} %get-tuple-element.114), channel_id=1, source_target_pairs={{0,8},{8,16},{16,24},{24,0},{1,9},{9,17},{17,25},{25,1},{2,10},{10... | collective-permute-start | bytes 442376 | tf_op jit(solution)/shard_map/ppermute | solution.py:785
  259.5 15.5 %collective-permute-start.17 = (bf16[64,1152]{1,0:T(8,128)(2,1)S(1)}, bf16[64,1152]{1,0:T(8,128)(2,1)S(1)}, u32[]{:S(2)}, u32[]{:S(2)}) collective-permute-start(bf16[64,1152]{1,0:T(8,128)(2,1)S(1)} %get-tuple-element.115), channel_id=1, source_target_pairs={{0,16},{8,24},{16,0},{24,8},{1,17},{9,25},{17,1},{25,9},{2,18},{10... | collective-permute-start | bytes 442376 | tf_op jit(solution)/shard_map/ppermute | solution.py:785
  260.3 14.7 %collective-permute-start.18 = (bf16[64,1152]{1,0:T(8,128)(2,1)S(1)}, bf16[64,1152]{1,0:T(8,128)(2,1)S(1)}, u32[]{:S(2)}, u32[]{:S(2)}) collective-permute-start(bf16[64,1152]{1,0:T(8,128)(2,1)S(1)} %get-tuple-element.116), channel_id=1, source_target_pairs={{0,24},{8,0},{16,8},{24,16},{1,25},{9,1},{17,9},{25,17},{2,26},{10... | collective-permute-start | bytes 442376 | tf_op jit(solution)/shard_map/ppermute | solution.py:785
  (9 other events, 82.6 us)
Sparse Core Ops, SparseCore 0:
  11.5 96.9 all-gather.1
  172.0 60.5 reduce-scatter.2
  235.0 36.1 reduce-scatter.4

commit v6 on v5

--- a/solution.py
+++ b/solution.py
@@ -190,7 +190,7 @@
 
 def backward_kernel(sched, q_ref, k_ref, v_ref, cos_ref, sin_ref, start_ref, lse_ref,
                     o_oth_ref, o_own_ref, g_oth_ref, g_own_ref, x_own_ref, x_oth_ref,
-                    gains_ref, all_ref, *rest, bq, bk, sub, blocks, share):
+                    gains_ref, gains_oth_ref, all_ref, *rest, bq, bk, sub, blocks, share):
     step = pl.program_id(1)
     half = blocks // 2
     i = lax.rem(step + (1 - sched[0]) * half, blocks)
@@ -286,7 +286,8 @@
         if share is None:
             dw_refs[0][...] = total
         else:
-            part_rows(total, gains_ref[0:2, :], sched[BIT_X], sched[BIT_Y], *dw_refs, share)
+            gains = gains_ref[0:2, :] + gains_oth_ref[0:2, :]
+            part_rows(total, gains, sched[BIT_X], sched[BIT_Y], *dw_refs, share)
 
 
 def encode(value):
@@ -322,7 +323,7 @@
 
 
 def attend_backward(sched, qkv, cosine, sine, start, lse, o_oth, o_own, g_oth, g_own, x_own, x_oth,
-                    gains, bq, bk, share, sub=256):
+                    gains, gains_oth, bq, bk, share, sub=256):
     slots, cols = qkv.shape[0], qkv.shape[1] // 3
     pairs, blocks = cols // PAIR, slots // bq
     local, width = x_own.shape
@@ -352,6 +353,7 @@
                 pl.BlockSpec((None, 2, bq), lambda p, n, s: (p, 0, place(n, s))),
                 oth, own, oth, own, rows, rows,
                 pl.BlockSpec((8, 3 * PAIR), lambda p, n, s: (0, p)),
+                pl.BlockSpec((8, 3 * PAIR), lambda p, n, s: (0, p)),
             ],
             out_specs=[pl.BlockSpec((slots, 3 * PAIR), lambda p, n, s: (0, p)), *dw_specs],
             scratch_shapes=[
@@ -365,7 +367,8 @@
         cost_estimate=cost(10 * slots * slots * cols + 6 * slots * width * cols,
                            20 * slots * cols, slots * slots * 6),
         name="attend_backward",
-    )(sched, qkv, qkv, qkv, cosine, sine, start, lse, o_oth, o_own, g_oth, g_own, x_own, x_oth, gains)
+    )(sched, qkv, qkv, qkv, cosine, sine, start, lse, o_oth, o_own, g_oth, g_own, x_own, x_oth,
+      gains, gains_oth)
 
 
 def feed_kernel(sched, x_ref, own_ref, oth_ref, dy_ref, w_hbm, ga_ref, gf_ref,
@@ -575,10 +578,10 @@
         ],
         out_specs=out_spec,
         out_shape=jax.ShapeDtypeStruct((*shape, total), BF16),
-        compiler_params=params(),
+        compiler_params=params(48 * 1024 * 1024),
         cost_estimate=cost(2 * local * width * total, 2 * local * (4 * width + 3 * hid)),
         name="own_grads",
-    )(left, right, d_attn, mixed)
+    )(*[pltpu.with_memory_space_constraint(value, pltpu.HBM) for value in (left, right, d_attn, mixed)])
     return by_near(grads, share, near)
 
 
@@ -688,6 +691,25 @@
     )(sched, d_qkv, weights, d_first)
 
 
+def add_kernel(left_ref, right_ref, out_ref):
+    out_ref[...] = add(left_ref[...], right_ref[...]).astype(BF16)
+
+
+def add_rows(left, right, parts=4):
+    rows, cols = left.shape
+    spec = pl.BlockSpec((rows // parts, cols), lambda n: (n, 0))
+    return pl.pallas_call(
+        add_kernel,
+        grid=(parts,),
+        in_specs=[spec, spec],
+        out_specs=spec,
+        out_shape=jax.ShapeDtypeStruct(left.shape, BF16),
+        compiler_params=params(),
+        cost_estimate=cost(rows * cols, 8 * rows * cols),
+        name="add_rows",
+    )(left, right)
+
+
 def finish_kernel(total_ref, gate_ref, up_ref, down_ref, out_ref):
     hid = gate_ref.shape[1]
     gate_ref[...] = total_ref[:, 0:hid].astype(F32)
@@ -726,7 +748,7 @@
     return left.astype(F32) + right.astype(F32)
 
 
-def near_kernel(sched, keep_a, got_a, keep_b, got_b, gains, next_a, send_a, next_b, send_b, total,
+def near_kernel(sched, keep_a, got_a, keep_b, got_b, gains, gains_oth, next_a, send_a, next_b, send_b, total,
                 *, share):
     size = next_a.shape[0]
     for held, got, bit, stay, go in ((keep_a, got_a, sched[BIT_Y], next_a, send_a),
@@ -737,7 +759,7 @@
             other = pl.ds(pl.multiple_of((2 * n + 1 - bit) * share, share), share)
             stay[here] = add(held[mine], got[mine]).astype(BF16)
             go[here] = add(held[other], got[other]).astype(BF16)
-    total[...] = gains[0:2, :] + decode(got_a[2 * size:])
+    total[...] = gains[0:2, :] + gains_oth[0:2, :] + decode(got_a[2 * size:])
     send_a[size:] = encode(total[...])
 
 
@@ -761,8 +783,8 @@
 
 
 def last_kernel(sched, own, gains, *rest):
-    got, outs, total = rest[:-4], rest[-4:-1], rest[-1]
-    value, share, far = own[...], own.shape[0], 1 + len(rest[:-4])
+    got, outs, totals = rest[:-5], rest[-5:-2], rest[-2:]
+    value, share, far = own[...], own.shape[0], 1 + len(got)
     arrived = [gains[...]]
     for piece in got:
         value = value + piece[:share].astype(F32)
@@ -777,7 +799,8 @@
         for k in range(1, far):
             term = jnp.where(shift == k, arrived[k], term)
         summed = term if summed is None else summed + term
-    total[...] = summed
+    for row, total in enumerate(totals):
+        total[...] = summed[row, :total.shape[0]]
 
 
 def shifted(value, shift):
@@ -785,7 +808,7 @@
     return lax.ppermute(value, "far", [(at, (at + shift) % far) for at in range(far)])
 
 
-def sum_parts(sched, share, keep_a, send_a, keep_b, send_b, gains, meanwhile):
+def sum_parts(sched, share, keep_a, send_a, keep_b, send_b, gains, gains_oth, meanwhile):
     size, width = keep_a.shape
     far = lax.axis_size("far")
     got_a, got_b = flip(send_a, 0), flip(send_b, 1)
@@ -794,7 +817,7 @@
     sizes = [size // 2, size // 2 + EXTRA, size // 2, size // 2]
     keep_a, send_a, keep_b, send_b, gains = whole_call(
         partial(near_kernel, share=share), "near_sums", sched,
-        (keep_a, got_a, keep_b, got_b, gains),
+        (keep_a, got_a, keep_b, got_b, gains, gains_oth),
         [((rows, width), BF16) for rows in sizes] + [((2, width), F32)])
     got_a, got_b = flip(send_a, 1), flip(send_b, 0)
     own, gains, *sends = whole_call(
@@ -804,11 +827,12 @@
     return (own, gains, *got), beside
 
 
-def last_sums(sched, own, gains, *got):
+def last_sums(sched, own, gains, *got, features):
     share, width = own.shape
-    *dw, gains = whole_call(last_kernel, "last_sums", sched, (own, gains, *got),
-                            [((share, width // 3), F32)] * 3 + [(gains.shape, F32)])
-    return dw, gains
+    *dw, gain_attn, gain_ffn = whole_call(
+        last_kernel, "last_sums", sched, (own, gains, *got),
+        [((share, width // 3), F32)] * 3 + [((features,), F32)] * 2)
+    return dw, (gain_attn, gain_ffn)
 
 
 def exchange(value):
@@ -916,31 +940,33 @@
     other_grads = exchange(grads)
     grads = own_grads(left, right, d_attn, mixed_own, share, lax.axis_size("near"))
     grads = (grads.astype(F32) + other_grads.astype(F32)).astype(BF16)
-    grads, g_oth = lax.optimization_barrier((grads, g_oth))
+    gains_oth = exchange(gains)
+    grads, g_oth, gains_oth = lax.optimization_barrier((grads, g_oth, gains_oth))
     reduced = lax.psum_scatter(grads, "near", scatter_dimension=0, tiled=True)
-    gains = gains + exchange(gains)
     parted = share % 16 == 0 and lax.axis_size("near") == 4 and lax.axis_size("far") % 2 == 0
     d_qkv, *dw = attend_backward(sched, qkv, cosine, sine, start, lse, mixed_send, mixed_own,
-                                 g_oth, g_own, tokens, other_x, gains, bq, bk // 2,
+                                 g_oth, g_own, tokens, other_x, gains, gains_oth, bq, bk // 2,
                                  share if parted else None)
     d_qkv, reduced, *dw = lax.optimization_barrier((d_qkv, reduced, *dw))
     into_input = partial(input_grads, sched, d_qkv, full_qkv, d_first, 512)
     if parted:
-        last, (x_send, x_own) = sum_parts(sched, share, *dw, gains, into_input)
+        last, (x_send, x_own) = sum_parts(sched, share, *dw, gains, gains_oth, into_input)
     else:
         x_send, x_own = into_input()
         fore, back = bit_orders(count)
         dw = jnp.concatenate([scatter_rows(dw[0][:, :edge], fore[::-1]),
                               scatter_rows(dw[0][:, edge:], back[::-1])], axis=1).astype(F32)
         dw = dw.reshape(share, cols // PAIR, 3, PAIR).transpose(2, 0, 1, 3).reshape(3, share, cols)
+        gains = gains + gains_oth
         for bit in range(count.bit_length() - 1):
             gains = gains + flip(gains, bit)
+        gains = gains[0, :width], gains[1, :width]
     reduced = lax.psum_scatter(reduced, "far", scatter_dimension=0, tiled=True)
-    input_grad = (x_own + exchange(x_send).astype(F32)).astype(BF16)
+    input_grad = add_rows(x_own, exchange(x_send))
     ready = (input_grad, *finish(reduced, hid))
     if parted:
         ready, last = lax.optimization_barrier((ready, last))
-        dw, gains = last_sums(sched, *last)
+        dw, gains = last_sums(sched, *last, features=width)
     input_grad, grad_gate, grad_up, grad_down, grad_out = ready
     return (
         output,
@@ -952,8 +978,7 @@
         grad_gate,
         grad_up,
         grad_down,
-        gains[0, :width],
-        gains[1, :width],
+        *gains,
     )
 
 

time: 285 us -> 282 us (0.989)
  Pallas kernels: 153 us -> 160 us
  other arithmetic: 23 us -> 16.9 us
  waiting for transfers between devices: 66.7 us -> 62.2 us
    pallas_call x0 -> x1, Pallas kernels: none -> 4.18 us  [add_rows(): pl.pallas_call(add_kernel, grid=(parts,), in_specs=[spec, spec], out_spec...]
    pallas_call x1, Pallas kernels: 46.3 us -> 50 us  [attend_backward(): pl.pallas_call(partial(backward_kernel, bq=bq, bk=bk, sub=sub, blocks=blo...]
    convert_element_type x1 -> x0, other arithmetic: 3.37 us -> none  [local(): input_grad = (x_own + exchange(x_send).astype(F32)).astype(BF16)]
  transfers between devices with their start and end apart: 22 -> 22, of which waited for: 14 -> 13; matrix products, arithmetic and copies ran while one was open for 9% -> 7% of each run, Pallas kernels for 38% -> 41%
where the time goes in v6:
time: 282 us; the launch traced here: 280 us
  Pallas kernels  160 us (57%)
  waiting for transfers between devices  62.2 us (22%)
  starting transfers between devices  20.4 us (7%)
  other arithmetic  16.9 us (6%)
  between operations  14 us (5%)
  local copies, waits for them, and re-layouts  6.35 us (2%)
    pallas_call x1, Pallas kernels, attend_backward(): pl.pallas_call(partial(backward_kernel, bq=bq, bk=bk, sub=sub, blocks=blo...  50 us
    pallas_call x1, Pallas kernels, feed(): pl.pallas_call(partial(feed_kernel, block=block, sub=sub, chunk=chunk, lo...  43.6 us
    pallas_call x1, Pallas kernels, attend_forward(): pl.pallas_call(partial(forward_kernel, bq=bq, bk=bk, sub=sub, chunk=chunk...  34.8 us
    ppermute x10, waiting for transfers between devices, flip(): return lax.ppermute(value, DP, [(at, at ^ 1 << bit) for at in range(count)])  31.3 us
    ppermute x10, starting transfers between devices, flip(): return lax.ppermute(value, DP, [(at, at ^ 1 << bit) for at in range(count)])  14 us
    all_gather x1, waiting for transfers between devices, local(): feed_w = lax.all_gather(packed, ('tensor',) + DP, axis=0, tiled=True)  13.7 us
    pallas_call x1, Pallas kernels, own_grads(): pl.pallas_call(partial(own_grads_kernel, tiles=tiles, share=share if pack...  12.4 us
    pallas_call x1, Pallas kernels, input_grads(): pl.pallas_call(partial(input_grad_kernel, half=half), grid_spec=pltpu.Pre...  10.4 us
  transfers between devices with their start and end apart: 22, of which 13 were waited for; matrix products, arithmetic and copies ran while one was open for 7% of the time, Pallas kernels for 41%

profile of v6, /device:TPU:0, one launch (start us, length us, event | category | flops | bytes accessed | tf_op | source)
XLA Modules:
  0.0 280.2 jit_solution(248746725156882873)
XLA Ops:
  7.2 1.8 pad_maximum_fusion.3
  9.9 4.1 %collective-permute-start.1 = (bf16[1,48,1152]{2,1,0:T(8,128)(2,1)S(1)}, bf16[1,48,1152]{2,1,0:T(8,128)(2,1)S(1)}, u32[]{:S(2)}, u32[]{:S(2)}) collective-permute-start(bf16[1,48,1152]{2,1,0:T(8,128)(2,1)S(1)} %maximum_bitcast_fusion.2), channel_id=1, source_target_pairs={{0,16},{2,18},{4,20},{6,22},{8,24},{10,26},{12,28},{14,30},{16,0},... | collective-permute-start | bytes 331784 | tf_op jit(solution)/shard_map/ppermute | solution.py:844
  15.6 3.8 %collective-permute-done.1 = bf16[1,48,1152]{2,1,0:T(8,128)(2,1)S(1)} collective-permute-done((bf16[1,48,1152]{2,1,0:T(8,128)(2,1)S(1)}, bf16[1,48,1152]{2,1,0:T(8,128)(2,1)S(1)}, u32[]{:S(2)}, u32[]{:S(2)}) %collective-permute-start.1) | collective-permute-done | bytes 110624 | tf_op jit(solution)/shard_map/ppermute | solution.py:844
  21.1 5.6 %negate_select_fusion = (f32[2048,128]{1,0:T(8,128)}, f32[2048,128]{1,0:T(8,128)}) fusion(f32[128]{0:T(128)S(1)} %fusion.14, f32[2048]{0:T(1024)S(1)} %subtract_convert_fusion, pred[128]{0:T(512)(128)(4,1)S(1)} %broadcast_compare_fusion), kind=kLoop, calls=%fused_computation.3 | loop fusion | flops 786432 | bytes 2105984 | tf_op jit(solution)/shard_map/jit(_where)/select_n | solution.py:925
  26.8 2.6 collective-permute-done.2
  32.7 1.6 collective-permute-start.3
  36.7 5.0 %collective-permute-done.3 = bf16[2,2,1,48,640]{4,3,1,0,2:T(8,128)(2,1)S(1)} collective-permute-done((bf16[2,2,1,48,640]{4,3,1,0,2:T(8,128)(2,1)S(1)}, bf16[2,2,1,48,640]{4,3,1,0,2:T(8,128)(2,1)S(1)}, u32[]{:S(2)}, u32[]{:S(2)}) %collective-permute-start.3) | collective-permute-done | bytes 245792 | tf_op jit(solution)/shard_map/ppermute | solution.py:844
  42.6 8.0 %collective-permute-done.6 = bf16[2,2,2,1,48,512]{5,4,2,1,0,3:T(8,128)(2,1)S(1)} collective-permute-done((bf16[2,2,2,1,48,512]{5,4,2,1,0,3:T(8,128)(2,1)S(1)}, bf16[2,2,2,1,48,512]{5,4,2,1,0,3:T(8,128)(2,1)S(1)}, u32[]{:S(2)}, u32[]{:S(2)}) %collective-permute-start.6) | collective-permute-done | bytes 393248 | tf_op jit(solution)/shard_map/ppermute | solution.py:844
  50.8 3.8 %collective-permute-done.4 = bf16[2,2,2,1,48,640]{5,4,2,1,0,3:T(8,128)(2,1)S(1)} collective-permute-done((bf16[2,2,2,1,48,640]{5,4,2,1,0,3:T(8,128)(2,1)S(1)}, bf16[2,2,2,1,48,640]{5,4,2,1,0,3:T(8,128)(2,1)S(1)}, u32[]{:S(2)}, u32[]{:S(2)}) %collective-permute-start.4) | collective-permute-done | bytes 491552 | tf_op jit(solution)/shard_map/ppermute | solution.py:844
  57.5 34.8 %attend_forward.1 = (bf16[2048,1152]{1,0:T(8,128)(2,1)}, bf16[1024,384]{1,0:T(8,128)(2,1)}, bf16[1024,384]{1,0:T(8,128)(2,1)}, f32[3,2,2048]{2,1,0:T(2,128)}) custom-call(s32[9]{0:T(128)} %concatenate.12.sched, bf16[1024,768]{1,0:T(8,128)(2,1)} %x_own_ref.1, bf16[1024,768]{1,0:T(8,128)(2,1)} %copy-done.10, ...), custom_call_target="tpu_custom_call" | custom-call | flops 10066329600 | bytes 12582912 | tf_op jit(solution)/shard_map/attend_forward/pallas_call | solution.py:158
  94.8 13.7 %all-gather.2.cloned.1.call-done = bf16[1536,3456]{1,0:T(8,128)(2,1)} async-done(((bf16[48,3456]{1,0:T(8,128)(2,1)}), bf16[1536,3456]{1,0:T(8,128)(2,1)}) %all-gather.2.cloned.1.call-update) | async-done | bytes 10616848 | tf_op jit(solution)/shard_map/all_gather | solution.py:910
  108.5 43.6 %feed.1 = (bf16[1024,768]{1,0:T(8,128)(2,1)}, f32[1024,768]{1,0:T(8,128)}, bf16[1024,384]{1,0:T(8,128)(2,1)}, bf16[1024,384]{1,0:T(8,128)(2,1)}, bf16[4,4,48,345...) custom-call(s32[9]{0:T(128)} %concatenate.12.sched, ...), custom_call_target="tpu_custom_call" | custom-call | flops 32614907904 | bytes 23592960 | tf_op jit(solution)/shard_map/feed/pallas_call | solution.py:623
  153.0 12.4 %own_grads.1 = bf16[4,4,48,3456]{3,2,1,0:T(8,128)(2,1)S(1)} custom-call(bf16[2,1024,768]{2,1,0:T(8,128)(2,1)} %get-tuple-element.78.left_ref, bf16[3,1024,1024]{2,1,0:T(8,128)(2,1)} %get-tuple-element.79.right_ref, bf16[1024,768]{1,0:T(8,128)(2,1)} %get-tuple-element.80.dattn_ref, bf16[1024,384]{1,0:T(8,128)(2,1)} %get-tuple-element.73.own_ref.mixed_ref.o_own_ref), custom_call_target="tpu_custom_call" | custom-call | flops 5435817984 | bytes 12582912 | tf_op jit(solution)/shard_map/own_grads/pallas_call | solution.py:570
  165.4 4.0 %fusion = bf16[768,3456]{1,0:T(8,128)(2,1)} fusion(bf16[768,3456]{1,0:T(8,128)(2,1)S(1)} %collective-permute-done.8, bf16[4,4,48,3456]{3,2,1,0:T(8,128)(2,1)S(1)} %own_grads.1), kind=kLoop, calls=%fused_computation.1 | loop fusion | flops 10616832 | bytes 15925248 | tf_op jit(solution)/shard_map/convert_element_type | solution.py:942
  170.3 50.0 %attend_backward.1 = (bf16[2048,1152]{1,0:T(8,128)(2,1)}, bf16[192,1152]{1,0:T(8,128)(2,1)}, bf16[208,1152]{1,0:T(8,128)(2,1)}, bf16[192,1152]{1,0:T(8,128)(2,1)}, bf16[192,1152]{1,0:T(8,128)(2,1)}) custom-call(s32[9]{0:T(128)} %concatenate.12.sched, bf16[2048,1152]{1,0:T(8,128)(2,1)} %get-tuple-element.76.q_ref.k_ref.v_ref, ...), custom_call_target="tpu_custom_call" | custom-call | flops 19730006016 | bytes 15728640 | tf_op jit(solution)/shard_map/attend_backward/pallas_call | solution.py:342
  220.3 9.9 %reduce-scatter.3.cloned.1.call-done = bf16[192,3456]{1,0:T(8,128)(2,1)} async-done(((bf16[768,3456]{1,0:T(8,128)(2,1)}), bf16[192,3456]{1,0:T(8,128)(2,1)}) %reduce-scatter.3.cloned.1.call-update) | async-done | bytes 1327120 | tf_op jit(solution)/shard_map/reduce_scatter | solution.py:945
  232.3 10.4 %input_grads.1 = (bf16[1024,768]{1,0:T(8,128)(2,1)}, f32[1024,768]{1,0:T(8,128)}) custom-call(s32[9]{0:T(128)} %concatenate.12.sched, bf16[2048,1152]{1,0:T(8,128)(2,1)} %get-tuple-element.95.d_ref, bf16[768,1152]{1,0:T(8,128)(2,1)} %pad_maximum_fusion.wq_ref.wk_ref.wv_ref.w_ref, f32[1024,768]{1,0:T(8,128)} %get-tuple-element.96.dfirst_ref), custom_call_target="tpu_custom_call" | custom-call | flops 3623878656 | bytes 7864320 | tf_op jit(solution)/shard_map/input_grads/pallas_call | solution.py:677
  246.4 6.6 %collective-permute-done.15.got_b = bf16[96,1152]{1,0:T(8,128)(2,1)S(1)} collective-permute-done((bf16[96,1152]{1,0:T(8,128)(2,1)S(1)}, bf16[96,1152]{1,0:T(8,128)(2,1)S(1)}, u32[]{:S(2)}, u32[]{:S(2)}) %collective-permute-start.15) | collective-permute-done | bytes 221216 | tf_op jit(solution)/shard_map/ppermute | solution.py:844
  253.9 1.6 collective-permute-start.16
  255.4 2.4 collective-permute-start.17
  260.4 4.2 %add_rows.1 = bf16[1024,768]{1,0:T(8,128)(2,1)} custom-call(f32[1024,768]{1,0:T(8,128)} %get-tuple-element.99.left_ref, bf16[1024,768]{1,0:T(8,128)(2,1)} %copy-done.6), custom_call_target="tpu_custom_call" | custom-call | flops 786432 | bytes 6291456 | tf_op jit(solution)/shard_map/add_rows/pallas_call | solution.py:701
  264.6 4.1 %reduce-scatter.5.cloned.1.call-done.total_ref = bf16[48,3456]{1,0:T(8,128)(2,1)} async-done(((bf16[192,3456]{1,0:T(8,128)(2,1)}), bf16[48,3456]{1,0:T(8,128)(2,1)}) %reduce-scatter.5.cloned.1.call-update) | async-done | bytes 331792 | tf_op jit(solution)/shard_map/reduce_scatter | solution.py:964
  268.7 1.8 finish.1
  270.5 1.9 collective-permute-done.17.rest_1_
  (95 shorter events, 28.7 us)
Async XLA Ops:
  7.2 101.4 %all-gather.2.cloned.1.call-start = ((), (), s32[]{:S(2)}) async-start(), calls=%async_computation.2 | async-start | bytes 10948608 | tf_op jit(solution)/shard_map/all_gather | solution.py:910
  9.0 221.2 %reduce-scatter.3.cloned.1.call-start = ((), (), s32[]{:S(2)}) async-start(), calls=%async_computation.3 | async-start | bytes 6635520 | tf_op jit(solution)/shard_map/reduce_scatter | solution.py:945
  9.9 9.5 %collective-permute-start.1 = (bf16[1,48,1152]{2,1,0:T(8,128)(2,1)S(1)}, bf16[1,48,1152]{2,1,0:T(8,128)(2,1)S(1)}, u32[]{:S(2)}, u32[]{:S(2)}) collective-permute-start(bf16[1,48,1152]{2,1,0:T(8,128)(2,1)S(1)} %maximum_bitcast_fusion.2), channel_id=1, source_target_pairs={{0,16},{2,18},{4,20},{6,22},{8,24},{10,26},{12,28},{14,30},{16,0},... | collective-permute-start | bytes 331784 | tf_op jit(solution)/shard_map/ppermute | solution.py:844
  14.0 42.3 %collective-permute-start = (bf16[1024,768]{1,0:T(8,128)(2,1)}, bf16[1024,768]{1,0:T(8,128)(2,1)S(1)}, u32[]{:S(2)}, u32[]{:S(2)}) collective-permute-start(bf16[1024,768]{1,0:T(8,128)(2,1)} %x_own_ref.1), channel_id=1, source_target_pairs={{0,1},{1,0},{2,3},{3,2},{4,5},{5,4},{6,7},{7,6},{8,9},{9,8},{10,11... | collective-permute-start | bytes 4718600 | tf_op jit(solution)/shard_map/ppermute | solution.py:839
  20.3 9.1 %collective-permute-start.2 = (bf16[2,1,48,1152]{3,2,0,1:T(8,128)(2,1)S(1)}, bf16[2,1,48,1152]{3,2,0,1:T(8,128)(2,1)S(1)}, u32[]{:S(2)}, u32[]{:S(2)}) collective-permute-start(bf16[2,1,48,1152]{3,2,0,1:T(8,128)(2,1)S(1)} %fusion.9), channel_id=1, source_target_pairs={{0,8},{2,10},{4,12},{6,14},{8,0},{10,2},{12,4},{14,6},{16,24},{18,... | collective-permute-start | bytes 663560 | tf_op jit(solution)/shard_map/ppermute | solution.py:844
  29.5 5.7 %collective-permute-start.5 = (bf16[2,2,1,48,512]{4,3,1,0,2:T(8,128)(2,1)S(1)}, bf16[2,2,1,48,512]{4,3,1,0,2:T(8,128)(2,1)S(1)}, u32[]{:S(2)}, u32[]{:S(2)}) collective-permute-start(bf16[2,2,1,48,512]{4,3,1,0,2:T(8,128)(2,1)S(1)} %fusion.10), channel_id=1, source_target_pairs={{0,4},{2,6},{4,0},{6,2},{8,12},{10,14},{12,8},{14,10},{16,20},{18,... | collective-permute-start | bytes 589832 | tf_op jit(solution)/shard_map/ppermute | solution.py:844
  32.7 9.0 %collective-permute-start.3 = (bf16[2,2,1,48,640]{4,3,1,0,2:T(8,128)(2,1)S(1)}, bf16[2,2,1,48,640]{4,3,1,0,2:T(8,128)(2,1)S(1)}, u32[]{:S(2)}, u32[]{:S(2)}) collective-permute-start(bf16[2,2,1,48,640]{4,3,1,0,2:T(8,128)(2,1)S(1)} %fusion.16), channel_id=1, source_target_pairs={{0,2},{2,0},{4,6},{6,4},{8,10},{10,8},{12,14},{14,12},{16,18},{18,... | collective-permute-start | bytes 737288 | tf_op jit(solution)/shard_map/ppermute | solution.py:844
  35.4 15.2 %collective-permute-start.6 = (bf16[2,2,2,1,48,512]{5,4,2,1,0,3:T(8,128)(2,1)S(1)}, bf16[2,2,2,1,48,512]{5,4,2,1,0,3:T(8,128)(2,1)S(1)}, u32[]{:S(2)}, u32[]{:S(2)}) collective-permute-start(bf16[2,2,2,1,48,512]{5,4,2,1,0,3:T(8,128)(2,1)S(1)} %fusion.4), channel_id=1, source_target_pairs={{0,2},{2,0},{4,6},{6,4},{8,10},{10,8},{12,14},{14,12},{16,18},{18,... | collective-permute-start | bytes 1179656 | tf_op jit(solution)/shard_map/ppermute | solution.py:844
  41.8 12.8 %collective-permute-start.4 = (bf16[2,2,2,1,48,640]{5,4,2,1,0,3:T(8,128)(2,1)S(1)}, bf16[2,2,2,1,48,640]{5,4,2,1,0,3:T(8,128)(2,1)S(1)}, u32[]{:S(2)}, u32[]{:S(2)}) collective-permute-start(bf16[2,2,2,1,48,640]{5,4,2,1,0,3:T(8,128)(2,1)S(1)} %fusion.3), channel_id=1, source_target_pairs={{0,4},{2,6},{4,0},{6,2},{8,12},{10,14},{12,8},{14,10},{16,20},{18,... | collective-permute-start | bytes 1474568 | tf_op jit(solution)/shard_map/ppermute | solution.py:844
  57.5 34.9 %copy-start.8 = (f32[768]{0:T(1024)S(1)}, f32[768]{0:T(1024)}, u32[]{:S(2)}) copy-start(f32[768]{0:T(1024)} %param.20) | copy-start | bytes 9220
  57.5 35.5 %copy-start.9 = (f32[768]{0:T(1024)S(1)}, f32[768]{0:T(1024)}, u32[]{:S(2)}) copy-start(f32[768]{0:T(1024)} %param.21) | copy-start | bytes 9220
  92.3 2.6 collective-permute-start.7
  152.1 13.3 %collective-permute-start.8 = (bf16[768,3456]{1,0:T(8,128)(2,1)}, bf16[768,3456]{1,0:T(8,128)(2,1)S(1)}, u32[]{:S(2)}, u32[]{:S(2)}) collective-permute-start(bf16[768,3456]{1,0:T(8,128)(2,1)} %bitcast.117), channel_id=1, source_target_pairs={{0,1},{1,0},{2,3},{3,2},{4,5},{5,4},{6,7},{7,6},{8,9},{9,8},{10,11... | collective-permute-start | bytes 15925256 | tf_op jit(solution)/shard_map/ppermute | solution.py:839
  152.4 16.9 %collective-permute-start.10 = (f32[8,1152]{1,0:T(8,128)}, f32[8,1152]{1,0:T(8,128)S(1)}, u32[]{:S(2)}, u32[]{:S(2)}) collective-permute-start(f32[8,1152]{1,0:T(8,128)} %get-tuple-element.83.gains_ref.gains), channel_id=1, source_target_pairs={{0,1},{1,0},{2,3},{3,2},{4,5},{5,4},{6,7},{7,6},{8,9},{9,8},{10,11... | collective-permute-start | bytes 110600 | tf_op jit(solution)/shard_map/ppermute | solution.py:839
  152.7 16.7 %collective-permute-start.9 = (bf16[1024,384]{1,0:T(8,128)(2,1)}, bf16[1024,384]{1,0:T(8,128)(2,1)S(1)}, u32[]{:S(2)}, u32[]{:S(2)}) collective-permute-start(bf16[1024,384]{1,0:T(8,128)(2,1)} %get-tuple-element.82), channel_id=1, source_target_pairs={{0,1},{1,0},{2,3},{3,2},{4,5},{5,4},{6,7},{7,6},{8,9},{9,8},{10,11... | collective-permute-start | bytes 2359304 | tf_op jit(solution)/shard_map/ppermute | solution.py:839
  169.4 99.3 %reduce-scatter.5.cloned.1.call-start = ((), (), s32[]{:S(2)}) async-start(), calls=%async_computation.4 | async-start | bytes 1658880 | tf_op jit(solution)/shard_map/reduce_scatter | solution.py:964
  230.2 13.2 %collective-permute-start.11 = (bf16[208,1152]{1,0:T(8,128)(2,1)}, bf16[208,1152]{1,0:T(8,128)(2,1)S(1)}, u32[]{:S(2)}, u32[]{:S(2)}) collective-permute-start(bf16[208,1152]{1,0:T(8,128)(2,1)} %get-tuple-element.93), channel_id=1, source_target_pairs={{0,2},{2,0},{4,6},{6,4},{8,10},{10,8},{12,14},{14,12},{16,18},{18,... | collective-permute-start | bytes 1437704 | tf_op jit(solution)/shard_map/ppermute | solution.py:844
  231.6 11.8 %collective-permute-start.12 = (bf16[192,1152]{1,0:T(8,128)(2,1)}, bf16[192,1152]{1,0:T(8,128)(2,1)S(1)}, u32[]{:S(2)}, u32[]{:S(2)}) collective-permute-start(bf16[192,1152]{1,0:T(8,128)(2,1)} %get-tuple-element.94), channel_id=1, source_target_pairs={{0,4},{2,6},{4,0},{6,2},{8,12},{10,14},{12,8},{14,10},{16,20},{18,... | collective-permute-start | bytes 1327112 | tf_op jit(solution)/shard_map/ppermute | solution.py:844
  243.4 15.8 %collective-permute-start.13 = (bf16[1024,768]{1,0:T(8,128)(2,1)}, bf16[1024,768]{1,0:T(8,128)(2,1)S(1)}, u32[]{:S(2)}, u32[]{:S(2)}) collective-permute-start(bf16[1024,768]{1,0:T(8,128)(2,1)} %get-tuple-element.100), channel_id=1, source_target_pairs={{0,1},{1,0},{2,3},{3,2},{4,5},{5,4},{6,7},{7,6},{8,9},{9,8},{10,11... | collective-permute-start | bytes 4718600 | tf_op jit(solution)/shard_map/ppermute | solution.py:839
  244.3 8.7 %collective-permute-start.14 = (bf16[112,1152]{1,0:T(8,128)(2,1)S(1)}, bf16[112,1152]{1,0:T(8,128)(2,1)S(1)}, u32[]{:S(2)}, u32[]{:S(2)}) collective-permute-start(bf16[112,1152]{1,0:T(8,128)(2,1)S(1)} %get-tuple-element.111), channel_id=1, source_target_pairs={{0,4},{2,6},{4,0},{6,2},{8,12},{10,14},{12,8},{14,10},{16,20},{18,... | collective-permute-start | bytes 774152 | tf_op jit(solution)/shard_map/ppermute | solution.py:844
  245.4 7.5 %collective-permute-start.15 = (bf16[96,1152]{1,0:T(8,128)(2,1)S(1)}, bf16[96,1152]{1,0:T(8,128)(2,1)S(1)}, u32[]{:S(2)}, u32[]{:S(2)}) collective-permute-start(bf16[96,1152]{1,0:T(8,128)(2,1)S(1)} %get-tuple-element.113), channel_id=1, source_target_pairs={{0,2},{2,0},{4,6},{6,4},{8,10},{10,8},{12,14},{14,12},{16,18},{18,... | collective-permute-start | bytes 663560 | tf_op jit(solution)/shard_map/ppermute | solution.py:844
  253.9 16.6 %collective-permute-start.16 = (bf16[64,1152]{1,0:T(8,128)(2,1)S(1)}, bf16[64,1152]{1,0:T(8,128)(2,1)S(1)}, u32[]{:S(2)}, u32[]{:S(2)}) collective-permute-start(bf16[64,1152]{1,0:T(8,128)(2,1)S(1)} %get-tuple-element.117), channel_id=1, source_target_pairs={{0,8},{8,16},{16,24},{24,0},{1,9},{9,17},{17,25},{25,1},{2,10},{10... | collective-permute-start | bytes 442376 | tf_op jit(solution)/shard_map/ppermute | solution.py:808
  255.4 16.9 %collective-permute-start.17 = (bf16[64,1152]{1,0:T(8,128)(2,1)S(1)}, bf16[64,1152]{1,0:T(8,128)(2,1)S(1)}, u32[]{:S(2)}, u32[]{:S(2)}) collective-permute-start(bf16[64,1152]{1,0:T(8,128)(2,1)S(1)} %get-tuple-element.118), channel_id=1, source_target_pairs={{0,16},{8,24},{16,0},{24,8},{1,17},{9,25},{17,1},{25,9},{2,18},{10... | collective-permute-start | bytes 442376 | tf_op jit(solution)/shard_map/ppermute | solution.py:808
  257.8 14.5 %collective-permute-start.18 = (bf16[64,1152]{1,0:T(8,128)(2,1)S(1)}, bf16[64,1152]{1,0:T(8,128)(2,1)S(1)}, u32[]{:S(2)}, u32[]{:S(2)}) collective-permute-start(bf16[64,1152]{1,0:T(8,128)(2,1)S(1)} %get-tuple-element.119), channel_id=1, source_target_pairs={{0,24},{8,0},{16,8},{24,16},{1,25},{9,1},{17,9},{25,17},{2,26},{10... | collective-permute-start | bytes 442376 | tf_op jit(solution)/shard_map/ppermute | solution.py:808
  (11 other events, 93.0 us)
Sparse Core Ops, SparseCore 0:
  11.5 97.0 all-gather.1
  169.5 60.5 reduce-scatter.2
  232.5 36.1 reduce-scatter.4
